TPU v7x, 256 devices: a whole 4x4x8 slice. The times are simulated.
256 devices in a mesh: row: 2 (over core), col: 64 (over z, y, x_hi), layer: 2 (over x_lo).
Axes of the slice: x: 4 (x_hi: 2, x_lo: 2; x = x_hi * 2 + x_lo), y: 4, z: 8, core: 2. Of those that a mesh axis runs over, the one named last changes fastest.
Arguments:
- flow_cols: int32 [16, 2, 64], P('row', 'layer', 'col'), may hold values from 0 to 64, as said below
- flow_vals: bfloat16 [16, 2, 64, 128, 128], P('row', 'layer', 'col'), may hold values from -22 to 22
- window_flow: bfloat16 [2, 8192, 32768], P('layer', 'row', 'col'), may hold values from -0.1403165 to 0.1403165
Outputs:
- flow_next: float32 [2048, 32768], P(('row', 'layer'), 'col')
Inputs may be any that keep to these rules, and one draw needn't show every extreme that they name: `flow_cols`: an entry 64 marks an empty slot; the live entries of one block row and layer are distinct; every block row and layer has at least one live slot, and some block row and layer has all 64 slots live.
All inputs are finite; a program needn't handle non-finite values.
Results may differ from a plain program's by a relative error of at most 0.0003.
Values may be sent and summed in bfloat16 or wider, within the bound.
A program may use at most 128 MiB of HBM per device.

v0:
```python
import jax
import jax.numpy as jnp
from jax import lax
from jax.sharding import PartitionSpec as P


def body(flow_cols, flow_vals, window_flow):
    window_panel = lax.all_gather(window_flow[0], "row", axis=0, tiled=True)
    block_size = flow_vals.shape[-1]
    block_count = window_panel.shape[0] // block_size
    row_blocks = flow_vals.shape[0]
    all_cols, all_vals = (
        lax.all_gather(flow_cols, "col", axis=2, tiled=True),
        lax.all_gather(flow_vals, "col", axis=2, tiled=True),
    )
    slot_cols = all_cols[:, 0, :]
    slot_vals = all_vals[:, 0]
    column_ids = jnp.arange(block_count, dtype=jnp.int32)
    one_hot = (slot_cols[:, :, None] == column_ids[None, None, :]).astype(jnp.bfloat16)
    dense_row = jnp.einsum(
        "isab,isk->iakb", slot_vals, one_hot, preferred_element_type=jnp.bfloat16
    )
    dense_row = dense_row.reshape(row_blocks * block_size, block_count * block_size)
    expanded = jnp.dot(dense_row, window_panel, preferred_element_type=jnp.float32)
    total_rows = row_blocks * block_size * lax.axis_size("row")
    summed = lax.psum(expanded, "layer")
    all_squares = summed * summed
    column_sums = lax.psum(jnp.sum(all_squares, axis=0), "row")
    share_rows = summed.shape[0] // lax.axis_size("layer")
    squares = lax.dynamic_slice_in_dim(
        all_squares, lax.axis_index("layer") * share_rows, share_rows, 0
    )
    return squares / (column_sums / total_rows + 1e-06)


def solution(mesh):
    placed = (
        P("row", "layer", "col"),
        P("row", "layer", "col", None, None),
        P("layer", "row", "col"),
    )
    return jax.shard_map(
        body, mesh=mesh, in_specs=placed, out_specs=P(("row", "layer"), "col"), check_vma=False
    )
```

profile of v0, /device:TPU:1, one launch (start us, length us, event | category | flops | bytes accessed | tf_op | source)
XLA Modules:
  0.0 361.2 jit_solution(3582234207168179350)
XLA Ops:
  6.5 0.0 all-gather.4.cloned.1.call-start
  6.5 0.7 all-gather.4.cloned.1.call-update
  7.3 0.0 all-gather.6.cloned.1.call-start
  7.3 0.7 all-gather.6.cloned.1.call-update
  8.0 0.0 all-reduce.2.cloned.1.call-start
  8.1 156.8 %all_gather.9 = s32[8,1,64]{0,1,2:T(1,128)S(1)} all-gather(s32[8,1,1]{0,1,2:T(1,128)} %bitcast.23), channel_id=1, replica_groups=mesh['row'=2,'col'=64,'layer'=2] {'col'}, dimensions={2}, use_global_device_ids=true | all-gather | bytes 2080 | tf_op jit(solution)/shard_map/all_gather | solution.py:13
  164.9 0.1 copy.7
  165.0 58.9 %all-gather.4.cloned.1.call-done = bf16[8,1,64,128,128]{4,3,1,0,2:T(8,128)(2,1)} async-done(((bf16[8,1,1,128,128]{4,3,1,0,2:T(8,128)(2,1)}), bf16[8,1,64,128,128]{4,3,1,0,2:T(8,128)(2,1)}) %all-gather.4.cloned.1.call-update) | async-done | bytes 16777232 | tf_op jit(solution)/shard_map/all_gather | solution.py:14
  223.9 22.9 %fusion.3 = bf16[8,64,128,128]{3,1,2,0:T(8,128)(2,1)} fusion(bf16[8,1,64,128,128]{4,3,1,0,2:T(8,128)(2,1)} %all-gather.4.cloned.1.call-done, s32[8,64]{1,0:T(8,128)S(1)} %copy.7), kind=kOutput, calls=%fused_computation.3 | convolution fusion | flops 1073774592 | bytes 33556480 | tf_op jit(solution)/shard_map/isab,isk->iakb/dot_general | solution.py:20
  246.8 2.1 all-gather.6.cloned.1.call-done
  248.9 24.6 %fusion = f32[1024,512]{1,0:T(8,128)} fusion(bf16[128,8,64,128]{3,2,1,0:T(8,128)(2,1)} %bitcast.20, bf16[1,8192,512]{2,1,0:T(8,128)(2,1)} %all-gather.6.cloned.1.call-done), kind=kOutput, calls=%fused_computation | convolution fusion | flops 8589934592 | bytes 27262976 | tf_op jit(solution)/shard_map/dot_general | solution.py:24
  273.5 0.0 all-reduce.2.cloned.1.call-update
  273.5 75.3 %all-reduce.2.cloned.1.call-done = f32[1024,512]{1,0:T(8,128)} async-done(((f32[1024,512]{1,0:T(8,128)}), f32[1024,512]{1,0:T(8,128)}) %all-reduce.2.cloned.1.call-update) | async-done | bytes 2097168 | tf_op jit(solution)/shard_map/psum | solution.py:26
  348.8 1.9 multiply_reduce_fusion
  350.7 2.8 psum.15
  353.6 1.1 dynamic-slice_divide_fusion
  (1 shorter events, 0.0 us)
Async XLA Ops:
  6.5 217.4 %all-gather.4.cloned.1.call-start = ((), (), s32[]{:S(2)}) async-start(), calls=%async_computation | async-start | bytes 17039360 | tf_op jit(solution)/shard_map/all_gather | solution.py:14
  7.3 241.6 %all-gather.6.cloned.1.call-start = ((), (), s32[]{:S(2)}) async-start(), calls=%async_computation.2 | async-start | bytes 12582912 | tf_op jit(solution)/shard_map/all_gather | solution.py:8
  8.0 340.8 %all-reduce.2.cloned.1.call-start = ((), (), s32[]{:S(2)}) async-start(), calls=%async_computation.1 | async-start | bytes 4194304 | tf_op jit(solution)/shard_map/psum | solution.py:26
Sparse Core Ops, SparseCore 0:
  11.1 212.7 all-gather.3
  225.7 23.1 all-gather.5
  273.6 75.1 all-reduce.1
where the time goes:
time: 361 us
  blocking collectives  160 us (44%)
  waiting for transfers between devices  138 us (38%)
  matrix products  47.5 us (13%)
  between operations  13.1 us (4%)
    all_gather x1, blocking collectives, body(): lax.all_gather(flow_cols, 'col', axis=2, tiled=True)  157 us
    psum x1, waiting for transfers between devices, body(): summed = lax.psum(expanded, 'layer')  75.3 us
    all_gather x1, waiting for transfers between devices, body(): lax.all_gather(flow_vals, 'col', axis=2, tiled=True)  58.9 us
    dot_general x1, matrix products, body(): jnp.dot(dense_row, window_panel, preferred_element_type=jnp.float32)  24.6 us
    dot_general x1, matrix products, body(): jnp.einsum('isab,isk->iakb', slot_vals, one_hot, preferred_element_type=j...  22.9 us
  transfers between devices with their start and end apart: 3, of which 3 were waited for; matrix products, arithmetic and copies ran while one was open for 6% of the time, Pallas kernels for 0%

commit v1 on v0

v1 whole, which is shorter than its diff:
```python
import jax
import jax.numpy as jnp
from jax import lax
from jax.sharding import PartitionSpec as P


def body(flow_cols, flow_vals, window_flow):
    row = lax.axis_index("row")
    layer = lax.axis_index("layer")
    n_layer = lax.axis_size("layer")
    own_g = window_flow[0]
    half_rows = own_g.shape[0]
    other_g = lax.ppermute(own_g, "row", perm=[(0, 1), (1, 0)])
    panel = jnp.zeros((2 * half_rows, own_g.shape[1]), own_g.dtype)
    panel = lax.dynamic_update_slice_in_dim(panel, own_g, row * half_rows, 0)
    panel = lax.dynamic_update_slice_in_dim(panel, other_g, (1 - row) * half_rows, 0)

    block_size = flow_vals.shape[-1]
    block_count = panel.shape[0] // block_size
    row_blocks = flow_vals.shape[0]
    wide_cols = jnp.broadcast_to(flow_cols.astype(jnp.bfloat16)[..., None, None], flow_cols.shape + (16, 128))
    wide_cols = lax.optimization_barrier(wide_cols)
    slot_cols = lax.all_gather(wide_cols, "col", axis=2, tiled=True)[:, 0, :, 0, 0].astype(jnp.float32)
    slot_vals = lax.all_gather(flow_vals, "col", axis=2, tiled=True)[:, 0]
    column_ids = jnp.arange(block_count, dtype=jnp.float32)
    one_hot = (slot_cols[:, :, None] == column_ids[None, None, :]).astype(jnp.bfloat16)

    share = row_blocks // n_layer
    send_blocks = (1 - layer) * share
    keep_blocks = layer * share

    def expand(first_block):
        vals = lax.dynamic_slice_in_dim(slot_vals, first_block, share, 0)
        hot = lax.dynamic_slice_in_dim(one_hot, first_block, share, 0)
        dense = jnp.einsum("isab,isk->iakb", vals, hot, preferred_element_type=jnp.bfloat16)
        dense = dense.reshape(share * block_size, block_count * block_size)
        return jnp.dot(dense, panel, preferred_element_type=jnp.float32)

    sent = expand(send_blocks)
    received = lax.ppermute(sent, "layer", perm=[(0, 1), (1, 0)])
    summed = expand(keep_blocks) + received
    squares = summed * summed
    total_rows = row_blocks * block_size * lax.axis_size("row")
    column_sums = lax.psum(jnp.sum(squares, axis=0), ("row", "layer"))
    return squares / (column_sums / total_rows + 1e-06)


def solution(mesh):
    placed = (
        P("row", "layer", "col"),
        P("row", "layer", "col", None, None),
        P("layer", "row", "col"),
    )
    return jax.shard_map(
        body, mesh=mesh, in_specs=placed, out_specs=P(("row", "layer"), "col"), check_vma=False
    )
```

time: 361 us -> 436 us (1.21)
  waiting for transfers between devices: 138 us -> 336 us
  blocking collectives: 160 us -> 8.44 us
  local copies, waits for them, and re-layouts: 0.06 us -> 22.5 us
    all_gather x2, waiting for transfers between devices: 61 us -> 321 us  [the longest x1 209 us: body(): slot_vals = lax.all_gather(flow_vals, 'col', axis=2, tiled=True)[:, 0]]
    all_gather x1 -> x0, blocking collectives: 157 us -> none  [body(): lax.all_gather(flow_cols, 'col', axis=2, tiled=True)]
    psum x1 -> x0, waiting for transfers between devices: 75.3 us -> none  [body(): summed = lax.psum(expanded, 'layer')]
    ppermute x0 -> x2, waiting for transfers between devices: none -> 14.9 us  [the longest x1 14.9 us: body(): received = lax.ppermute(sent, 'layer', perm=[(0, 1), (1, 0)])]
    dynamic_slice x0 -> x1, local copies, waits for them, and re-layouts: none -> 9.42 us  [expand(): vals = lax.dynamic_slice_in_dim(slot_vals, first_block, share, 0)]
    dynamic_update_slice x0 -> x2, local copies, waits for them, and re-layouts: none -> 6.63 us  [the longest x1 4.42 us: body(): lax.dynamic_update_slice_in_dim(panel, other_g, (1 - row) * half_rows, 0)]
    psum x1, blocking collectives: 2.8 us -> 8.44 us  [body(): column_sums = lax.psum(jnp.sum(squares, axis=0), ('row', 'layer'))]
    broadcast_in_dim x0 -> x2, local copies, waits for them, and re-layouts: none -> 4.87 us  [the longest x1 4.18 us: body(): panel = jnp.zeros((2 * half_rows, own_g.shape[1]), own_g.dtype)]
  transfers between devices with their start and end apart: 3 -> 4, of which waited for: 3 -> 3; matrix products, arithmetic and copies ran while one was open for 6% -> 5% of each run, Pallas kernels for 0% -> 0%
where the time goes in v1:
time: 436 us
  waiting for transfers between devices  336 us (77%)
  matrix products  49.5 us (11%)
  local copies, waits for them, and re-layouts  22.5 us (5%)
  between operations  13.4 us (3%)
  blocking collectives  8.44 us (2%)
    all_gather x1, waiting for transfers between devices, body(): slot_vals = lax.all_gather(flow_vals, 'col', axis=2, tiled=True)[:, 0]  209 us
    all_gather x1, waiting for transfers between devices, body(): lax.all_gather(wide_cols, 'col', axis=2, tiled=True)[:, 0, :, 0, 0]  112 us
    dot_general x2, matrix products, expand(): return jnp.dot(dense, panel, preferred_element_type=jnp.float32)  27.6 us
    dot_general x2, matrix products, expand(): jnp.einsum('isab,isk->iakb', vals, hot, preferred_element_type=jnp.bfloat16)  21.9 us
    ppermute x1, waiting for transfers between devices, body(): received = lax.ppermute(sent, 'layer', perm=[(0, 1), (1, 0)])  14.9 us
    dynamic_slice x1, local copies, waits for them, and re-layouts, expand(): vals = lax.dynamic_slice_in_dim(slot_vals, first_block, share, 0)  9.42 us
  transfers between devices with their start and end apart: 4, of which 3 were waited for; matrix products, arithmetic and copies ran while one was open for 5% of the time, Pallas kernels for 0%

profile of v1, /device:TPU:1, one launch (start us, length us, event | category | flops | bytes accessed | tf_op | source)
XLA Modules:
  0.0 435.7 jit_solution(5035930560204560066)
XLA Ops:
  6.5 0.7 convert_bitcast_fusion
  7.2 0.7 broadcast_in_dim.7
  7.9 0.0 all-gather.3.cloned.1.call-update
  7.9 0.0 all-gather.5.cloned.1.call-start
  8.0 0.7 all-gather.5.cloned.1.call-update
  8.7 3.3 collective-permute-start
  12.0 4.2 broadcast_in_dim.16
  16.2 2.2 constant_dynamic-update-slice_fusion.1
  18.4 111.7 %all-gather.3.cloned.1.call-done = bf16[8,1,64,16,128]{4,3,1,0,2:T(8,128)(2,1)} async-done(((bf16[8,1,1,16,128]{4,3,1,0,2:T(8,128)(2,1)}), bf16[8,1,64,16,128]{4,3,1,0,2:T(8,128)(2,1)}) %all-gather.3.cloned.1.call-update) | async-done | bytes 2097168 | tf_op jit(solution)/shard_map/all_gather | solution.py:23
  130.1 1.4 slice.4
  131.5 0.2 copy.14
  131.6 0.1 iota_compare_fusion
  131.7 0.0 collective-permute-done
  131.7 4.4 %constant_dynamic-update-slice_fusion = bf16[8192,512]{1,0:T(8,128)(2,1)} fusion(bf16[8192,512]{1,0:T(8,128)(2,1)} %constant_dynamic-update-slice_fusion.1, bf16[4096,512]{1,0:T(8,128)(2,1)} %collective-permute-done, s32[]{:T(128)S(6)} %select_n.16), kind=kLoop, calls=%fused_computation.24 | loop fusion | bytes 8388612 | tf_op jit(solution)/shard_map/dynamic_update_slice | solution.py:16
  136.1 209.0 %all-gather.5.cloned.1.call-done = bf16[8,1,64,128,128]{4,3,2,1,0:T(8,128)(2,1)} async-done(((bf16[8,1,1,128,128]{4,3,2,1,0:T(8,128)(2,1)}), bf16[8,1,64,128,128]{4,3,2,1,0:T(8,128)(2,1)}) %all-gather.5.cloned.1.call-update) | async-done | bytes 16777232 | tf_op jit(solution)/shard_map/all_gather | solution.py:24
  345.1 9.4 %constant_dynamic-slice_fusion.1 = (bf16[4,1,64,128,128]{4,3,2,1,0:T(8,128)(2,1)S(1)}, bf16[4,1,64,128,128]{4,3,2,1,0:T(8,128)(2,1)}) fusion(bf16[8,1,64,128,128]{4,3,2,1,0:T(8,128)(2,1)} %all-gather.5.cloned.1.call-done, s32[]{:T(128)S(6)} %select_n.14, s32[]{:T(128)S(6)} %select_n.17), kind=kLoop, calls=%fused_computation.26 | loop fusion | bytes 33554440 | tf_op jit(solution)/shard_map/dynamic_slice | solution.py:33
  354.6 13.4 %fusion.6 = bf16[4,64,128,128]{3,1,2,0:T(8,128)(2,1)} fusion(bf16[4,1,64,128,128]{4,3,2,1,0:T(8,128)(2,1)} %get-tuple-element.6, pred[8,64,64]{1,2,0:T(32,128)(4,1)S(1)} %iota_compare_fusion, s32[]{:T(128)S(6)} %select_n.17), kind=kOutput, calls=%fused_computation.6 | convolution fusion | flops 536870912 | bytes 16809988 | tf_op jit(solution)/shard_map/isab,isk->iakb/dot_general | solution.py:35
  368.0 13.8 %fusion = f32[512,512]{1,0:T(8,128)S(1)} fusion(bf16[8192,512]{1,0:T(8,128)(2,1)} %constant_dynamic-update-slice_fusion, bf16[64,8,64,128]{3,2,1,0:T(8,128)(2,1)} %bitcast.44), kind=kOutput, calls=%fused_computation | convolution fusion | flops 4294967296 | bytes 17825792 | tf_op jit(solution)/shard_map/dot_general | solution.py:37
  381.8 0.4 collective-permute-start.1
  382.2 8.4 %fusion.8 = bf16[4,64,128,128]{3,1,2,0:T(8,128)(2,1)} fusion(bf16[4,1,64,128,128]{4,3,2,1,0:T(8,128)(2,1)S(1)} %get-tuple-element.5, pred[8,64,64]{1,2,0:T(32,128)(4,1)S(1)} %iota_compare_fusion, s32[]{:T(128)S(6)} %select_n.14), kind=kOutput, calls=%fused_computation.8 | convolution fusion | flops 536870912 | bytes 16809988 | tf_op jit(solution)/shard_map/isab,isk->iakb/dot_general | solution.py:35
  390.6 14.9 %collective-permute-done.1 = f32[512,512]{1,0:T(8,128)S(1)} collective-permute-done((f32[512,512]{1,0:T(8,128)S(1)}, f32[512,512]{1,0:T(8,128)S(1)}, u32[]{:S(2)}, u32[]{:S(2)}) %collective-permute-start.1) | collective-permute-done | bytes 1048608 | tf_op jit(solution)/shard_map/ppermute | solution.py:40
  405.5 13.8 %fusion.24 = (f32[512]{0:T(512)S(1)}, f32[512,512]{1,0:T(8,128)S(1)}) fusion(f32[512,512]{1,0:T(8,128)S(1)} %collective-permute-done.1, bf16[8192,512]{1,0:T(8,128)(2,1)} %constant_dynamic-update-slice_fusion, bf16[64,8,64,128]{3,2,1,0:T(8,128)(2,1)} %bitcast.43), kind=kOutput, calls=%fused_computation.29 | convolution fusion | flops 4295753216 | bytes 18876416 | tf_op jit(solution)/shard_map/dot_general | solution.py:37
  419.3 8.4 %psum.7 = f32[512]{0:T(512)S(1)} all-reduce(f32[512]{0:T(512)S(1)} %get-tuple-element.7), channel_id=1, replica_groups=mesh['row'=2,'col'=64,'layer'=2] {'row','layer'}, use_global_device_ids=true, to_apply=%region_1.0 | all-reduce | flops 512 | bytes 4096 | tf_op jit(solution)/shard_map/psum | solution.py:44
  427.7 1.1 broadcast_divide_fusion
  (5 shorter events, 0.0 us)
Async XLA Ops:
  6.5 123.5 %all-gather.3.cloned.1.call-start = ((), (), s32[]{:S(2)}) async-start(), calls=%async_computation | async-start | bytes 2129920 | tf_op jit(solution)/shard_map/all_gather | solution.py:23
  7.9 337.2 %all-gather.5.cloned.1.call-start = ((), (), s32[]{:S(2)}) async-start(), calls=%async_computation.1 | async-start | bytes 17039360 | tf_op jit(solution)/shard_map/all_gather | solution.py:24
  8.7 123.0 %collective-permute-start = (bf16[4096,512]{1,0:T(8,128)(2,1)}, bf16[4096,512]{1,0:T(8,128)(2,1)}, u32[]{:S(2)}, u32[]{:S(2)}) collective-permute-start(bf16[4096,512]{1,0:T(8,128)(2,1)} %bitcast.45), channel_id=1, source_target_pairs={{0,128},{128,0},{1,129},{129,1},{2,130},{130,2},{3,131},{131,3},{4... | collective-permute-start | bytes 12582920 | tf_op jit(solution)/shard_map/ppermute | solution.py:13
  12.0 4.2 copy-start
  381.8 23.7 %collective-permute-start.1 = (f32[512,512]{1,0:T(8,128)S(1)}, f32[512,512]{1,0:T(8,128)S(1)}, u32[]{:S(2)}, u32[]{:S(2)}) collective-permute-start(f32[512,512]{1,0:T(8,128)S(1)} %fusion), channel_id=1, source_target_pairs={{0,1},{1,0},{2,3},{3,2},{4,5},{5,4},{6,7},{7,6},{8,9},{9,8},{10,11... | collective-permute-start | bytes 3145736 | tf_op jit(solution)/shard_map/ppermute | solution.py:40
Sparse Core Ops, SparseCore 0:
  10.9 119.0 all-gather.2
  133.6 211.5 all-gather.4

commit v2 on v1

v2 whole, which is shorter than its diff:
```python
import jax
import jax.numpy as jnp
from jax import lax
from jax.sharding import Mesh, PartitionSpec as P

COL_FACTORS = (8, 4, 2)
COL_PARTS = ("col_z", "col_y", "col_x")


def gather_slots(packed, split):
    if split:
        packed = lax.all_gather(packed, COL_PARTS[2], axis=0, tiled=True)
        return lax.all_gather(packed, COL_PARTS[:2], axis=0, tiled=True)
    return lax.all_gather(packed, "col", axis=0, tiled=True)


def body(flow_cols, flow_vals, window_flow, split):
    row = lax.axis_index("row")
    layer = lax.axis_index("layer")
    n_layer = lax.axis_size("layer")
    own_g = window_flow[0]
    half_rows = own_g.shape[0]
    other_g = lax.ppermute(own_g, "row", perm=[(0, 1), (1, 0)])
    panel = jnp.zeros((2 * half_rows, own_g.shape[1]), own_g.dtype)
    panel = lax.dynamic_update_slice_in_dim(panel, own_g, row * half_rows, 0)
    panel = lax.dynamic_update_slice_in_dim(panel, other_g, (1 - row) * half_rows, 0)

    block_size = flow_vals.shape[-1]
    block_count = panel.shape[0] // block_size
    row_blocks = flow_vals.shape[0]
    stacked = flow_vals.reshape(1, row_blocks * block_size, block_size)
    col_tile = jnp.zeros((1, 16, block_size), jnp.bfloat16)
    col_tile = col_tile.at[0, 0, :row_blocks].set(flow_cols.reshape(row_blocks).astype(jnp.bfloat16))
    packed = jnp.concatenate([stacked, col_tile], axis=1)
    gathered = gather_slots(packed, split)
    slot_count = gathered.shape[0]
    slot_vals = gathered[:, : row_blocks * block_size].reshape(slot_count, row_blocks, block_size, block_size)
    slot_cols = gathered[:, row_blocks * block_size, :row_blocks].astype(jnp.float32).T
    column_ids = jnp.arange(block_count, dtype=jnp.float32)
    one_hot = (slot_cols[:, :, None] == column_ids[None, None, :]).astype(jnp.bfloat16)

    share = row_blocks // n_layer
    send_blocks = (1 - layer) * share
    keep_blocks = layer * share

    def expand(first_block):
        vals = lax.dynamic_slice_in_dim(slot_vals, first_block, share, 1)
        hot = lax.dynamic_slice_in_dim(one_hot, first_block, share, 0)
        dense = jnp.einsum("siab,isk->iakb", vals, hot, preferred_element_type=jnp.bfloat16)
        dense = dense.reshape(share * block_size, block_count * block_size)
        return jnp.dot(dense, panel, preferred_element_type=jnp.float32)

    sent = expand(send_blocks)
    received = lax.ppermute(sent, "layer", perm=[(0, 1), (1, 0)])
    summed = expand(keep_blocks) + received
    squares = summed * summed
    total_rows = row_blocks * block_size * lax.axis_size("row")
    column_sums = lax.psum(jnp.sum(squares, axis=0), ("row", "layer"))
    return squares / (column_sums / total_rows + 1e-06)


def solution(mesh):
    split = mesh.shape["col"] == COL_FACTORS[0] * COL_FACTORS[1] * COL_FACTORS[2]
    if split:
        devices = mesh.devices.reshape(
            (mesh.shape["row"],) + COL_FACTORS + (mesh.shape["layer"],)
        )
        mesh = Mesh(devices, ("row",) + COL_PARTS + ("layer",))
        col = COL_PARTS
    else:
        col = "col"
    placed = (
        P("row", "layer", col),
        P("row", "layer", col, None, None),
        P("layer", "row", col),
    )
    return jax.shard_map(
        lambda c, v, w: body(c, v, w, split),
        mesh=mesh, in_specs=placed, out_specs=P(("row", "layer"), col), check_vma=False,
    )
```

time: 436 us -> 281 us (0.64)
  waiting for transfers between devices: 336 us -> 150 us
  local copies, waits for them, and re-layouts: 22.5 us -> 57.1 us
  matrix products: 49.5 us -> 35.2 us
  blocking collectives: 8.44 us -> 18.6 us
    all_gather x2 -> x1, waiting for transfers between devices: 321 us -> 132 us  [gather_slots(): return lax.all_gather(packed, COL_PARTS[:2], axis=0, tiled=True)]
    slice x1 -> x3, local copies, waits for them, and re-layouts: 1.4 us -> 46 us  [body(): gathered[:, :row_blocks * block_size]]
    dot_general x2, matrix products: 21.9 us -> 11.4 us  [expand(): jnp.einsum('siab,isk->iakb', vals, hot, preferred_element_type=jnp.bfloat16)]
    dynamic_slice x1 -> x0, local copies, waits for them, and re-layouts: 9.42 us -> none  [expand(): vals = lax.dynamic_slice_in_dim(slot_vals, first_block, share, 0)]
    all_gather x0 -> x1, blocking collectives: none -> 9.31 us  [gather_slots(): packed = lax.all_gather(packed, COL_PARTS[2], axis=0, tiled=True)]
  transfers between devices with their start and end apart: 4 -> 3, of which waited for: 3 -> 3; matrix products, arithmetic and copies ran while one was open for 5% -> 6% of each run, Pallas kernels for 0% -> 0%
where the time goes in v2:
time: 281 us
  waiting for transfers between devices  150 us (53%)
  local copies, waits for them, and re-layouts  57.1 us (20%)
  matrix products  35.2 us (13%)
  blocking collectives  18.6 us (7%)
  between operations  13.5 us (5%)
  starting transfers between devices  3.99 us (1%)
  other arithmetic  2.83 us (1%)
    all_gather x1, waiting for transfers between devices, gather_slots(): return lax.all_gather(packed, COL_PARTS[:2], axis=0, tiled=True)  132 us
    slice x3, local copies, waits for them, and re-layouts, body(): gathered[:, :row_blocks * block_size]  46 us
    dot_general x2, matrix products, expand(): return jnp.dot(dense, panel, preferred_element_type=jnp.float32)  23.8 us
    ppermute x1, waiting for transfers between devices, body(): received = lax.ppermute(sent, 'layer', perm=[(0, 1), (1, 0)])  16.7 us
    dot_general x2, matrix products, expand(): jnp.einsum('siab,isk->iakb', vals, hot, preferred_element_type=jnp.bfloat16)  11.4 us
    all_gather x1, blocking collectives, gather_slots(): packed = lax.all_gather(packed, COL_PARTS[2], axis=0, tiled=True)  9.31 us
    psum x1, blocking collectives, body(): column_sums = lax.psum(jnp.sum(squares, axis=0), ('row', 'layer'))  9.29 us
  transfers between devices with their start and end apart: 3, of which 3 were waited for; matrix products, arithmetic and copies ran while one was open for 6% of the time, Pallas kernels for 0%

profile of v2, /device:TPU:1, one launch (start us, length us, event | category | flops | bytes accessed | tf_op | source)
XLA Modules:
  0.0 280.8 jit_solution(518433369213402317)
XLA Ops:
  6.5 0.7 convert_bitcast_fusion
  7.2 1.0 fusion.17
  8.2 9.3 %all_gather.6 = bf16[2,1040,128]{2,1,0:T(8,128)(2,1)} all-gather(bf16[1,1040,128]{2,1,0:T(8,128)(2,1)S(1)} %fusion.17), channel_id=1, replica_groups=mesh['row'=2,'col_z'=8,'col_y'=4,'col_x'=2,'layer'=2] {'col_x'}, dimensions={0}, use_global_device_ids=true | all-gather | bytes 798720 | tf_op jit(solution)/shard_map/all_gather | solution.py:12
  17.5 0.0 all-gather.2.cloned.1.call-update
  17.5 2.7 collective-permute-start
  20.2 4.2 %broadcast_in_dim.2 = bf16[8192,512]{1,0:T(8,128)(2,1)} broadcast(bf16[]{:T(256)} %constant.46.clone.1), dimensions={} | broadcast | bytes 8388610 | tf_op jit(solution)/shard_map/broadcast_in_dim | solution.py:24
  24.4 2.3 constant_dynamic-update-slice_fusion.1
  26.7 0.7 collective-permute-done
  27.4 4.5 %constant_dynamic-update-slice_fusion = bf16[8192,512]{1,0:T(8,128)(2,1)} fusion(bf16[8192,512]{1,0:T(8,128)(2,1)} %constant_dynamic-update-slice_fusion.1, bf16[4096,512]{1,0:T(8,128)(2,1)} %collective-permute-done, s32[]{:T(128)S(6)} %select_n.16), kind=kLoop, calls=%fused_computation.23 | loop fusion | bytes 8388612 | tf_op jit(solution)/shard_map/dynamic_update_slice | solution.py:26
  31.9 132.2 %all-gather.2.cloned.1.call-done = bf16[64,1040,128]{2,1,0:T(8,128)(2,1)} async-done(((bf16[2,1040,128]{2,1,0:T(8,128)(2,1)}), bf16[64,1040,128]{2,1,0:T(8,128)(2,1)}) %all-gather.2.cloned.1.call-update) | async-done | bytes 17039376 | tf_op jit(solution)/shard_map/all_gather | solution.py:13
  164.1 5.8 %slice-done.5 = bf16[64,1024,128]{2,1,0:T(8,128)(2,1)S(1)} async-done(((bf16[64,1040,128]{2,1,0:T(8,128)(2,1)}), bf16[64,1024,128]{2,1,0:T(8,128)(2,1)S(1)}, s32[]{:S(2)}) %slice-start.5) | async-done | bytes 16777240 | tf_op jit(solution)/shard_map/slice | solution.py:37
  169.9 40.3 %copy.8 = bf16[64,1024,128]{2,0,1:T(8,128)(2,1)} copy(bf16[64,1024,128]{2,1,0:T(8,128)(2,1)S(1)} %slice-done.5) | data formatting | bytes 33554432 | tf_op jit(solution)/shard_map/slice | solution.py:37
  210.2 0.0 slice-done.3
  210.2 0.0 slice-done.4
  210.2 0.1 copy.7
  210.3 0.1 iota_compare_fusion.1
  210.3 5.7 %fusion.6 = bf16[4,64,128,128]{3,1,2,0:T(8,128)(2,1)S(1)} fusion(bf16[64,8,128,128]{3,0,2,1:T(8,128)(2,1)} %bitcast.39, s32[]{:T(128)S(6)} %select_n.17, pred[8,64,64]{1,2,0:T(32,128)(4,1)S(1)} %iota_compare_fusion.1), kind=kOutput, calls=%fused_computation.6 | convolution fusion | flops 536870912 | bytes 16811008 | tf_op jit(solution)/shard_map/siab,isk->iakb/dot_general | solution.py:49
  216.0 12.0 %fusion = f32[512,512]{1,0:T(8,128)S(1)} fusion(bf16[8192,512]{1,0:T(8,128)(2,1)} %constant_dynamic-update-slice_fusion, bf16[64,8,64,128]{3,2,1,0:T(8,128)(2,1)S(1)} %bitcast.44), kind=kOutput, calls=%fused_computation | convolution fusion | flops 4294967296 | bytes 17825792 | tf_op jit(solution)/shard_map/dot_general | solution.py:51
  228.0 1.3 collective-permute-start.1
  229.3 5.7 %fusion.8 = bf16[4,64,128,128]{3,1,2,0:T(8,128)(2,1)S(1)} fusion(bf16[64,8,128,128]{3,0,2,1:T(8,128)(2,1)} %bitcast.40, s32[]{:T(128)S(6)} %select_n.14, pred[8,64,64]{1,2,0:T(32,128)(4,1)S(1)} %iota_compare_fusion.1), kind=kOutput, calls=%fused_computation.8 | convolution fusion | flops 536870912 | bytes 16811008 | tf_op jit(solution)/shard_map/siab,isk->iakb/dot_general | solution.py:49
  235.0 16.7 %collective-permute-done.1 = f32[512,512]{1,0:T(8,128)S(1)} collective-permute-done((f32[512,512]{1,0:T(8,128)S(1)}, f32[512,512]{1,0:T(8,128)S(1)}, u32[]{:S(2)}, u32[]{:S(2)}) %collective-permute-start.1) | collective-permute-done | bytes 1048608 | tf_op jit(solution)/shard_map/ppermute | solution.py:54
  251.7 11.9 %fusion.24 = (f32[512]{0:T(512)S(1)}, f32[512,512]{1,0:T(8,128)S(1)}) fusion(f32[512,512]{1,0:T(8,128)S(1)} %collective-permute-done.1, bf16[8192,512]{1,0:T(8,128)(2,1)} %constant_dynamic-update-slice_fusion, bf16[64,8,64,128]{3,2,1,0:T(8,128)(2,1)S(1)} %bitcast.43), kind=kOutput, calls=%fused_computation.28 | convolution fusion | flops 4295753216 | bytes 18876416 | tf_op jit(solution)/shard_map/dot_general | solution.py:51
  263.6 9.3 %psum.7 = f32[512]{0:T(512)S(1)} all-reduce(f32[512]{0:T(512)S(1)} %get-tuple-element.17), channel_id=1, replica_groups=mesh['row'=2,'col_z'=8,'col_y'=4,'col_x'=2,'layer'=2] {'row','layer'}, use_global_device_ids=true, to_apply=%region_1.0 | all-reduce | flops 512 | bytes 4096 | tf_op jit(solution)/shard_map/psum | solution.py:58
  272.9 1.1 broadcast_divide_fusion
  (15 shorter events, 0.1 us)
Async XLA Ops:
  6.5 157.6 %all-gather.2.cloned.1.call-start = ((), (), s32[]{:S(2)}) async-start(), calls=%async_computation | async-start | bytes 17571840 | tf_op jit(solution)/shard_map/all_gather | solution.py:13
  17.5 9.8 %collective-permute-start = (bf16[4096,512]{1,0:T(8,128)(2,1)}, bf16[4096,512]{1,0:T(8,128)(2,1)}, u32[]{:S(2)}, u32[]{:S(2)}) collective-permute-start(bf16[4096,512]{1,0:T(8,128)(2,1)} %bitcast.45), channel_id=1, source_target_pairs={{0,128},{128,0},{1,129},{129,1},{2,130},{130,2},{3,131},{131,3},{4... | collective-permute-start | bytes 12582920 | tf_op jit(solution)/shard_map/ppermute | solution.py:23
  20.2 4.2 %copy-start = (bf16[1,4096,512]{2,1,0:T(8,128)(2,1)S(1)}, bf16[1,4096,512]{2,1,0:T(8,128)(2,1)}, u32[]{:S(2)}) copy-start(bf16[1,4096,512]{2,1,0:T(8,128)(2,1)} %param.7) | copy-start | bytes 12582916
  164.1 5.8 %slice-start.5 = ((bf16[64,1040,128]{2,1,0:T(8,128)(2,1)}), bf16[64,1024,128]{2,1,0:T(8,128)(2,1)S(1)}, s32[]{:S(2)}) async-start(bf16[64,1040,128]{2,1,0:T(8,128)(2,1)} %all-gather.2.cloned.1.call-done), calls=%async_computation.6 | async-start | bytes 33554432 | tf_op jit(solution)/shard_map/slice | solution.py:37
  164.1 46.0 %slice-start = ((s8[17039360]{0:T(1024)(128)(4,1)}), s8[4194304]{0:T(1024)(128)(4,1)S(1)}, s32[]{:S(2)}) async-start(s8[17039360]{0:T(1024)(128)(4,1)} %bitcast.41), calls=%async_computation.1 | async-start | bytes 8388608
  164.1 46.0 %slice-start.1 = ((s8[17039360]{0:T(1024)(128)(4,1)}), s8[4194304]{0:T(1024)(128)(4,1)S(1)}, s32[]{:S(2)}) async-start(s8[17039360]{0:T(1024)(128)(4,1)} %bitcast.41), calls=%async_computation.2 | async-start | bytes 8388608
  164.1 46.0 %slice-start.2 = ((s8[17039360]{0:T(1024)(128)(4,1)}), s8[4194304]{0:T(1024)(128)(4,1)S(1)}, s32[]{:S(2)}) async-start(s8[17039360]{0:T(1024)(128)(4,1)} %bitcast.41), calls=%async_computation.3 | async-start | bytes 8388608
  169.9 40.3 %slice-start.3 = ((s8[17039360]{0:T(1024)(128)(4,1)}), s8[4194304]{0:T(1024)(128)(4,1)S(1)}, s32[]{:S(2)}) async-start(s8[17039360]{0:T(1024)(128)(4,1)} %bitcast.41), calls=%async_computation.4 | async-start | bytes 8388608
  169.9 40.3 %slice-start.4 = ((s8[17039360]{0:T(1024)(128)(4,1)}), s8[262144]{0:T(1024)(128)(4,1)S(1)}, s32[]{:S(2)}) async-start(s8[17039360]{0:T(1024)(128)(4,1)} %bitcast.41), calls=%async_computation.5 | async-start | bytes 524288
  228.0 23.7 %collective-permute-start.1 = (f32[512,512]{1,0:T(8,128)S(1)}, f32[512,512]{1,0:T(8,128)S(1)}, u32[]{:S(2)}, u32[]{:S(2)}) collective-permute-start(f32[512,512]{1,0:T(8,128)S(1)} %fusion), channel_id=1, source_target_pairs={{0,1},{1,0},{2,3},{3,2},{4,5},{5,4},{6,7},{7,6},{8,9},{9,8},{10,11... | collective-permute-start | bytes 3145736 | tf_op jit(solution)/shard_map/ppermute | solution.py:54
Sparse Core Ops, SparseCore 0:
  17.6 146.4 all-gather.1

commit v3 on v2

--- a/solution.py
+++ b/solution.py
@@ -1,7 +1,59 @@
 import jax
 import jax.numpy as jnp
+from jax.experimental import pallas as pl
+from jax.experimental.pallas import tpu as pltpu
 from jax import lax
 from jax.sharding import Mesh, PartitionSpec as P
+
+
+def sparse_rows_kernel(first_ref, cols_ref, vals_ref, panel_ref, out_ref, acc_ref):
+    i = pl.program_id(0)
+    block_row = first_ref[0] + i
+    block_size = vals_ref.shape[-1]
+    block_count = panel_ref.shape[0] // block_size
+    acc_ref[...] = jnp.zeros_like(acc_ref)
+
+    def step(s, carry):
+        col = cols_ref[block_row, s]
+
+        @pl.when(jnp.logical_and(col >= 0, col < block_count))
+        def _():
+            start = pl.multiple_of(col * block_size, block_size)
+            acc_ref[...] += jnp.dot(
+                vals_ref[s], panel_ref[pl.ds(start, block_size), :],
+                preferred_element_type=jnp.float32,
+            )
+
+        return carry
+
+    lax.fori_loop(0, vals_ref.shape[0], step, 0)
+    out_ref[...] = acc_ref[...]
+
+
+def sparse_rows(first, cols, gathered, panel, share):
+    slot_count = gathered.shape[0]
+    block_size = gathered.shape[-1]
+    width = panel.shape[1]
+    return pl.pallas_call(
+        sparse_rows_kernel,
+        out_shape=jax.ShapeDtypeStruct((share * block_size, width), jnp.float32),
+        grid_spec=pltpu.PrefetchScalarGridSpec(
+            num_scalar_prefetch=2,
+            grid=(share,),
+            in_specs=[
+                pl.BlockSpec((slot_count, block_size, block_size), lambda i, f, c: (0, f[0] + i, 0)),
+                pl.BlockSpec(panel.shape, lambda i, f, c: (0, 0), pipeline_mode=pl.Buffered(1)),
+            ],
+            out_specs=pl.BlockSpec((block_size, width), lambda i, f, c: (i, 0)),
+            scratch_shapes=[pltpu.VMEM((block_size, width), jnp.float32)],
+        ),
+        compiler_params=pltpu.CompilerParams(vmem_limit_bytes=48 * 1024 * 1024),
+        cost_estimate=pl.CostEstimate(
+            flops=2 * share * slot_count * block_size * block_size * width,
+            transcendentals=0,
+            bytes_accessed=share * slot_count * block_size * block_size * 2 + panel.size * 2 + share * block_size * width * 4,
+        ),
+    )(first, cols, gathered, panel)
 
 COL_FACTORS = (8, 4, 2)
 COL_PARTS = ("col_z", "col_y", "col_x")
@@ -33,26 +85,18 @@
     col_tile = col_tile.at[0, 0, :row_blocks].set(flow_cols.reshape(row_blocks).astype(jnp.bfloat16))
     packed = jnp.concatenate([stacked, col_tile], axis=1)
     gathered = gather_slots(packed, split)
-    slot_count = gathered.shape[0]
-    slot_vals = gathered[:, : row_blocks * block_size].reshape(slot_count, row_blocks, block_size, block_size)
-    slot_cols = gathered[:, row_blocks * block_size, :row_blocks].astype(jnp.float32).T
-    column_ids = jnp.arange(block_count, dtype=jnp.float32)
-    one_hot = (slot_cols[:, :, None] == column_ids[None, None, :]).astype(jnp.bfloat16)
+    slot_cols = gathered[:, row_blocks * block_size, :row_blocks].astype(jnp.int32).T
 
     share = row_blocks // n_layer
-    send_blocks = (1 - layer) * share
-    keep_blocks = layer * share
+    send_first = ((1 - layer) * share).astype(jnp.int32).reshape(1)
+    keep_first = (layer * share).astype(jnp.int32).reshape(1)
 
-    def expand(first_block):
-        vals = lax.dynamic_slice_in_dim(slot_vals, first_block, share, 1)
-        hot = lax.dynamic_slice_in_dim(one_hot, first_block, share, 0)
-        dense = jnp.einsum("siab,isk->iakb", vals, hot, preferred_element_type=jnp.bfloat16)
-        dense = dense.reshape(share * block_size, block_count * block_size)
-        return jnp.dot(dense, panel, preferred_element_type=jnp.float32)
+    def expand(first):
+        return sparse_rows(first, slot_cols, gathered, panel, share)
 
-    sent = expand(send_blocks)
+    sent = expand(send_first)
     received = lax.ppermute(sent, "layer", perm=[(0, 1), (1, 0)])
-    summed = expand(keep_blocks) + received
+    summed = expand(keep_first) + received
     squares = summed * summed
     total_rows = row_blocks * block_size * lax.axis_size("row")
     column_sums = lax.psum(jnp.sum(squares, axis=0), ("row", "layer"))

time: 281 us -> 252 us (0.90)
  Pallas kernels: 0 us -> 52.2 us
  local copies, waits for them, and re-layouts: 57.1 us -> 11.8 us
  matrix products: 35.2 us -> 0 us
  waiting for transfers between devices: 150 us -> 133 us
  blocking collectives: 18.6 us -> 32.5 us
    pallas_call x0 -> x2, Pallas kernels: none -> 52.2 us  [sparse_rows(): pl.pallas_call(sparse_rows_kernel, out_shape=jax.ShapeDtypeStruct((share...]
    slice x3 -> x1, local copies, waits for them, and re-layouts: 46 us -> 0.92 us  [body(): gathered[:, row_blocks * block_size, :row_blocks].astype(jnp.int32)]
    dot_general x4 -> x0, matrix products: 35.2 us -> none  [the longest x2 23.8 us: expand(): return jnp.dot(dense, panel, preferred_element_type=jnp.float32)]
    ppermute x1, waiting for transfers between devices: 16.7 us -> 0.01 us  [body(): received = lax.ppermute(sent, 'layer', perm=[(0, 1), (1, 0)])]
    psum x1, blocking collectives: 9.29 us -> 23.2 us  [body(): column_sums = lax.psum(jnp.sum(squares, axis=0), ('row', 'layer'))]
  transfers between devices with their start and end apart: 3 -> 3, of which waited for: 3 -> 2; matrix products, arithmetic and copies ran while one was open for 6% -> 4% of each run, Pallas kernels for 0% -> 10%
where the time goes in v3:
time: 252 us
  waiting for transfers between devices  133 us (53%)
  Pallas kernels  52.2 us (21%)
  blocking collectives  32.5 us (13%)
  between operations  13.4 us (5%)
  local copies, waits for them, and re-layouts  11.8 us (5%)
  starting transfers between devices  5.52 us (2%)
  other arithmetic  3.15 us (1%)
    all_gather x1, waiting for transfers between devices, gather_slots(): return lax.all_gather(packed, COL_PARTS[:2], axis=0, tiled=True)  132 us
    pallas_call x2, Pallas kernels, sparse_rows(): pl.pallas_call(sparse_rows_kernel, out_shape=jax.ShapeDtypeStruct((share...  52.2 us
    psum x1, blocking collectives, body(): column_sums = lax.psum(jnp.sum(squares, axis=0), ('row', 'layer'))  23.2 us
    all_gather x1, blocking collectives, gather_slots(): packed = lax.all_gather(packed, COL_PARTS[2], axis=0, tiled=True)  9.31 us
  transfers between devices with their start and end apart: 3, of which 2 were waited for; matrix products, arithmetic and copies ran while one was open for 4% of the time, Pallas kernels for 10%

profile of v3, /device:TPU:1, one launch (start us, length us, event | category | flops | bytes accessed | tf_op | source)
XLA Modules:
  0.0 251.7 jit_solution(6187139918295625595)
XLA Ops:
  6.5 0.0 all-gather.2.cloned.1.call-start
  6.5 0.7 convert_bitcast_fusion.1
  7.2 1.0 fusion.2
  8.2 9.3 %all_gather.6 = bf16[2,1040,128]{2,1,0:T(8,128)(2,1)} all-gather(bf16[1,1040,128]{2,1,0:T(8,128)(2,1)S(1)} %fusion.2), channel_id=1, replica_groups=mesh['row'=2,'col_z'=8,'col_y'=4,'col_x'=2,'layer'=2] {'col_x'}, dimensions={0}, use_global_device_ids=true | all-gather | bytes 798720 | tf_op jit(solution)/shard_map/all_gather | solution.py:64
  17.5 0.0 all-gather.2.cloned.1.call-update
  17.5 2.7 %collective-permute-start = (bf16[4096,512]{1,0:T(8,128)(2,1)}, bf16[4096,512]{1,0:T(8,128)(2,1)}, u32[]{:S(2)}, u32[]{:S(2)}) collective-permute-start(bf16[4096,512]{1,0:T(8,128)(2,1)} %bitcast.12), channel_id=1, source_target_pairs={{0,128},{128,0},{1,129},{129,1},{2,130},{130,2},{3,131},{131,3},{4... | collective-permute-start | bytes 12582920 | tf_op jit(solution)/shard_map/ppermute | solution.py:75
  20.2 0.0 copy-start
  20.2 4.2 %broadcast_in_dim.2 = bf16[8192,512]{1,0:T(8,128)(2,1)} broadcast(bf16[]{:T(256)} %constant.47.clone.1), dimensions={} | broadcast | bytes 8388610 | tf_op jit(solution)/shard_map/broadcast_in_dim | solution.py:76
  24.4 0.0 copy-done
  24.4 2.3 constant_dynamic-update-slice_fusion.1
  26.7 0.7 collective-permute-done
  27.4 4.4 %constant_dynamic-update-slice_fusion.panel_ref = bf16[8192,512]{1,0:T(8,128)(2,1)} fusion(bf16[8192,512]{1,0:T(8,128)(2,1)} %constant_dynamic-update-slice_fusion.1, bf16[4096,512]{1,0:T(8,128)(2,1)} %collective-permute-done, s32[]{:T(128)S(6)} %select_n.7), kind=kLoop, calls=%fused_computation.8 | loop fusion | bytes 8388612 | tf_op jit(solution)/shard_map/dynamic_update_slice | solution.py:78
  31.8 132.3 %all-gather.2.cloned.1.call-done.vals_ref = bf16[64,1040,128]{2,1,0:T(8,128)(2,1)} async-done(((bf16[2,1040,128]{2,1,0:T(8,128)(2,1)}), bf16[64,1040,128]{2,1,0:T(8,128)(2,1)}) %all-gather.2.cloned.1.call-update) | async-done | bytes 17039376 | tf_op jit(solution)/shard_map/all_gather | solution.py:65
  164.1 0.9 slice.25
  165.0 0.1 copy.7
  165.1 26.4 %shard_map.38 = f32[512,512]{1,0:T(8,128)S(1)} custom-call(s32[1]{0:T(128)} %bitcast.6.first_ref, s32[8,64]{1,0:T(8,128)S(1)} %convert_bitcast_fusion.cols_ref, bf16[64,1040,128]{2,1,0:T(8,128)(2,1)} %all-gather.2.cloned.1.call-done.vals_ref, bf16[8192,512]{1,0:T(8,128)(2,1)} %constant_dynamic-update-slice_fusion.panel_ref), custom_call_target="tpu_custom_call" | custom-call | flops 4294967296 | bytes 17825792 | tf_op jit(solution)/shard_map/pallas_call | solution.py:37
  191.5 2.8 %collective-permute-start.1 = (f32[512,512]{1,0:T(8,128)S(1)}, f32[512,512]{1,0:T(8,128)S(1)}, u32[]{:S(2)}, u32[]{:S(2)}) collective-permute-start(f32[512,512]{1,0:T(8,128)S(1)} %shard_map.38), channel_id=1, source_target_pairs={{0,1},{1,0},{2,3},{3,2},{4,5},{5,4},{6,7},{7,6},{8,9},{9,8},{10,11... | collective-permute-start | bytes 3145736 | tf_op jit(solution)/shard_map/ppermute | solution.py:98
  194.3 25.8 %shard_map.37 = f32[512,512]{1,0:T(8,128)S(1)} custom-call(s32[1]{0:T(128)} %bitcast.first_ref, s32[8,64]{1,0:T(8,128)S(1)} %convert_bitcast_fusion.cols_ref, bf16[64,1040,128]{2,1,0:T(8,128)(2,1)} %all-gather.2.cloned.1.call-done.vals_ref, bf16[8192,512]{1,0:T(8,128)(2,1)} %constant_dynamic-update-slice_fusion.panel_ref), custom_call_target="tpu_custom_call" | custom-call | flops 4294967296 | bytes 17825792 | tf_op jit(solution)/shard_map/pallas_call | solution.py:37
  220.1 0.0 collective-permute-done.1
  220.1 0.3 fusion.1
  220.4 23.2 %psum.7 = f32[512]{0:T(512)S(1)} all-reduce(f32[512]{0:T(512)S(1)} %fusion.1), channel_id=1, replica_groups=mesh['row'=2,'col_z'=8,'col_y'=4,'col_x'=2,'layer'=2] {'row','layer'}, use_global_device_ids=true, to_apply=%region_1.0 | all-reduce | flops 512 | bytes 4096 | tf_op jit(solution)/shard_map/psum | solution.py:102
  243.7 1.2 broadcast_divide_fusion
  (2 shorter events, 0.0 us)
Async XLA Ops:
  6.5 157.6 %all-gather.2.cloned.1.call-start = ((), (), s32[]{:S(2)}) async-start(), calls=%async_computation | async-start | bytes 17571840 | tf_op jit(solution)/shard_map/all_gather | solution.py:65
  17.5 9.8 %collective-permute-start = (bf16[4096,512]{1,0:T(8,128)(2,1)}, bf16[4096,512]{1,0:T(8,128)(2,1)}, u32[]{:S(2)}, u32[]{:S(2)}) collective-permute-start(bf16[4096,512]{1,0:T(8,128)(2,1)} %bitcast.12), channel_id=1, source_target_pairs={{0,128},{128,0},{1,129},{129,1},{2,130},{130,2},{3,131},{131,3},{4... | collective-permute-start | bytes 12582920 | tf_op jit(solution)/shard_map/ppermute | solution.py:75
  20.2 4.2 %copy-start = (bf16[1,4096,512]{2,1,0:T(8,128)(2,1)S(1)}, bf16[1,4096,512]{2,1,0:T(8,128)(2,1)}, u32[]{:S(2)}) copy-start(bf16[1,4096,512]{2,1,0:T(8,128)(2,1)} %param.7) | copy-start | bytes 12582916
  191.5 28.6 %collective-permute-start.1 = (f32[512,512]{1,0:T(8,128)S(1)}, f32[512,512]{1,0:T(8,128)S(1)}, u32[]{:S(2)}, u32[]{:S(2)}) collective-permute-start(f32[512,512]{1,0:T(8,128)S(1)} %shard_map.38), channel_id=1, source_target_pairs={{0,1},{1,0},{2,3},{3,2},{4,5},{5,4},{6,7},{7,6},{8,9},{9,8},{10,11... | collective-permute-start | bytes 3145736 | tf_op jit(solution)/shard_map/ppermute | solution.py:98
Sparse Core Ops, SparseCore 0:
  17.6 146.4 all-gather.1

commit v4 on v3

--- a/solution.py
+++ b/solution.py
@@ -6,54 +6,65 @@
 from jax.sharding import Mesh, PartitionSpec as P
 
 
-def sparse_rows_kernel(first_ref, cols_ref, vals_ref, panel_ref, out_ref, acc_ref):
-    i = pl.program_id(0)
-    block_row = first_ref[0] + i
+def dense_rows_kernel(first_ref, slot_of_ref, vals_ref, panel_ref, out_ref, stage_ref):
     block_size = vals_ref.shape[-1]
-    block_count = panel_ref.shape[0] // block_size
-    acc_ref[...] = jnp.zeros_like(acc_ref)
+    share = vals_ref.shape[1] // block_size
+    width = stage_ref.shape[1] // block_size
+    chunks = panel_ref.shape[0] // stage_ref.shape[1]
+    first = first_ref[0]
+    out_ref[...] = jnp.zeros_like(out_ref)
 
-    def step(s, carry):
-        col = cols_ref[block_row, s]
+    def chunk(j, carry):
+        for i in range(share):
+            for kk in range(width):
+                slot = slot_of_ref[first + i, j * width + kk]
+                rows = pl.ds(i * block_size, block_size)
+                cols = pl.ds(kk * block_size, block_size)
 
-        @pl.when(jnp.logical_and(col >= 0, col < block_count))
-        def _():
-            start = pl.multiple_of(col * block_size, block_size)
-            acc_ref[...] += jnp.dot(
-                vals_ref[s], panel_ref[pl.ds(start, block_size), :],
-                preferred_element_type=jnp.float32,
-            )
+                @pl.when(slot >= 0)
+                def _():
+                    stage_ref[rows, cols] = vals_ref[slot, rows, :]
 
+                @pl.when(slot < 0)
+                def _():
+                    stage_ref[rows, cols] = jnp.zeros((block_size, block_size), stage_ref.dtype)
+
+        start = pl.multiple_of(j * stage_ref.shape[1], stage_ref.shape[1])
+        out_ref[...] += jnp.dot(
+            stage_ref[...], panel_ref[pl.ds(start, stage_ref.shape[1]), :],
+            preferred_element_type=jnp.float32,
+        )
         return carry
 
-    lax.fori_loop(0, vals_ref.shape[0], step, 0)
-    out_ref[...] = acc_ref[...]
+    lax.fori_loop(0, chunks, chunk, 0)
 
 
-def sparse_rows(first, cols, gathered, panel, share):
+def dense_rows(first, slot_of, gathered, panel, share, width=4):
     slot_count = gathered.shape[0]
     block_size = gathered.shape[-1]
-    width = panel.shape[1]
+    out_cols = panel.shape[1]
     return pl.pallas_call(
-        sparse_rows_kernel,
-        out_shape=jax.ShapeDtypeStruct((share * block_size, width), jnp.float32),
+        dense_rows_kernel,
+        out_shape=jax.ShapeDtypeStruct((share * block_size, out_cols), jnp.float32),
         grid_spec=pltpu.PrefetchScalarGridSpec(
             num_scalar_prefetch=2,
-            grid=(share,),
+            grid=(1,),
             in_specs=[
-                pl.BlockSpec((slot_count, block_size, block_size), lambda i, f, c: (0, f[0] + i, 0)),
-                pl.BlockSpec(panel.shape, lambda i, f, c: (0, 0), pipeline_mode=pl.Buffered(1)),
+                pl.BlockSpec((slot_count, share * block_size, block_size),
+                             lambda i, f, t: (0, f[0] // share, 0), pipeline_mode=pl.Buffered(1)),
+                pl.BlockSpec(panel.shape, lambda i, f, t: (0, 0), pipeline_mode=pl.Buffered(1)),
             ],
-            out_specs=pl.BlockSpec((block_size, width), lambda i, f, c: (i, 0)),
-            scratch_shapes=[pltpu.VMEM((block_size, width), jnp.float32)],
+            out_specs=pl.BlockSpec((share * block_size, out_cols), lambda i, f, t: (0, 0)),
+            scratch_shapes=[pltpu.VMEM((share * block_size, width * block_size), jnp.bfloat16)],
         ),
         compiler_params=pltpu.CompilerParams(vmem_limit_bytes=48 * 1024 * 1024),
         cost_estimate=pl.CostEstimate(
-            flops=2 * share * slot_count * block_size * block_size * width,
+            flops=2 * share * block_size * panel.shape[0] * out_cols,
             transcendentals=0,
-            bytes_accessed=share * slot_count * block_size * block_size * 2 + panel.size * 2 + share * block_size * width * 4,
+            bytes_accessed=slot_count * share * block_size * block_size * 2 + panel.size * 2 + share * block_size * out_cols * 4,
         ),
-    )(first, cols, gathered, panel)
+    )(first, slot_of, gathered, panel)
+
 
 COL_FACTORS = (8, 4, 2)
 COL_PARTS = ("col_z", "col_y", "col_x")
@@ -86,13 +97,17 @@
     packed = jnp.concatenate([stacked, col_tile], axis=1)
     gathered = gather_slots(packed, split)
     slot_cols = gathered[:, row_blocks * block_size, :row_blocks].astype(jnp.int32).T
+    slot_count = gathered.shape[0]
+    hit = slot_cols[:, :, None] == jnp.arange(block_count, dtype=jnp.int32)[None, None, :]
+    slot_ids = jnp.arange(slot_count, dtype=jnp.int32)[None, :, None]
+    slot_of = jnp.max(jnp.where(hit, slot_ids, -1), axis=1)
 
     share = row_blocks // n_layer
     send_first = ((1 - layer) * share).astype(jnp.int32).reshape(1)
     keep_first = (layer * share).astype(jnp.int32).reshape(1)
 
     def expand(first):
-        return sparse_rows(first, slot_cols, gathered, panel, share)
+        return dense_rows(first, slot_of, gathered, panel, share)
 
     sent = expand(send_first)
     received = lax.ppermute(sent, "layer", perm=[(0, 1), (1, 0)])

time: 252 us -> 224 us (0.89)
  Pallas kernels: 52.2 us -> 35.5 us
  blocking collectives: 32.5 us -> 18.3 us
  waiting for transfers between devices: 133 us -> 138 us
    pallas_call x2, Pallas kernels: 52.2 us -> 35.5 us  [dense_rows(): pl.pallas_call(dense_rows_kernel, out_shape=jax.ShapeDtypeStruct((share *...]
    psum x1, blocking collectives: 23.2 us -> 9.01 us  [body(): column_sums = lax.psum(jnp.sum(squares, axis=0), ('row', 'layer'))]
    ppermute x1, waiting for transfers between devices: 0.01 us -> 5.01 us  [body(): received = lax.ppermute(sent, 'layer', perm=[(0, 1), (1, 0)])]
  transfers between devices with their start and end apart: 3 -> 3, of which waited for: 2 -> 3; matrix products, arithmetic and copies ran while one was open for 4% -> 5% of each run, Pallas kernels for 10% -> 8%
where the time goes in v4:
time: 224 us
  waiting for transfers between devices  138 us (62%)
  Pallas kernels  35.5 us (16%)
  blocking collectives  18.3 us (8%)
  between operations  13.4 us (6%)
  local copies, waits for them, and re-layouts  10.9 us (5%)
  other arithmetic  4.23 us (2%)
  starting transfers between devices  3.83 us (2%)
    all_gather x1, waiting for transfers between devices, gather_slots(): return lax.all_gather(packed, COL_PARTS[:2], axis=0, tiled=True)  132 us
    pallas_call x2, Pallas kernels, dense_rows(): pl.pallas_call(dense_rows_kernel, out_shape=jax.ShapeDtypeStruct((share *...  35.5 us
    all_gather x1, blocking collectives, gather_slots(): packed = lax.all_gather(packed, COL_PARTS[2], axis=0, tiled=True)  9.31 us
    psum x1, blocking collectives, body(): column_sums = lax.psum(jnp.sum(squares, axis=0), ('row', 'layer'))  9.01 us
    ppermute x1, waiting for transfers between devices, body(): received = lax.ppermute(sent, 'layer', perm=[(0, 1), (1, 0)])  5.01 us
  transfers between devices with their start and end apart: 3, of which 3 were waited for; matrix products, arithmetic and copies ran while one was open for 5% of the time, Pallas kernels for 8%

profile of v4, /device:TPU:1, one launch (start us, length us, event | category | flops | bytes accessed | tf_op | source)
XLA Modules:
  0.0 224.2 jit_solution(4602299976951212864)
XLA Ops:
  6.5 0.0 all-gather.2.cloned.1.call-start
  6.5 0.7 convert_bitcast_fusion
  7.2 1.0 fusion.2
  8.2 9.3 %all_gather.6 = bf16[2,1040,128]{2,1,0:T(8,128)(2,1)} all-gather(bf16[1,1040,128]{2,1,0:T(8,128)(2,1)S(1)} %fusion.2), channel_id=1, replica_groups=mesh['row'=2,'col_z'=8,'col_y'=4,'col_x'=2,'layer'=2] {'col_x'}, dimensions={0}, use_global_device_ids=true | all-gather | bytes 798720 | tf_op jit(solution)/shard_map/all_gather | solution.py:75
  17.5 0.0 all-gather.2.cloned.1.call-update
  17.5 2.7 %collective-permute-start = (bf16[4096,512]{1,0:T(8,128)(2,1)}, bf16[4096,512]{1,0:T(8,128)(2,1)}, u32[]{:S(2)}, u32[]{:S(2)}) collective-permute-start(bf16[4096,512]{1,0:T(8,128)(2,1)} %bitcast.10), channel_id=1, source_target_pairs={{0,128},{128,0},{1,129},{129,1},{2,130},{130,2},{3,131},{131,3},{4... | collective-permute-start | bytes 12582920 | tf_op jit(solution)/shard_map/ppermute | solution.py:86
  20.2 0.0 copy-start
  20.2 4.2 %broadcast_in_dim.22 = bf16[8192,512]{1,0:T(8,128)(2,1)} broadcast(bf16[]{:T(256)} %constant.49.clone.1), dimensions={} | broadcast | bytes 8388610 | tf_op jit(solution)/shard_map/broadcast_in_dim | solution.py:87
  24.4 0.0 copy-done
  24.4 2.2 constant_dynamic-update-slice_fusion.1
  26.6 0.7 collective-permute-done
  27.4 4.4 %constant_dynamic-update-slice_fusion.panel_ref = bf16[8192,512]{1,0:T(8,128)(2,1)} fusion(bf16[8192,512]{1,0:T(8,128)(2,1)} %constant_dynamic-update-slice_fusion.1, bf16[4096,512]{1,0:T(8,128)(2,1)} %collective-permute-done, s32[]{:T(128)S(6)} %select_n.12), kind=kLoop, calls=%fused_computation.10 | loop fusion | bytes 8388612 | tf_op jit(solution)/shard_map/dynamic_update_slice | solution.py:89
  31.8 132.3 %all-gather.2.cloned.1.call-done.vals_ref = bf16[64,1040,128]{2,1,0:T(8,128)(2,1)} async-done(((bf16[2,1040,128]{2,1,0:T(8,128)(2,1)}), bf16[64,1040,128]{2,1,0:T(8,128)(2,1)}) %all-gather.2.cloned.1.call-update) | async-done | bytes 17039376 | tf_op jit(solution)/shard_map/all_gather | solution.py:76
  164.1 0.9 slice_convert_fusion
  165.0 0.1 copy.6
  165.1 0.2 select_reduce_fusion.slot_of_ref
  165.3 17.8 %shard_map.38 = f32[512,512]{1,0:T(8,128)S(1)} custom-call(s32[1]{0:T(128)} %bitcast.6.first_ref, s32[8,64]{1,0:T(8,128)S(1)} %select_reduce_fusion.slot_of_ref, bf16[64,1040,128]{2,1,0:T(8,128)(2,1)} %all-gather.2.cloned.1.call-done.vals_ref, bf16[8192,512]{1,0:T(8,128)(2,1)} %constant_dynamic-update-slice_fusion.panel_ref), custom_call_target="tpu_custom_call" | custom-call | flops 4294967296 | bytes 17825792 | tf_op jit(solution)/shard_map/pallas_call | solution.py:46
  183.1 1.1 collective-permute-start.1
  184.2 17.7 %shard_map.37 = f32[512,512]{1,0:T(8,128)S(1)} custom-call(s32[1]{0:T(128)} %bitcast.first_ref, s32[8,64]{1,0:T(8,128)S(1)} %select_reduce_fusion.slot_of_ref, bf16[64,1040,128]{2,1,0:T(8,128)(2,1)} %all-gather.2.cloned.1.call-done.vals_ref, bf16[8192,512]{1,0:T(8,128)(2,1)} %constant_dynamic-update-slice_fusion.panel_ref), custom_call_target="tpu_custom_call" | custom-call | flops 4294967296 | bytes 17825792 | tf_op jit(solution)/shard_map/pallas_call | solution.py:46
  201.9 5.0 %collective-permute-done.1 = f32[512,512]{1,0:T(8,128)S(1)} collective-permute-done((f32[512,512]{1,0:T(8,128)S(1)}, f32[512,512]{1,0:T(8,128)S(1)}, u32[]{:S(2)}, u32[]{:S(2)}) %collective-permute-start.1) | collective-permute-done | bytes 1048608 | tf_op jit(solution)/shard_map/ppermute | solution.py:113
  206.9 0.3 fusion.1
  207.2 9.0 %psum.7 = f32[512]{0:T(512)S(1)} all-reduce(f32[512]{0:T(512)S(1)} %fusion.1), channel_id=1, replica_groups=mesh['row'=2,'col_z'=8,'col_y'=4,'col_x'=2,'layer'=2] {'row','layer'}, use_global_device_ids=true, to_apply=%region_2.3 | all-reduce | flops 512 | bytes 4096 | tf_op jit(solution)/shard_map/psum | solution.py:117
  216.2 1.2 broadcast_divide_fusion
  (1 shorter events, 0.0 us)
Async XLA Ops:
  6.5 157.6 %all-gather.2.cloned.1.call-start = ((), (), s32[]{:S(2)}) async-start(), calls=%async_computation | async-start | bytes 17571840 | tf_op jit(solution)/shard_map/all_gather | solution.py:76
  17.5 9.8 %collective-permute-start = (bf16[4096,512]{1,0:T(8,128)(2,1)}, bf16[4096,512]{1,0:T(8,128)(2,1)}, u32[]{:S(2)}, u32[]{:S(2)}) collective-permute-start(bf16[4096,512]{1,0:T(8,128)(2,1)} %bitcast.10), channel_id=1, source_target_pairs={{0,128},{128,0},{1,129},{129,1},{2,130},{130,2},{3,131},{131,3},{4... | collective-permute-start | bytes 12582920 | tf_op jit(solution)/shard_map/ppermute | solution.py:86
  20.2 4.2 %copy-start = (bf16[1,4096,512]{2,1,0:T(8,128)(2,1)S(1)}, bf16[1,4096,512]{2,1,0:T(8,128)(2,1)}, u32[]{:S(2)}) copy-start(bf16[1,4096,512]{2,1,0:T(8,128)(2,1)} %param.7) | copy-start | bytes 12582916
  183.1 23.8 %collective-permute-start.1 = (f32[512,512]{1,0:T(8,128)S(1)}, f32[512,512]{1,0:T(8,128)S(1)}, u32[]{:S(2)}, u32[]{:S(2)}) collective-permute-start(f32[512,512]{1,0:T(8,128)S(1)} %shard_map.38), channel_id=1, source_target_pairs={{0,1},{1,0},{2,3},{3,2},{4,5},{5,4},{6,7},{7,6},{8,9},{9,8},{10,11... | collective-permute-start | bytes 3145736 | tf_op jit(solution)/shard_map/ppermute | solution.py:113
Sparse Core Ops, SparseCore 0:
  17.6 146.4 all-gather.1

commit v5 on v4

--- a/solution.py
+++ b/solution.py
@@ -10,33 +10,23 @@
     block_size = vals_ref.shape[-1]
     share = vals_ref.shape[1] // block_size
     width = stage_ref.shape[1] // block_size
-    chunks = panel_ref.shape[0] // stage_ref.shape[1]
+    j = pl.program_id(0)
     first = first_ref[0]
-    out_ref[...] = jnp.zeros_like(out_ref)
 
-    def chunk(j, carry):
-        for i in range(share):
-            for kk in range(width):
-                slot = slot_of_ref[first + i, j * width + kk]
-                rows = pl.ds(i * block_size, block_size)
-                cols = pl.ds(kk * block_size, block_size)
+    @pl.when(j == 0)
+    def _():
+        out_ref[...] = jnp.zeros_like(out_ref)
 
-                @pl.when(slot >= 0)
-                def _():
-                    stage_ref[rows, cols] = vals_ref[slot, rows, :]
+    for i in range(share):
+        for kk in range(width):
+            slot = slot_of_ref[first + i, j * width + kk]
+            rows = pl.ds(i * block_size, block_size)
+            block = vals_ref[jnp.maximum(slot, 0), rows, :]
+            stage_ref[rows, pl.ds(kk * block_size, block_size)] = jnp.where(
+                slot >= 0, block, jnp.zeros_like(block)
+            )
 
-                @pl.when(slot < 0)
-                def _():
-                    stage_ref[rows, cols] = jnp.zeros((block_size, block_size), stage_ref.dtype)
-
-        start = pl.multiple_of(j * stage_ref.shape[1], stage_ref.shape[1])
-        out_ref[...] += jnp.dot(
-            stage_ref[...], panel_ref[pl.ds(start, stage_ref.shape[1]), :],
-            preferred_element_type=jnp.float32,
-        )
-        return carry
-
-    lax.fori_loop(0, chunks, chunk, 0)
+    out_ref[...] += jnp.dot(stage_ref[...], panel_ref[...], preferred_element_type=jnp.float32)
 
 
 def dense_rows(first, slot_of, gathered, panel, share, width=4):
@@ -48,13 +38,13 @@
         out_shape=jax.ShapeDtypeStruct((share * block_size, out_cols), jnp.float32),
         grid_spec=pltpu.PrefetchScalarGridSpec(
             num_scalar_prefetch=2,
-            grid=(1,),
+            grid=(panel.shape[0] // (width * block_size),),
             in_specs=[
                 pl.BlockSpec((slot_count, share * block_size, block_size),
-                             lambda i, f, t: (0, f[0] // share, 0), pipeline_mode=pl.Buffered(1)),
-                pl.BlockSpec(panel.shape, lambda i, f, t: (0, 0), pipeline_mode=pl.Buffered(1)),
+                             lambda j, f, t: (0, f[0] // share, 0), pipeline_mode=pl.Buffered(1)),
+                pl.BlockSpec((width * block_size, out_cols), lambda j, f, t: (j, 0)),
             ],
-            out_specs=pl.BlockSpec((share * block_size, out_cols), lambda i, f, t: (0, 0)),
+            out_specs=pl.BlockSpec((share * block_size, out_cols), lambda j, f, t: (0, 0)),
             scratch_shapes=[pltpu.VMEM((share * block_size, width * block_size), jnp.bfloat16)],
         ),
         compiler_params=pltpu.CompilerParams(vmem_limit_bytes=48 * 1024 * 1024),

time: 224 us -> 223 us (level)
  Pallas kernels: 35.5 us -> 32.1 us
    pallas_call x2, Pallas kernels: 35.5 us -> 32.1 us  [dense_rows(): pl.pallas_call(dense_rows_kernel, out_shape=jax.ShapeDtypeStruct((share *...]
  transfers between devices with their start and end apart: 3 -> 3, of which waited for: 3 -> 3; matrix products, arithmetic and copies ran while one was open for 5% -> 5% of each run, Pallas kernels for 8% -> 7%
where the time goes in v5:
time: 223 us
  waiting for transfers between devices  139 us (62%)
  Pallas kernels  32.1 us (14%)
  blocking collectives  18.6 us (8%)
  between operations  13.4 us (6%)
  local copies, waits for them, and re-layouts  10.9 us (5%)
  other arithmetic  4.23 us (2%)
  starting transfers between devices  4 us (2%)
    all_gather x1, waiting for transfers between devices, gather_slots(): return lax.all_gather(packed, COL_PARTS[:2], axis=0, tiled=True)  132 us
    pallas_call x2, Pallas kernels, dense_rows(): pl.pallas_call(dense_rows_kernel, out_shape=jax.ShapeDtypeStruct((share *...  32.1 us
    all_gather x1, blocking collectives, gather_slots(): packed = lax.all_gather(packed, COL_PARTS[2], axis=0, tiled=True)  9.31 us
    psum x1, blocking collectives, body(): column_sums = lax.psum(jnp.sum(squares, axis=0), ('row', 'layer'))  9.3 us
    ppermute x1, waiting for transfers between devices, body(): received = lax.ppermute(sent, 'layer', perm=[(0, 1), (1, 0)])  6.37 us
  transfers between devices with their start and end apart: 3, of which 3 were waited for; matrix products, arithmetic and copies ran while one was open for 5% of the time, Pallas kernels for 7%

profile of v5, /device:TPU:1, one launch (start us, length us, event | category | flops | bytes accessed | tf_op | source)
XLA Modules:
  0.0 222.7 jit_solution(2996239055758034527)
XLA Ops:
  6.5 0.0 all-gather.2.cloned.1.call-start
  6.5 0.7 convert_bitcast_fusion
  7.2 1.0 fusion.2
  8.2 9.3 %all_gather.6 = bf16[2,1040,128]{2,1,0:T(8,128)(2,1)} all-gather(bf16[1,1040,128]{2,1,0:T(8,128)(2,1)S(1)} %fusion.2), channel_id=1, replica_groups=mesh['row'=2,'col_z'=8,'col_y'=4,'col_x'=2,'layer'=2] {'col_x'}, dimensions={0}, use_global_device_ids=true | all-gather | bytes 798720 | tf_op jit(solution)/shard_map/all_gather | solution.py:65
  17.5 0.0 all-gather.2.cloned.1.call-update
  17.5 2.7 %collective-permute-start = (bf16[4096,512]{1,0:T(8,128)(2,1)}, bf16[4096,512]{1,0:T(8,128)(2,1)}, u32[]{:S(2)}, u32[]{:S(2)}) collective-permute-start(bf16[4096,512]{1,0:T(8,128)(2,1)} %bitcast.10), channel_id=1, source_target_pairs={{0,128},{128,0},{1,129},{129,1},{2,130},{130,2},{3,131},{131,3},{4... | collective-permute-start | bytes 12582920 | tf_op jit(solution)/shard_map/ppermute | solution.py:76
  20.2 0.0 copy-start
  20.2 4.2 %broadcast_in_dim.22 = bf16[8192,512]{1,0:T(8,128)(2,1)} broadcast(bf16[]{:T(256)} %constant.49.clone.1), dimensions={} | broadcast | bytes 8388610 | tf_op jit(solution)/shard_map/broadcast_in_dim | solution.py:77
  24.4 0.0 copy-done
  24.4 2.2 %constant_dynamic-update-slice_fusion.1 = bf16[8192,512]{1,0:T(8,128)(2,1)} fusion(bf16[8192,512]{1,0:T(8,128)(2,1)} %broadcast_in_dim.22, s32[]{:T(128)S(6)} %select_n.11, bf16[1,4096,512]{2,1,0:T(8,128)(2,1)S(1)} %copy-done), kind=kLoop, calls=%fused_computation.11 | loop fusion | bytes 8388612 | tf_op jit(solution)/shard_map/dynamic_update_slice | solution.py:78
  26.6 0.7 collective-permute-done
  27.4 4.4 %constant_dynamic-update-slice_fusion.panel_ref = bf16[8192,512]{1,0:T(8,128)(2,1)} fusion(bf16[8192,512]{1,0:T(8,128)(2,1)} %constant_dynamic-update-slice_fusion.1, bf16[4096,512]{1,0:T(8,128)(2,1)} %collective-permute-done, s32[]{:T(128)S(6)} %select_n.12), kind=kLoop, calls=%fused_computation.10 | loop fusion | bytes 8388612 | tf_op jit(solution)/shard_map/dynamic_update_slice | solution.py:79
  31.8 132.3 %all-gather.2.cloned.1.call-done.vals_ref = bf16[64,1040,128]{2,1,0:T(8,128)(2,1)} async-done(((bf16[2,1040,128]{2,1,0:T(8,128)(2,1)}), bf16[64,1040,128]{2,1,0:T(8,128)(2,1)}) %all-gather.2.cloned.1.call-update) | async-done | bytes 17039376 | tf_op jit(solution)/shard_map/all_gather | solution.py:66
  164.1 0.9 slice_convert_fusion
  165.0 0.1 copy.6
  165.1 0.2 select_reduce_fusion.slot_of_ref
  165.3 16.0 %shard_map.38 = f32[512,512]{1,0:T(8,128)S(1)} custom-call(s32[1]{0:T(128)} %bitcast.6.first_ref, s32[8,64]{1,0:T(8,128)S(1)} %select_reduce_fusion.slot_of_ref, bf16[64,1040,128]{2,1,0:T(8,128)(2,1)} %all-gather.2.cloned.1.call-done.vals_ref, bf16[8192,512]{1,0:T(8,128)(2,1)} %constant_dynamic-update-slice_fusion.panel_ref), custom_call_target="tpu_custom_call" | custom-call | flops 4294967296 | bytes 17825792 | tf_op jit(solution)/shard_map/pallas_call | solution.py:36
  181.3 1.3 collective-permute-start.1
  182.6 16.0 %shard_map.37 = f32[512,512]{1,0:T(8,128)S(1)} custom-call(s32[1]{0:T(128)} %bitcast.first_ref, s32[8,64]{1,0:T(8,128)S(1)} %select_reduce_fusion.slot_of_ref, bf16[64,1040,128]{2,1,0:T(8,128)(2,1)} %all-gather.2.cloned.1.call-done.vals_ref, bf16[8192,512]{1,0:T(8,128)(2,1)} %constant_dynamic-update-slice_fusion.panel_ref), custom_call_target="tpu_custom_call" | custom-call | flops 4294967296 | bytes 17825792 | tf_op jit(solution)/shard_map/pallas_call | solution.py:36
  198.6 6.4 %collective-permute-done.1 = f32[512,512]{1,0:T(8,128)S(1)} collective-permute-done((f32[512,512]{1,0:T(8,128)S(1)}, f32[512,512]{1,0:T(8,128)S(1)}, u32[]{:S(2)}, u32[]{:S(2)}) %collective-permute-start.1) | collective-permute-done | bytes 1048608 | tf_op jit(solution)/shard_map/ppermute | solution.py:103
  205.0 0.3 fusion.1
  205.3 9.3 %psum.7 = f32[512]{0:T(512)S(1)} all-reduce(f32[512]{0:T(512)S(1)} %fusion.1), channel_id=1, replica_groups=mesh['row'=2,'col_z'=8,'col_y'=4,'col_x'=2,'layer'=2] {'row','layer'}, use_global_device_ids=true, to_apply=%region_2.3 | all-reduce | flops 512 | bytes 4096 | tf_op jit(solution)/shard_map/psum | solution.py:107
  214.6 1.2 broadcast_divide_fusion
  (1 shorter events, 0.0 us)
Async XLA Ops:
  6.5 157.6 %all-gather.2.cloned.1.call-start = ((), (), s32[]{:S(2)}) async-start(), calls=%async_computation | async-start | bytes 17571840 | tf_op jit(solution)/shard_map/all_gather | solution.py:66
  17.5 9.8 %collective-permute-start = (bf16[4096,512]{1,0:T(8,128)(2,1)}, bf16[4096,512]{1,0:T(8,128)(2,1)}, u32[]{:S(2)}, u32[]{:S(2)}) collective-permute-start(bf16[4096,512]{1,0:T(8,128)(2,1)} %bitcast.10), channel_id=1, source_target_pairs={{0,128},{128,0},{1,129},{129,1},{2,130},{130,2},{3,131},{131,3},{4... | collective-permute-start | bytes 12582920 | tf_op jit(solution)/shard_map/ppermute | solution.py:76
  20.2 4.2 %copy-start = (bf16[1,4096,512]{2,1,0:T(8,128)(2,1)S(1)}, bf16[1,4096,512]{2,1,0:T(8,128)(2,1)}, u32[]{:S(2)}) copy-start(bf16[1,4096,512]{2,1,0:T(8,128)(2,1)} %param.7) | copy-start | bytes 12582916
  181.3 23.7 %collective-permute-start.1 = (f32[512,512]{1,0:T(8,128)S(1)}, f32[512,512]{1,0:T(8,128)S(1)}, u32[]{:S(2)}, u32[]{:S(2)}) collective-permute-start(f32[512,512]{1,0:T(8,128)S(1)} %shard_map.38), channel_id=1, source_target_pairs={{0,1},{1,0},{2,3},{3,2},{4,5},{5,4},{6,7},{7,6},{8,9},{9,8},{10,11... | collective-permute-start | bytes 3145736 | tf_op jit(solution)/shard_map/ppermute | solution.py:103
Sparse Core Ops, SparseCore 0:
  17.6 146.4 all-gather.1

commit v6 on v5

--- a/solution.py
+++ b/solution.py
@@ -62,7 +62,8 @@
 
 def gather_slots(packed, split):
     if split:
-        packed = lax.all_gather(packed, COL_PARTS[2], axis=0, tiled=True)
+        partner = lax.ppermute(packed, COL_PARTS[2], perm=[(0, 1), (1, 0)])
+        packed = jnp.concatenate([packed, partner], axis=0)
         return lax.all_gather(packed, COL_PARTS[:2], axis=0, tiled=True)
     return lax.all_gather(packed, "col", axis=0, tiled=True)
 
@@ -96,12 +97,12 @@
     send_first = ((1 - layer) * share).astype(jnp.int32).reshape(1)
     keep_first = (layer * share).astype(jnp.int32).reshape(1)
 
-    def expand(first):
-        return dense_rows(first, slot_of, gathered, panel, share)
-
-    sent = expand(send_first)
-    received = lax.ppermute(sent, "layer", perm=[(0, 1), (1, 0)])
-    summed = expand(keep_first) + received
+    piece = share // 2
+    received = []
+    for part in range(2):
+        sent = dense_rows(send_first + part * piece, slot_of, gathered, panel, piece)
+        received.append(lax.ppermute(sent, "layer", perm=[(0, 1), (1, 0)]))
+    summed = dense_rows(keep_first, slot_of, gathered, panel, share) + jnp.concatenate(received, axis=0)
     squares = summed * summed
     total_rows = row_blocks * block_size * lax.axis_size("row")
     column_sums = lax.psum(jnp.sum(squares, axis=0), ("row", "layer"))

time: 223 us -> 229 us (1.027)
  Pallas kernels: 32.1 us -> 43.1 us
  blocking collectives: 18.6 us -> 8.93 us
  starting transfers between devices: 4 us -> 7.91 us
    pallas_call x2 -> x3, Pallas kernels: 32.1 us -> 43.1 us  [dense_rows(): pl.pallas_call(dense_rows_kernel, out_shape=jax.ShapeDtypeStruct((share *...]
    all_gather x1 -> x0, blocking collectives: 9.31 us -> none  [gather_slots(): packed = lax.all_gather(packed, COL_PARTS[2], axis=0, tiled=True)]
    ppermute x1 -> x3, starting transfers between devices: 1.28 us -> 5.3 us  [the longest x1 3.66 us: gather_slots(): partner = lax.ppermute(packed, COL_PARTS[2], perm=[(0, 1), (1, 0)])]
    ppermute x1 -> x3, waiting for transfers between devices: 6.37 us -> 5.07 us  [the longest x1 5.06 us: gather_slots(): partner = lax.ppermute(packed, COL_PARTS[2], perm=[(0, 1), (1, 0)])]
  transfers between devices with their start and end apart: 3 -> 5, of which waited for: 3 -> 3; matrix products, arithmetic and copies ran while one was open for 5% -> 5% of each run, Pallas kernels for 7% -> 13%
where the time goes in v6:
time: 229 us; the launch traced here: 228 us
  waiting for transfers between devices  138 us (60%)
  Pallas kernels  43.1 us (19%)
  between operations  13.5 us (6%)
  local copies, waits for them, and re-layouts  10.9 us (5%)
  blocking collectives  8.93 us (4%)
  starting transfers between devices  7.91 us (3%)
  other arithmetic  6.01 us (3%)
    all_gather x1, waiting for transfers between devices, gather_slots(): return lax.all_gather(packed, COL_PARTS[:2], axis=0, tiled=True)  132 us
    pallas_call x3, Pallas kernels, dense_rows(): pl.pallas_call(dense_rows_kernel, out_shape=jax.ShapeDtypeStruct((share *...  43.1 us
    psum x1, blocking collectives, body(): column_sums = lax.psum(jnp.sum(squares, axis=0), ('row', 'layer'))  8.93 us
    ppermute x1, waiting for transfers between devices, gather_slots(): partner = lax.ppermute(packed, COL_PARTS[2], perm=[(0, 1), (1, 0)])  5.06 us
  transfers between devices with their start and end apart: 5, of which 3 were waited for; matrix products, arithmetic and copies ran while one was open for 5% of the time, Pallas kernels for 13%

profile of v6, /device:TPU:1, one launch (start us, length us, event | category | flops | bytes accessed | tf_op | source)
XLA Modules:
  0.0 228.4 jit_solution(10029284729242808998)
XLA Ops:
  6.5 0.7 convert_bitcast_fusion
  7.2 1.0 pad_maximum_fusion.1
  8.2 3.7 %collective-permute-start = (bf16[1,1040,128]{2,1,0:T(8,128)(2,1)S(1)}, bf16[1,1040,128]{2,1,0:T(8,128)(2,1)S(1)}, u32[]{:S(2)}, u32[]{:S(2)}) collective-permute-start(bf16[1,1040,128]{2,1,0:T(8,128)(2,1)S(1)} %pad_maximum_fusion.1), channel_id=1, source_target_pairs={{0,2},{2,0},{1,3},{3,1},{4,6},{6,4},{5,7},{7,5},{8,10},{10,8},{9,1... | collective-permute-start | bytes 798728 | tf_op jit(solution)/shard_map/ppermute | solution.py:65
  11.8 5.1 %collective-permute-done = bf16[1,1040,128]{2,1,0:T(8,128)(2,1)S(1)} collective-permute-done((bf16[1,1040,128]{2,1,0:T(8,128)(2,1)S(1)}, bf16[1,1040,128]{2,1,0:T(8,128)(2,1)S(1)}, u32[]{:S(2)}, u32[]{:S(2)}) %collective-permute-start) | collective-permute-done | bytes 266272 | tf_op jit(solution)/shard_map/ppermute | solution.py:65
  16.9 1.8 pad_maximum_fusion
  18.7 0.0 all-gather.2.cloned.1.call-update
  18.7 2.6 %collective-permute-start.1 = (bf16[4096,512]{1,0:T(8,128)(2,1)}, bf16[4096,512]{1,0:T(8,128)(2,1)}, u32[]{:S(2)}, u32[]{:S(2)}) collective-permute-start(bf16[4096,512]{1,0:T(8,128)(2,1)} %bitcast.10), channel_id=1, source_target_pairs={{0,128},{128,0},{1,129},{129,1},{2,130},{130,2},{3,131},{131,3},{4... | collective-permute-start | bytes 12582920 | tf_op jit(solution)/shard_map/ppermute | solution.py:77
  21.3 4.2 %broadcast_in_dim.22 = bf16[8192,512]{1,0:T(8,128)(2,1)} broadcast(bf16[]{:T(256)} %constant.50.clone.1), dimensions={} | broadcast | bytes 8388610 | tf_op jit(solution)/shard_map/broadcast_in_dim | solution.py:78
  25.5 2.2 constant_dynamic-update-slice_fusion.1
  27.7 0.7 collective-permute-done.1
  28.4 4.4 %constant_dynamic-update-slice_fusion.panel_ref = bf16[8192,512]{1,0:T(8,128)(2,1)} fusion(bf16[8192,512]{1,0:T(8,128)(2,1)} %constant_dynamic-update-slice_fusion.1, bf16[4096,512]{1,0:T(8,128)(2,1)} %collective-permute-done.1, s32[]{:T(128)S(6)} %select_n.12), kind=kLoop, calls=%fused_computation.10 | loop fusion | bytes 8388612 | tf_op jit(solution)/shard_map/dynamic_update_slice | solution.py:80
  32.8 132.3 %all-gather.2.cloned.1.call-done.vals_ref = bf16[64,1040,128]{2,1,0:T(8,128)(2,1)} async-done(((bf16[2,1040,128]{2,1,0:T(8,128)(2,1)}), bf16[64,1040,128]{2,1,0:T(8,128)(2,1)}) %all-gather.2.cloned.1.call-update) | async-done | bytes 17039376 | tf_op jit(solution)/shard_map/all_gather | solution.py:67
  165.2 0.9 slice_convert_fusion
  166.1 0.1 copy.6
  166.2 0.2 select_reduce_fusion.slot_of_ref
  166.4 13.5 %shard_map.38 = f32[256,512]{1,0:T(8,128)S(1)} custom-call(s32[1]{0:T(128)} %bitcast.6.first_ref, s32[8,64]{1,0:T(8,128)S(1)} %select_reduce_fusion.slot_of_ref, bf16[64,1040,128]{2,1,0:T(8,128)(2,1)} %all-gather.2.cloned.1.call-done.vals_ref, bf16[8192,512]{1,0:T(8,128)(2,1)} %constant_dynamic-update-slice_fusion.panel_ref), custom_call_target="tpu_custom_call" | custom-call | flops 2147483648 | bytes 13107200 | tf_op jit(solution)/shard_map/pallas_call | solution.py:36
  179.9 1.3 collective-permute-start.2
  181.2 13.5 %shard_map.39 = f32[256,512]{1,0:T(8,128)S(1)} custom-call(s32[1]{0:T(128)S(6)} %add.26.first_ref, s32[8,64]{1,0:T(8,128)S(1)} %select_reduce_fusion.slot_of_ref, bf16[64,1040,128]{2,1,0:T(8,128)(2,1)} %all-gather.2.cloned.1.call-done.vals_ref, bf16[8192,512]{1,0:T(8,128)(2,1)} %constant_dynamic-update-slice_fusion.panel_ref), custom_call_target="tpu_custom_call" | custom-call | flops 2147483648 | bytes 13107200 | tf_op jit(solution)/shard_map/pallas_call | solution.py:36
  194.7 0.4 collective-permute-start.3
  195.1 16.0 %shard_map.37 = f32[512,512]{1,0:T(8,128)S(1)} custom-call(s32[1]{0:T(128)} %bitcast.first_ref, s32[8,64]{1,0:T(8,128)S(1)} %select_reduce_fusion.slot_of_ref, bf16[64,1040,128]{2,1,0:T(8,128)(2,1)} %all-gather.2.cloned.1.call-done.vals_ref, bf16[8192,512]{1,0:T(8,128)(2,1)} %constant_dynamic-update-slice_fusion.panel_ref), custom_call_target="tpu_custom_call" | custom-call | flops 4294967296 | bytes 17825792 | tf_op jit(solution)/shard_map/pallas_call | solution.py:36
  211.1 0.0 collective-permute-done.2
  211.1 0.3 fusion.1
  211.4 8.9 %psum.7 = f32[512]{0:T(512)S(1)} all-reduce(f32[512]{0:T(512)S(1)} %fusion.1), channel_id=1, replica_groups=mesh['row'=2,'col_z'=8,'col_y'=4,'col_x'=2,'layer'=2] {'row','layer'}, use_global_device_ids=true, to_apply=%region_2.3 | all-reduce | flops 512 | bytes 4096 | tf_op jit(solution)/shard_map/psum | solution.py:108
  220.4 1.2 broadcast_divide_fusion
  (6 shorter events, 0.0 us)
Async XLA Ops:
  6.5 158.7 %all-gather.2.cloned.1.call-start = ((), (), s32[]{:S(2)}) async-start(), calls=%async_computation | async-start | bytes 17571840 | tf_op jit(solution)/shard_map/all_gather | solution.py:67
  8.2 8.7 %collective-permute-start = (bf16[1,1040,128]{2,1,0:T(8,128)(2,1)S(1)}, bf16[1,1040,128]{2,1,0:T(8,128)(2,1)S(1)}, u32[]{:S(2)}, u32[]{:S(2)}) collective-permute-start(bf16[1,1040,128]{2,1,0:T(8,128)(2,1)S(1)} %pad_maximum_fusion.1), channel_id=1, source_target_pairs={{0,2},{2,0},{1,3},{3,1},{4,6},{6,4},{5,7},{7,5},{8,10},{10,8},{9,1... | collective-permute-start | bytes 798728 | tf_op jit(solution)/shard_map/ppermute | solution.py:65
  18.7 9.7 %collective-permute-start.1 = (bf16[4096,512]{1,0:T(8,128)(2,1)}, bf16[4096,512]{1,0:T(8,128)(2,1)}, u32[]{:S(2)}, u32[]{:S(2)}) collective-permute-start(bf16[4096,512]{1,0:T(8,128)(2,1)} %bitcast.10), channel_id=1, source_target_pairs={{0,128},{128,0},{1,129},{129,1},{2,130},{130,2},{3,131},{131,3},{4... | collective-permute-start | bytes 12582920 | tf_op jit(solution)/shard_map/ppermute | solution.py:77
  21.3 4.2 %copy-start = (bf16[1,4096,512]{2,1,0:T(8,128)(2,1)S(1)}, bf16[1,4096,512]{2,1,0:T(8,128)(2,1)}, u32[]{:S(2)}) copy-start(bf16[1,4096,512]{2,1,0:T(8,128)(2,1)} %param.7) | copy-start | bytes 12582916
  179.9 31.2 %collective-permute-start.2 = (f32[256,512]{1,0:T(8,128)S(1)}, f32[256,512]{1,0:T(8,128)S(1)}, u32[]{:S(2)}, u32[]{:S(2)}) collective-permute-start(f32[256,512]{1,0:T(8,128)S(1)} %shard_map.38), channel_id=1, source_target_pairs={{0,1},{1,0},{2,3},{3,2},{4,5},{5,4},{6,7},{7,6},{8,9},{9,8},{10,11... | collective-permute-start | bytes 1572872 | tf_op jit(solution)/shard_map/ppermute | solution.py:104
  194.7 16.4 %collective-permute-start.3 = (f32[256,512]{1,0:T(8,128)S(1)}, f32[256,512]{1,0:T(8,128)S(1)}, u32[]{:S(2)}, u32[]{:S(2)}) collective-permute-start(f32[256,512]{1,0:T(8,128)S(1)} %shard_map.39), channel_id=1, source_target_pairs={{0,1},{1,0},{2,3},{3,2},{4,5},{5,4},{6,7},{7,6},{8,9},{9,8},{10,11... | collective-permute-start | bytes 1572872 | tf_op jit(solution)/shard_map/ppermute | solution.py:104
Sparse Core Ops, SparseCore 0:
  18.8 146.3 all-gather.1

commit v7 on v5

--- a/solution.py
+++ b/solution.py
@@ -29,7 +29,7 @@
     out_ref[...] += jnp.dot(stage_ref[...], panel_ref[...], preferred_element_type=jnp.float32)
 
 
-def dense_rows(first, slot_of, gathered, panel, share, width=4):
+def dense_rows(first, slot_of, gathered, panel, share, width=8):
     slot_count = gathered.shape[0]
     block_size = gathered.shape[-1]
     out_cols = panel.shape[1]

time: 223 us -> 219 us (0.982)
  Pallas kernels: 32.1 us -> 24.1 us
  waiting for transfers between devices: 139 us -> 143 us
    pallas_call x2, Pallas kernels: 32.1 us -> 24.1 us  [dense_rows(): pl.pallas_call(dense_rows_kernel, out_shape=jax.ShapeDtypeStruct((share *...]
    ppermute x1, waiting for transfers between devices: 6.37 us -> 10.4 us  [body(): received = lax.ppermute(sent, 'layer', perm=[(0, 1), (1, 0)])]
  transfers between devices with their start and end apart: 3 -> 3, of which waited for: 3 -> 3; matrix products, arithmetic and copies ran while one was open for 5% -> 5% of each run, Pallas kernels for 7% -> 6%
where the time goes in v7:
time: 219 us
  waiting for transfers between devices  143 us (65%)
  Pallas kernels  24.1 us (11%)
  blocking collectives  18.6 us (8%)
  between operations  13.4 us (6%)
  local copies, waits for them, and re-layouts  10.9 us (5%)
  other arithmetic  4.23 us (2%)
  starting transfers between devices  3.99 us (2%)
    all_gather x1, waiting for transfers between devices, gather_slots(): return lax.all_gather(packed, COL_PARTS[:2], axis=0, tiled=True)  132 us
    pallas_call x2, Pallas kernels, dense_rows(): pl.pallas_call(dense_rows_kernel, out_shape=jax.ShapeDtypeStruct((share *...  24.1 us
    ppermute x1, waiting for transfers between devices, body(): received = lax.ppermute(sent, 'layer', perm=[(0, 1), (1, 0)])  10.4 us
    all_gather x1, blocking collectives, gather_slots(): packed = lax.all_gather(packed, COL_PARTS[2], axis=0, tiled=True)  9.31 us
    psum x1, blocking collectives, body(): column_sums = lax.psum(jnp.sum(squares, axis=0), ('row', 'layer'))  9.29 us
    dynamic_update_slice x1, local copies, waits for them, and re-layouts, body(): lax.dynamic_update_slice_in_dim(panel, other_g, (1 - row) * half_rows, 0)  4.4 us
  transfers between devices with their start and end apart: 3, of which 3 were waited for; matrix products, arithmetic and copies ran while one was open for 5% of the time, Pallas kernels for 6%

profile of v7, /device:TPU:1, one launch (start us, length us, event | category | flops | bytes accessed | tf_op | source)
XLA Modules:
  0.0 218.7 jit_solution(5153868287312846269)
XLA Ops:
  6.5 0.0 all-gather.2.cloned.1.call-start
  6.5 0.7 convert_bitcast_fusion
  7.2 1.0 fusion.2
  8.2 9.3 %all_gather.6 = bf16[2,1040,128]{2,1,0:T(8,128)(2,1)} all-gather(bf16[1,1040,128]{2,1,0:T(8,128)(2,1)S(1)} %fusion.2), channel_id=1, replica_groups=mesh['row'=2,'col_z'=8,'col_y'=4,'col_x'=2,'layer'=2] {'col_x'}, dimensions={0}, use_global_device_ids=true | all-gather | bytes 798720 | tf_op jit(solution)/shard_map/all_gather | solution.py:65
  17.5 0.0 all-gather.2.cloned.1.call-update
  17.5 2.7 %collective-permute-start = (bf16[4096,512]{1,0:T(8,128)(2,1)}, bf16[4096,512]{1,0:T(8,128)(2,1)}, u32[]{:S(2)}, u32[]{:S(2)}) collective-permute-start(bf16[4096,512]{1,0:T(8,128)(2,1)} %bitcast.10), channel_id=1, source_target_pairs={{0,128},{128,0},{1,129},{129,1},{2,130},{130,2},{3,131},{131,3},{4... | collective-permute-start | bytes 12582920 | tf_op jit(solution)/shard_map/ppermute | solution.py:76
  20.2 0.0 copy-start
  20.2 4.2 %broadcast_in_dim.22 = bf16[8192,512]{1,0:T(8,128)(2,1)} broadcast(bf16[]{:T(256)} %constant.49.clone.1), dimensions={} | broadcast | bytes 8388610 | tf_op jit(solution)/shard_map/broadcast_in_dim | solution.py:77
  24.4 0.0 copy-done
  24.4 2.2 %constant_dynamic-update-slice_fusion.1 = bf16[8192,512]{1,0:T(8,128)(2,1)} fusion(bf16[8192,512]{1,0:T(8,128)(2,1)} %broadcast_in_dim.22, s32[]{:T(128)S(6)} %select_n.11, bf16[1,4096,512]{2,1,0:T(8,128)(2,1)S(1)} %copy-done), kind=kLoop, calls=%fused_computation.11 | loop fusion | bytes 8388612 | tf_op jit(solution)/shard_map/dynamic_update_slice | solution.py:78
  26.6 0.7 collective-permute-done
  27.4 4.4 %constant_dynamic-update-slice_fusion.panel_ref = bf16[8192,512]{1,0:T(8,128)(2,1)} fusion(bf16[8192,512]{1,0:T(8,128)(2,1)} %constant_dynamic-update-slice_fusion.1, bf16[4096,512]{1,0:T(8,128)(2,1)} %collective-permute-done, s32[]{:T(128)S(6)} %select_n.12), kind=kLoop, calls=%fused_computation.10 | loop fusion | bytes 8388612 | tf_op jit(solution)/shard_map/dynamic_update_slice | solution.py:79
  31.8 132.3 %all-gather.2.cloned.1.call-done.vals_ref = bf16[64,1040,128]{2,1,0:T(8,128)(2,1)} async-done(((bf16[2,1040,128]{2,1,0:T(8,128)(2,1)}), bf16[64,1040,128]{2,1,0:T(8,128)(2,1)}) %all-gather.2.cloned.1.call-update) | async-done | bytes 17039376 | tf_op jit(solution)/shard_map/all_gather | solution.py:66
  164.1 0.9 slice_convert_fusion
  165.0 0.1 copy.6
  165.1 0.2 select_reduce_fusion.slot_of_ref
  165.3 12.0 %shard_map.38 = f32[512,512]{1,0:T(8,128)S(1)} custom-call(s32[1]{0:T(128)} %bitcast.6.first_ref, s32[8,64]{1,0:T(8,128)S(1)} %select_reduce_fusion.slot_of_ref, bf16[64,1040,128]{2,1,0:T(8,128)(2,1)} %all-gather.2.cloned.1.call-done.vals_ref, bf16[8192,512]{1,0:T(8,128)(2,1)} %constant_dynamic-update-slice_fusion.panel_ref), custom_call_target="tpu_custom_call" | custom-call | flops 4294967296 | bytes 17825792 | tf_op jit(solution)/shard_map/pallas_call | solution.py:36
  177.3 1.3 collective-permute-start.1
  178.6 12.0 %shard_map.37 = f32[512,512]{1,0:T(8,128)S(1)} custom-call(s32[1]{0:T(128)} %bitcast.first_ref, s32[8,64]{1,0:T(8,128)S(1)} %select_reduce_fusion.slot_of_ref, bf16[64,1040,128]{2,1,0:T(8,128)(2,1)} %all-gather.2.cloned.1.call-done.vals_ref, bf16[8192,512]{1,0:T(8,128)(2,1)} %constant_dynamic-update-slice_fusion.panel_ref), custom_call_target="tpu_custom_call" | custom-call | flops 4294967296 | bytes 17825792 | tf_op jit(solution)/shard_map/pallas_call | solution.py:36
  190.6 10.4 %collective-permute-done.1 = f32[512,512]{1,0:T(8,128)S(1)} collective-permute-done((f32[512,512]{1,0:T(8,128)S(1)}, f32[512,512]{1,0:T(8,128)S(1)}, u32[]{:S(2)}, u32[]{:S(2)}) %collective-permute-start.1) | collective-permute-done | bytes 1048608 | tf_op jit(solution)/shard_map/ppermute | solution.py:103
  201.0 0.3 fusion.1
  201.3 9.3 %psum.7 = f32[512]{0:T(512)S(1)} all-reduce(f32[512]{0:T(512)S(1)} %fusion.1), channel_id=1, replica_groups=mesh['row'=2,'col_z'=8,'col_y'=4,'col_x'=2,'layer'=2] {'row','layer'}, use_global_device_ids=true, to_apply=%region_2.3 | all-reduce | flops 512 | bytes 4096 | tf_op jit(solution)/shard_map/psum | solution.py:107
  210.6 1.2 broadcast_divide_fusion
  (1 shorter events, 0.0 us)
Async XLA Ops:
  6.5 157.6 %all-gather.2.cloned.1.call-start = ((), (), s32[]{:S(2)}) async-start(), calls=%async_computation | async-start | bytes 17571840 | tf_op jit(solution)/shard_map/all_gather | solution.py:66
  17.5 9.8 %collective-permute-start = (bf16[4096,512]{1,0:T(8,128)(2,1)}, bf16[4096,512]{1,0:T(8,128)(2,1)}, u32[]{:S(2)}, u32[]{:S(2)}) collective-permute-start(bf16[4096,512]{1,0:T(8,128)(2,1)} %bitcast.10), channel_id=1, source_target_pairs={{0,128},{128,0},{1,129},{129,1},{2,130},{130,2},{3,131},{131,3},{4... | collective-permute-start | bytes 12582920 | tf_op jit(solution)/shard_map/ppermute | solution.py:76
  20.2 4.2 %copy-start = (bf16[1,4096,512]{2,1,0:T(8,128)(2,1)S(1)}, bf16[1,4096,512]{2,1,0:T(8,128)(2,1)}, u32[]{:S(2)}) copy-start(bf16[1,4096,512]{2,1,0:T(8,128)(2,1)} %param.7) | copy-start | bytes 12582916
  177.3 23.7 %collective-permute-start.1 = (f32[512,512]{1,0:T(8,128)S(1)}, f32[512,512]{1,0:T(8,128)S(1)}, u32[]{:S(2)}, u32[]{:S(2)}) collective-permute-start(f32[512,512]{1,0:T(8,128)S(1)} %shard_map.38), channel_id=1, source_target_pairs={{0,1},{1,0},{2,3},{3,2},{4,5},{5,4},{6,7},{7,6},{8,9},{9,8},{10,11... | collective-permute-start | bytes 3145736 | tf_op jit(solution)/shard_map/ppermute | solution.py:103
Sparse Core Ops, SparseCore 0:
  17.6 146.4 all-gather.1

commit v8 on v7

--- a/solution.py
+++ b/solution.py
@@ -29,10 +29,10 @@
     out_ref[...] += jnp.dot(stage_ref[...], panel_ref[...], preferred_element_type=jnp.float32)
 
 
-def dense_rows(first, slot_of, gathered, panel, share, width=8):
+def dense_rows(first, slot_of, gathered, panel, share, width=8, col_parts=1, col_part=0):
     slot_count = gathered.shape[0]
     block_size = gathered.shape[-1]
-    out_cols = panel.shape[1]
+    out_cols = panel.shape[1] // col_parts
     return pl.pallas_call(
         dense_rows_kernel,
         out_shape=jax.ShapeDtypeStruct((share * block_size, out_cols), jnp.float32),
@@ -42,7 +42,7 @@
             in_specs=[
                 pl.BlockSpec((slot_count, share * block_size, block_size),
                              lambda j, f, t: (0, f[0] // share, 0), pipeline_mode=pl.Buffered(1)),
-                pl.BlockSpec((width * block_size, out_cols), lambda j, f, t: (j, 0)),
+                pl.BlockSpec((width * block_size, out_cols), lambda j, f, t: (j, col_part)),
             ],
             out_specs=pl.BlockSpec((share * block_size, out_cols), lambda j, f, t: (0, 0)),
             scratch_shapes=[pltpu.VMEM((share * block_size, width * block_size), jnp.bfloat16)],
@@ -51,7 +51,7 @@
         cost_estimate=pl.CostEstimate(
             flops=2 * share * block_size * panel.shape[0] * out_cols,
             transcendentals=0,
-            bytes_accessed=slot_count * share * block_size * block_size * 2 + panel.size * 2 + share * block_size * out_cols * 4,
+            bytes_accessed=slot_count * share * block_size * block_size * 2 + panel.size * 2 // col_parts + share * block_size * out_cols * 4,
         ),
     )(first, slot_of, gathered, panel)
 
@@ -99,9 +99,11 @@
     def expand(first):
         return dense_rows(first, slot_of, gathered, panel, share)
 
-    sent = expand(send_first)
-    received = lax.ppermute(sent, "layer", perm=[(0, 1), (1, 0)])
-    summed = expand(keep_first) + received
+    received = []
+    for part in range(2):
+        sent = dense_rows(send_first, slot_of, gathered, panel, share, col_parts=2, col_part=part)
+        received.append(lax.ppermute(sent, "layer", perm=[(0, 1), (1, 0)]))
+    summed = expand(keep_first) + jnp.concatenate(received, axis=1)
     squares = summed * summed
     total_rows = row_blocks * block_size * lax.axis_size("row")
     column_sums = lax.psum(jnp.sum(squares, axis=0), ("row", "layer"))

time: 219 us -> 217 us (level)
  waiting for transfers between devices: 143 us -> 133 us
  Pallas kernels: 24.1 us -> 32.3 us
    ppermute x1 -> x2, waiting for transfers between devices: 10.4 us -> 0.01 us  [body(): received.append(lax.ppermute(sent, 'layer', perm=[(0, 1), (1, 0)]))]
    pallas_call x2 -> x3, Pallas kernels: 24.1 us -> 32.3 us  [dense_rows(): pl.pallas_call(dense_rows_kernel, out_shape=jax.ShapeDtypeStruct((share *...]
  transfers between devices with their start and end apart: 3 -> 4, of which waited for: 3 -> 2; matrix products, arithmetic and copies ran while one was open for 5% -> 5% of each run, Pallas kernels for 6% -> 10%
where the time goes in v8:
time: 217 us
  waiting for transfers between devices  133 us (61%)
  Pallas kernels  32.3 us (15%)
  blocking collectives  18.4 us (8%)
  between operations  13.5 us (6%)
  local copies, waits for them, and re-layouts  10.9 us (5%)
  starting transfers between devices  4.36 us (2%)
  other arithmetic  4.13 us (2%)
    all_gather x1, waiting for transfers between devices, gather_slots(): return lax.all_gather(packed, COL_PARTS[:2], axis=0, tiled=True)  132 us
    pallas_call x3, Pallas kernels, dense_rows(): pl.pallas_call(dense_rows_kernel, out_shape=jax.ShapeDtypeStruct((share *...  32.3 us
    all_gather x1, blocking collectives, gather_slots(): packed = lax.all_gather(packed, COL_PARTS[2], axis=0, tiled=True)  9.31 us
    psum x1, blocking collectives, body(): column_sums = lax.psum(jnp.sum(squares, axis=0), ('row', 'layer'))  9.14 us
    dynamic_update_slice x1, local copies, waits for them, and re-layouts, body(): lax.dynamic_update_slice_in_dim(panel, other_g, (1 - row) * half_rows, 0)  4.4 us
  transfers between devices with their start and end apart: 4, of which 2 were waited for; matrix products, arithmetic and copies ran while one was open for 5% of the time, Pallas kernels for 10%

profile of v8, /device:TPU:1, one launch (start us, length us, event | category | flops | bytes accessed | tf_op | source)
XLA Modules:
  0.0 216.6 jit_solution(3230198029696630951)
XLA Ops:
  6.5 0.0 all-gather.2.cloned.1.call-start
  6.5 0.7 convert_bitcast_fusion
  7.2 1.0 fusion.2
  8.2 9.3 %all_gather.6 = bf16[2,1040,128]{2,1,0:T(8,128)(2,1)} all-gather(bf16[1,1040,128]{2,1,0:T(8,128)(2,1)S(1)} %fusion.2), channel_id=1, replica_groups=mesh['row'=2,'col_z'=8,'col_y'=4,'col_x'=2,'layer'=2] {'col_x'}, dimensions={0}, use_global_device_ids=true | all-gather | bytes 798720 | tf_op jit(solution)/shard_map/all_gather | solution.py:65
  17.5 0.0 all-gather.2.cloned.1.call-update
  17.5 2.7 %collective-permute-start = (bf16[4096,512]{1,0:T(8,128)(2,1)}, bf16[4096,512]{1,0:T(8,128)(2,1)}, u32[]{:S(2)}, u32[]{:S(2)}) collective-permute-start(bf16[4096,512]{1,0:T(8,128)(2,1)} %bitcast.10), channel_id=1, source_target_pairs={{0,128},{128,0},{1,129},{129,1},{2,130},{130,2},{3,131},{131,3},{4... | collective-permute-start | bytes 12582920 | tf_op jit(solution)/shard_map/ppermute | solution.py:76
  20.2 4.2 %broadcast_in_dim.22 = bf16[8192,512]{1,0:T(8,128)(2,1)} broadcast(bf16[]{:T(256)} %constant.49.clone.1), dimensions={} | broadcast | bytes 8388610 | tf_op jit(solution)/shard_map/broadcast_in_dim | solution.py:77
  24.4 2.2 %constant_dynamic-update-slice_fusion.1 = bf16[8192,512]{1,0:T(8,128)(2,1)} fusion(bf16[8192,512]{1,0:T(8,128)(2,1)} %broadcast_in_dim.22, s32[]{:T(128)S(6)} %select_n.11, bf16[1,4096,512]{2,1,0:T(8,128)(2,1)S(1)} %copy-done), kind=kLoop, calls=%fused_computation.12 | loop fusion | bytes 8388612 | tf_op jit(solution)/shard_map/dynamic_update_slice | solution.py:78
  26.6 0.7 collective-permute-done
  27.4 4.4 %constant_dynamic-update-slice_fusion.panel_ref = bf16[8192,512]{1,0:T(8,128)(2,1)} fusion(bf16[8192,512]{1,0:T(8,128)(2,1)} %constant_dynamic-update-slice_fusion.1, bf16[4096,512]{1,0:T(8,128)(2,1)} %collective-permute-done, s32[]{:T(128)S(6)} %select_n.12), kind=kLoop, calls=%fused_computation.11 | loop fusion | bytes 8388612 | tf_op jit(solution)/shard_map/dynamic_update_slice | solution.py:79
  31.8 132.3 %all-gather.2.cloned.1.call-done.vals_ref = bf16[64,1040,128]{2,1,0:T(8,128)(2,1)} async-done(((bf16[2,1040,128]{2,1,0:T(8,128)(2,1)}), bf16[64,1040,128]{2,1,0:T(8,128)(2,1)}) %all-gather.2.cloned.1.call-update) | async-done | bytes 17039376 | tf_op jit(solution)/shard_map/all_gather | solution.py:66
  164.1 0.9 slice_convert_fusion
  165.0 0.1 copy.6
  165.1 0.2 select_reduce_fusion.slot_of_ref
  165.3 10.1 %shard_map.38 = f32[512,256]{1,0:T(8,128)S(1)} custom-call(s32[1]{0:T(128)} %bitcast.6.first_ref, s32[8,64]{1,0:T(8,128)S(1)} %select_reduce_fusion.slot_of_ref, bf16[64,1040,128]{2,1,0:T(8,128)(2,1)} %all-gather.2.cloned.1.call-done.vals_ref, bf16[8192,512]{1,0:T(8,128)(2,1)} %constant_dynamic-update-slice_fusion.panel_ref), custom_call_target="tpu_custom_call" | custom-call | flops 2147483648 | bytes 13107200 | tf_op jit(solution)/shard_map/pallas_call | solution.py:36
  175.4 1.3 collective-permute-start.1
  176.7 10.1 %shard_map.39 = f32[512,256]{1,0:T(8,128)S(1)} custom-call(s32[1]{0:T(128)} %bitcast.6.first_ref, s32[8,64]{1,0:T(8,128)S(1)} %select_reduce_fusion.slot_of_ref, bf16[64,1040,128]{2,1,0:T(8,128)(2,1)} %all-gather.2.cloned.1.call-done.vals_ref, bf16[8192,512]{1,0:T(8,128)(2,1)} %constant_dynamic-update-slice_fusion.panel_ref), custom_call_target="tpu_custom_call" | custom-call | flops 2147483648 | bytes 13107200 | tf_op jit(solution)/shard_map/pallas_call | solution.py:36
  186.8 0.4 collective-permute-start.2
  187.2 12.0 %shard_map.37 = f32[512,512]{1,0:T(8,128)S(1)} custom-call(s32[1]{0:T(128)} %bitcast.first_ref, s32[8,64]{1,0:T(8,128)S(1)} %select_reduce_fusion.slot_of_ref, bf16[64,1040,128]{2,1,0:T(8,128)(2,1)} %all-gather.2.cloned.1.call-done.vals_ref, bf16[8192,512]{1,0:T(8,128)(2,1)} %constant_dynamic-update-slice_fusion.panel_ref), custom_call_target="tpu_custom_call" | custom-call | flops 4294967296 | bytes 17825792 | tf_op jit(solution)/shard_map/pallas_call | solution.py:36
  199.2 0.0 collective-permute-done.1
  199.2 0.0 collective-permute-done.2
  199.3 0.2 fusion.3
  199.5 9.1 %psum.7 = f32[512]{0:T(512)S(1)} all-reduce(f32[512]{0:T(512)S(1)} %fusion.3), channel_id=1, replica_groups=mesh['row'=2,'col_z'=8,'col_y'=4,'col_x'=2,'layer'=2] {'row','layer'}, use_global_device_ids=true, to_apply=%region_2.3 | all-reduce | flops 512 | bytes 4096 | tf_op jit(solution)/shard_map/psum | solution.py:109
  208.6 1.2 broadcast_divide_fusion
  (3 shorter events, 0.0 us)
Async XLA Ops:
  6.5 157.6 %all-gather.2.cloned.1.call-start = ((), (), s32[]{:S(2)}) async-start(), calls=%async_computation | async-start | bytes 17571840 | tf_op jit(solution)/shard_map/all_gather | solution.py:66
  17.5 9.8 %collective-permute-start = (bf16[4096,512]{1,0:T(8,128)(2,1)}, bf16[4096,512]{1,0:T(8,128)(2,1)}, u32[]{:S(2)}, u32[]{:S(2)}) collective-permute-start(bf16[4096,512]{1,0:T(8,128)(2,1)} %bitcast.10), channel_id=1, source_target_pairs={{0,128},{128,0},{1,129},{129,1},{2,130},{130,2},{3,131},{131,3},{4... | collective-permute-start | bytes 12582920 | tf_op jit(solution)/shard_map/ppermute | solution.py:76
  20.2 4.2 %copy-start = (bf16[1,4096,512]{2,1,0:T(8,128)(2,1)S(1)}, bf16[1,4096,512]{2,1,0:T(8,128)(2,1)}, u32[]{:S(2)}) copy-start(bf16[1,4096,512]{2,1,0:T(8,128)(2,1)} %param.7) | copy-start | bytes 12582916
  175.4 23.8 %collective-permute-start.1 = (f32[512,256]{1,0:T(8,128)S(1)}, f32[512,256]{1,0:T(8,128)S(1)}, u32[]{:S(2)}, u32[]{:S(2)}) collective-permute-start(f32[512,256]{1,0:T(8,128)S(1)} %shard_map.38), channel_id=1, source_target_pairs={{0,1},{1,0},{2,3},{3,2},{4,5},{5,4},{6,7},{7,6},{8,9},{9,8},{10,11... | collective-permute-start | bytes 1572872 | tf_op jit(solution)/shard_map/ppermute | solution.py:105
  186.8 12.4 %collective-permute-start.2 = (f32[512,256]{1,0:T(8,128)S(1)}, f32[512,256]{1,0:T(8,128)S(1)}, u32[]{:S(2)}, u32[]{:S(2)}) collective-permute-start(f32[512,256]{1,0:T(8,128)S(1)} %shard_map.39), channel_id=1, source_target_pairs={{0,1},{1,0},{2,3},{3,2},{4,5},{5,4},{6,7},{7,6},{8,9},{9,8},{10,11... | collective-permute-start | bytes 1572872 | tf_op jit(solution)/shard_map/ppermute | solution.py:105
Sparse Core Ops, SparseCore 0:
  17.6 146.4 all-gather.1

commit v9 on v8

--- a/solution.py
+++ b/solution.py
@@ -6,52 +6,82 @@
 from jax.sharding import Mesh, PartitionSpec as P
 
 
-def dense_rows_kernel(first_ref, slot_of_ref, vals_ref, panel_ref, out_ref, stage_ref):
-    block_size = vals_ref.shape[-1]
-    share = vals_ref.shape[1] // block_size
-    width = stage_ref.shape[1] // block_size
+def dense_rows_kernel(first_ref, slot_of_ref, vals_hbm, panel_ref, out_ref, stage_ref, sems):
+    share = stage_ref.shape[1] // vals_hbm.shape[-1]
+    block_size = vals_hbm.shape[-1]
+    width = stage_ref.shape[2] // block_size
+    chunks = pl.num_programs(0)
     j = pl.program_id(0)
+    buf = j % 2
     first = first_ref[0]
+
+    def copy(chunk, slot_buf, i, kk, slot):
+        return pltpu.make_async_copy(
+            vals_hbm.at[slot, pl.ds((first + i) * block_size, block_size), :],
+            stage_ref.at[slot_buf, pl.ds(i * block_size, block_size), pl.ds(kk * block_size, block_size)],
+            sems.at[slot_buf, i, kk],
+        )
+
+    def fetch(chunk, slot_buf):
+        for i in range(share):
+            for kk in range(width):
+                slot = slot_of_ref[first + i, chunk * width + kk]
+
+                @pl.when(slot >= 0)
+                def _():
+                    copy(chunk, slot_buf, i, kk, slot).start()
 
     @pl.when(j == 0)
     def _():
         out_ref[...] = jnp.zeros_like(out_ref)
+        fetch(0, 0)
+
+    @pl.when(j + 1 < chunks)
+    def _():
+        fetch(j + 1, 1 - buf)
 
     for i in range(share):
         for kk in range(width):
             slot = slot_of_ref[first + i, j * width + kk]
-            rows = pl.ds(i * block_size, block_size)
-            block = vals_ref[jnp.maximum(slot, 0), rows, :]
-            stage_ref[rows, pl.ds(kk * block_size, block_size)] = jnp.where(
-                slot >= 0, block, jnp.zeros_like(block)
-            )
 
-    out_ref[...] += jnp.dot(stage_ref[...], panel_ref[...], preferred_element_type=jnp.float32)
+            @pl.when(slot >= 0)
+            def _():
+                copy(j, buf, i, kk, slot).wait()
+
+            @pl.when(slot < 0)
+            def _():
+                stage_ref[buf, pl.ds(i * block_size, block_size), pl.ds(kk * block_size, block_size)] = (
+                    jnp.zeros((block_size, block_size), stage_ref.dtype)
+                )
+
+    out_ref[...] += jnp.dot(stage_ref[buf], panel_ref[...], preferred_element_type=jnp.float32)
 
 
 def dense_rows(first, slot_of, gathered, panel, share, width=8, col_parts=1, col_part=0):
-    slot_count = gathered.shape[0]
     block_size = gathered.shape[-1]
     out_cols = panel.shape[1] // col_parts
+    depth = width * block_size
     return pl.pallas_call(
         dense_rows_kernel,
         out_shape=jax.ShapeDtypeStruct((share * block_size, out_cols), jnp.float32),
         grid_spec=pltpu.PrefetchScalarGridSpec(
             num_scalar_prefetch=2,
-            grid=(panel.shape[0] // (width * block_size),),
+            grid=(panel.shape[0] // depth,),
             in_specs=[
-                pl.BlockSpec((slot_count, share * block_size, block_size),
-                             lambda j, f, t: (0, f[0] // share, 0), pipeline_mode=pl.Buffered(1)),
-                pl.BlockSpec((width * block_size, out_cols), lambda j, f, t: (j, col_part)),
+                pl.BlockSpec(memory_space=pl.ANY),
+                pl.BlockSpec((depth, out_cols), lambda j, f, t: (j, col_part)),
             ],
             out_specs=pl.BlockSpec((share * block_size, out_cols), lambda j, f, t: (0, 0)),
-            scratch_shapes=[pltpu.VMEM((share * block_size, width * block_size), jnp.bfloat16)],
+            scratch_shapes=[
+                pltpu.VMEM((2, share * block_size, depth), jnp.bfloat16),
+                pltpu.SemaphoreType.DMA((2, share, width)),
+            ],
         ),
         compiler_params=pltpu.CompilerParams(vmem_limit_bytes=48 * 1024 * 1024),
         cost_estimate=pl.CostEstimate(
             flops=2 * share * block_size * panel.shape[0] * out_cols,
             transcendentals=0,
-            bytes_accessed=slot_count * share * block_size * block_size * 2 + panel.size * 2 // col_parts + share * block_size * out_cols * 4,
+            bytes_accessed=share * block_size * panel.shape[0] * 2 + panel.size * 2 // col_parts + share * block_size * out_cols * 4,
         ),
     )(first, slot_of, gathered, panel)
 

time: 217 us -> 220 us (1.014)
  Pallas kernels: 32.3 us -> 35.4 us
    pallas_call x3, Pallas kernels: 32.3 us -> 35.4 us  [dense_rows(): pl.pallas_call(dense_rows_kernel, out_shape=jax.ShapeDtypeStruct((share *...]
  transfers between devices with their start and end apart: 4 -> 4, of which waited for: 2 -> 2; matrix products, arithmetic and copies ran while one was open for 5% -> 5% of each run, Pallas kernels for 10% -> 11%
where the time goes in v9:
time: 220 us; the launch traced here: 219 us
  waiting for transfers between devices  133 us (60%)
  Pallas kernels  35.4 us (16%)
  blocking collectives  17.6 us (8%)
  between operations  13.5 us (6%)
  local copies, waits for them, and re-layouts  10.9 us (5%)
  starting transfers between devices  4.48 us (2%)
  other arithmetic  4.13 us (2%)
    all_gather x1, waiting for transfers between devices, gather_slots(): return lax.all_gather(packed, COL_PARTS[:2], axis=0, tiled=True)  132 us
    pallas_call x3, Pallas kernels, dense_rows(): pl.pallas_call(dense_rows_kernel, out_shape=jax.ShapeDtypeStruct((share *...  35.4 us
    all_gather x1, blocking collectives, gather_slots(): packed = lax.all_gather(packed, COL_PARTS[2], axis=0, tiled=True)  9.31 us
    psum x1, blocking collectives, body(): column_sums = lax.psum(jnp.sum(squares, axis=0), ('row', 'layer'))  8.25 us
    dynamic_update_slice x1, local copies, waits for them, and re-layouts, body(): lax.dynamic_update_slice_in_dim(panel, other_g, (1 - row) * half_rows, 0)  4.4 us
  transfers between devices with their start and end apart: 4, of which 2 were waited for; matrix products, arithmetic and copies ran while one was open for 5% of the time, Pallas kernels for 11%

profile of v9, /device:TPU:1, one launch (start us, length us, event | category | flops | bytes accessed | tf_op | source)
XLA Modules:
  0.0 219.0 jit_solution(13023257690041050098)
XLA Ops:
  6.5 0.0 all-gather.2.cloned.1.call-start
  6.5 0.7 convert_bitcast_fusion
  7.2 1.0 fusion.2
  8.2 9.3 %all_gather.6 = bf16[2,1040,128]{2,1,0:T(8,128)(2,1)} all-gather(bf16[1,1040,128]{2,1,0:T(8,128)(2,1)S(1)} %fusion.2), channel_id=1, replica_groups=mesh['row'=2,'col_z'=8,'col_y'=4,'col_x'=2,'layer'=2] {'col_x'}, dimensions={0}, use_global_device_ids=true | all-gather | bytes 798720 | tf_op jit(solution)/shard_map/all_gather | solution.py:95
  17.5 0.0 all-gather.2.cloned.1.call-update
  17.5 2.7 %collective-permute-start = (bf16[4096,512]{1,0:T(8,128)(2,1)}, bf16[4096,512]{1,0:T(8,128)(2,1)}, u32[]{:S(2)}, u32[]{:S(2)}) collective-permute-start(bf16[4096,512]{1,0:T(8,128)(2,1)} %bitcast.10), channel_id=1, source_target_pairs={{0,128},{128,0},{1,129},{129,1},{2,130},{130,2},{3,131},{131,3},{4... | collective-permute-start | bytes 12582920 | tf_op jit(solution)/shard_map/ppermute | solution.py:106
  20.2 4.2 %broadcast_in_dim.22 = bf16[8192,512]{1,0:T(8,128)(2,1)} broadcast(bf16[]{:T(256)} %constant.49.clone.1), dimensions={} | broadcast | bytes 8388610 | tf_op jit(solution)/shard_map/broadcast_in_dim | solution.py:107
  24.4 2.2 %constant_dynamic-update-slice_fusion.1 = bf16[8192,512]{1,0:T(8,128)(2,1)} fusion(bf16[8192,512]{1,0:T(8,128)(2,1)} %broadcast_in_dim.22, s32[]{:T(128)S(6)} %select_n.11, bf16[1,4096,512]{2,1,0:T(8,128)(2,1)S(1)} %copy-done), kind=kLoop, calls=%fused_computation.12 | loop fusion | bytes 8388612 | tf_op jit(solution)/shard_map/dynamic_update_slice | solution.py:108
  26.6 0.7 collective-permute-done
  27.4 4.4 %constant_dynamic-update-slice_fusion.panel_ref = bf16[8192,512]{1,0:T(8,128)(2,1)} fusion(bf16[8192,512]{1,0:T(8,128)(2,1)} %constant_dynamic-update-slice_fusion.1, bf16[4096,512]{1,0:T(8,128)(2,1)} %collective-permute-done, s32[]{:T(128)S(6)} %select_n.12), kind=kLoop, calls=%fused_computation.11 | loop fusion | bytes 8388612 | tf_op jit(solution)/shard_map/dynamic_update_slice | solution.py:109
  31.8 132.3 %all-gather.2.cloned.1.call-done.vals_hbm = bf16[64,1040,128]{2,1,0:T(8,128)(2,1)} async-done(((bf16[2,1040,128]{2,1,0:T(8,128)(2,1)}), bf16[64,1040,128]{2,1,0:T(8,128)(2,1)}) %all-gather.2.cloned.1.call-update) | async-done | bytes 17039376 | tf_op jit(solution)/shard_map/all_gather | solution.py:96
  164.1 0.9 slice_convert_fusion
  165.0 0.1 copy.6
  165.1 0.2 select_reduce_fusion.slot_of_ref
  165.3 11.1 %shard_map.38 = f32[512,256]{1,0:T(8,128)S(1)} custom-call(s32[1]{0:T(128)} %bitcast.6.first_ref, s32[8,64]{1,0:T(8,128)S(1)} %select_reduce_fusion.slot_of_ref, bf16[64,1040,128]{2,1,0:T(8,128)(2,1)} %all-gather.2.cloned.1.call-done.vals_hbm, bf16[8192,512]{1,0:T(8,128)(2,1)} %constant_dynamic-update-slice_fusion.panel_ref), custom_call_target="tpu_custom_call" | custom-call | flops 2147483648 | bytes 13107200 | tf_op jit(solution)/shard_map/pallas_call | solution.py:64
  176.4 1.4 collective-permute-start.1
  177.8 11.1 %shard_map.39 = f32[512,256]{1,0:T(8,128)S(1)} custom-call(s32[1]{0:T(128)} %bitcast.6.first_ref, s32[8,64]{1,0:T(8,128)S(1)} %select_reduce_fusion.slot_of_ref, bf16[64,1040,128]{2,1,0:T(8,128)(2,1)} %all-gather.2.cloned.1.call-done.vals_hbm, bf16[8192,512]{1,0:T(8,128)(2,1)} %constant_dynamic-update-slice_fusion.panel_ref), custom_call_target="tpu_custom_call" | custom-call | flops 2147483648 | bytes 13107200 | tf_op jit(solution)/shard_map/pallas_call | solution.py:64
  188.9 0.4 collective-permute-start.2
  189.3 13.2 %shard_map.37 = f32[512,512]{1,0:T(8,128)S(1)} custom-call(s32[1]{0:T(128)} %bitcast.first_ref, s32[8,64]{1,0:T(8,128)S(1)} %select_reduce_fusion.slot_of_ref, bf16[64,1040,128]{2,1,0:T(8,128)(2,1)} %all-gather.2.cloned.1.call-done.vals_hbm, bf16[8192,512]{1,0:T(8,128)(2,1)} %constant_dynamic-update-slice_fusion.panel_ref), custom_call_target="tpu_custom_call" | custom-call | flops 4294967296 | bytes 17825792 | tf_op jit(solution)/shard_map/pallas_call | solution.py:64
  202.5 0.0 collective-permute-done.1
  202.5 0.0 collective-permute-done.2
  202.5 0.2 fusion.3
  202.8 8.2 %psum.7 = f32[512]{0:T(512)S(1)} all-reduce(f32[512]{0:T(512)S(1)} %fusion.3), channel_id=1, replica_groups=mesh['row'=2,'col_z'=8,'col_y'=4,'col_x'=2,'layer'=2] {'row','layer'}, use_global_device_ids=true, to_apply=%region_2.3 | all-reduce | flops 512 | bytes 4096 | tf_op jit(solution)/shard_map/psum | solution.py:139
  211.0 1.2 broadcast_divide_fusion
  (3 shorter events, 0.0 us)
Async XLA Ops:
  6.5 157.6 %all-gather.2.cloned.1.call-start = ((), (), s32[]{:S(2)}) async-start(), calls=%async_computation | async-start | bytes 17571840 | tf_op jit(solution)/shard_map/all_gather | solution.py:96
  17.5 9.8 %collective-permute-start = (bf16[4096,512]{1,0:T(8,128)(2,1)}, bf16[4096,512]{1,0:T(8,128)(2,1)}, u32[]{:S(2)}, u32[]{:S(2)}) collective-permute-start(bf16[4096,512]{1,0:T(8,128)(2,1)} %bitcast.10), channel_id=1, source_target_pairs={{0,128},{128,0},{1,129},{129,1},{2,130},{130,2},{3,131},{131,3},{4... | collective-permute-start | bytes 12582920 | tf_op jit(solution)/shard_map/ppermute | solution.py:106
  20.2 4.2 %copy-start = (bf16[1,4096,512]{2,1,0:T(8,128)(2,1)S(1)}, bf16[1,4096,512]{2,1,0:T(8,128)(2,1)}, u32[]{:S(2)}) copy-start(bf16[1,4096,512]{2,1,0:T(8,128)(2,1)} %param.7) | copy-start | bytes 12582916
  176.4 26.1 %collective-permute-start.1 = (f32[512,256]{1,0:T(8,128)S(1)}, f32[512,256]{1,0:T(8,128)S(1)}, u32[]{:S(2)}, u32[]{:S(2)}) collective-permute-start(f32[512,256]{1,0:T(8,128)S(1)} %shard_map.38), channel_id=1, source_target_pairs={{0,1},{1,0},{2,3},{3,2},{4,5},{5,4},{6,7},{7,6},{8,9},{9,8},{10,11... | collective-permute-start | bytes 1572872 | tf_op jit(solution)/shard_map/ppermute | solution.py:135
  188.9 13.6 %collective-permute-start.2 = (f32[512,256]{1,0:T(8,128)S(1)}, f32[512,256]{1,0:T(8,128)S(1)}, u32[]{:S(2)}, u32[]{:S(2)}) collective-permute-start(f32[512,256]{1,0:T(8,128)S(1)} %shard_map.39), channel_id=1, source_target_pairs={{0,1},{1,0},{2,3},{3,2},{4,5},{5,4},{6,7},{7,6},{8,9},{9,8},{10,11... | collective-permute-start | bytes 1572872 | tf_op jit(solution)/shard_map/ppermute | solution.py:135
Sparse Core Ops, SparseCore 0:
  17.6 146.4 all-gather.1

commit v10 on v8

--- a/solution.py
+++ b/solution.py
@@ -29,7 +29,7 @@
     out_ref[...] += jnp.dot(stage_ref[...], panel_ref[...], preferred_element_type=jnp.float32)
 
 
-def dense_rows(first, slot_of, gathered, panel, share, width=8, col_parts=1, col_part=0):
+def dense_rows(first, slot_of, gathered, panel, share, width=16, col_parts=1, col_part=0):
     slot_count = gathered.shape[0]
     block_size = gathered.shape[-1]
     out_cols = panel.shape[1] // col_parts

time: 217 us -> 215 us (level)
  Pallas kernels: 32.3 us -> 26.7 us
  waiting for transfers between devices: 133 us -> 137 us
    pallas_call x3, Pallas kernels: 32.3 us -> 26.7 us  [dense_rows(): pl.pallas_call(dense_rows_kernel, out_shape=jax.ShapeDtypeStruct((share *...]
    ppermute x2, waiting for transfers between devices: 0.01 us -> 3.53 us  [body(): received.append(lax.ppermute(sent, 'layer', perm=[(0, 1), (1, 0)]))]
  transfers between devices with their start and end apart: 4 -> 4, of which waited for: 2 -> 3; matrix products, arithmetic and copies ran while one was open for 5% -> 5% of each run, Pallas kernels for 10% -> 9%
where the time goes in v10:
time: 215 us
  waiting for transfers between devices  137 us (64%)
  Pallas kernels  26.7 us (12%)
  blocking collectives  18.6 us (9%)
  between operations  13.4 us (6%)
  local copies, waits for them, and re-layouts  10.9 us (5%)
  starting transfers between devices  4.36 us (2%)
  other arithmetic  4.12 us (2%)
    all_gather x1, waiting for transfers between devices, gather_slots(): return lax.all_gather(packed, COL_PARTS[:2], axis=0, tiled=True)  132 us
    pallas_call x3, Pallas kernels, dense_rows(): pl.pallas_call(dense_rows_kernel, out_shape=jax.ShapeDtypeStruct((share *...  26.7 us
    all_gather x1, blocking collectives, gather_slots(): packed = lax.all_gather(packed, COL_PARTS[2], axis=0, tiled=True)  9.31 us
    psum x1, blocking collectives, body(): column_sums = lax.psum(jnp.sum(squares, axis=0), ('row', 'layer'))  9.29 us
    dynamic_update_slice x1, local copies, waits for them, and re-layouts, body(): lax.dynamic_update_slice_in_dim(panel, other_g, (1 - row) * half_rows, 0)  4.4 us
  transfers between devices with their start and end apart: 4, of which 3 were waited for; matrix products, arithmetic and copies ran while one was open for 5% of the time, Pallas kernels for 9%

profile of v10, /device:TPU:1, one launch (start us, length us, event | category | flops | bytes accessed | tf_op | source)
XLA Modules:
  0.0 214.7 jit_solution(2080446901084722412)
XLA Ops:
  6.5 0.0 all-gather.2.cloned.1.call-start
  6.5 0.7 convert_bitcast_fusion
  7.2 1.0 fusion.2
  8.2 9.3 %all_gather.6 = bf16[2,1040,128]{2,1,0:T(8,128)(2,1)} all-gather(bf16[1,1040,128]{2,1,0:T(8,128)(2,1)S(1)} %fusion.2), channel_id=1, replica_groups=mesh['row'=2,'col_z'=8,'col_y'=4,'col_x'=2,'layer'=2] {'col_x'}, dimensions={0}, use_global_device_ids=true | all-gather | bytes 798720 | tf_op jit(solution)/shard_map/all_gather | solution.py:65
  17.5 0.0 all-gather.2.cloned.1.call-update
  17.5 2.7 %collective-permute-start = (bf16[4096,512]{1,0:T(8,128)(2,1)}, bf16[4096,512]{1,0:T(8,128)(2,1)}, u32[]{:S(2)}, u32[]{:S(2)}) collective-permute-start(bf16[4096,512]{1,0:T(8,128)(2,1)} %bitcast.10), channel_id=1, source_target_pairs={{0,128},{128,0},{1,129},{129,1},{2,130},{130,2},{3,131},{131,3},{4... | collective-permute-start | bytes 12582920 | tf_op jit(solution)/shard_map/ppermute | solution.py:76
  20.2 4.2 %broadcast_in_dim.22 = bf16[8192,512]{1,0:T(8,128)(2,1)} broadcast(bf16[]{:T(256)} %constant.49.clone.1), dimensions={} | broadcast | bytes 8388610 | tf_op jit(solution)/shard_map/broadcast_in_dim | solution.py:77
  24.4 2.2 %constant_dynamic-update-slice_fusion.1 = bf16[8192,512]{1,0:T(8,128)(2,1)} fusion(bf16[8192,512]{1,0:T(8,128)(2,1)} %broadcast_in_dim.22, s32[]{:T(128)S(6)} %select_n.11, bf16[1,4096,512]{2,1,0:T(8,128)(2,1)S(1)} %copy-done), kind=kLoop, calls=%fused_computation.12 | loop fusion | bytes 8388612 | tf_op jit(solution)/shard_map/dynamic_update_slice | solution.py:78
  26.6 0.7 collective-permute-done
  27.4 4.4 %constant_dynamic-update-slice_fusion.panel_ref = bf16[8192,512]{1,0:T(8,128)(2,1)} fusion(bf16[8192,512]{1,0:T(8,128)(2,1)} %constant_dynamic-update-slice_fusion.1, bf16[4096,512]{1,0:T(8,128)(2,1)} %collective-permute-done, s32[]{:T(128)S(6)} %select_n.12), kind=kLoop, calls=%fused_computation.11 | loop fusion | bytes 8388612 | tf_op jit(solution)/shard_map/dynamic_update_slice | solution.py:79
  31.8 132.3 %all-gather.2.cloned.1.call-done.vals_ref = bf16[64,1040,128]{2,1,0:T(8,128)(2,1)} async-done(((bf16[2,1040,128]{2,1,0:T(8,128)(2,1)}), bf16[64,1040,128]{2,1,0:T(8,128)(2,1)}) %all-gather.2.cloned.1.call-update) | async-done | bytes 17039376 | tf_op jit(solution)/shard_map/all_gather | solution.py:66
  164.1 0.9 slice_convert_fusion
  165.0 0.1 copy.6
  165.1 0.2 select_reduce_fusion.slot_of_ref
  165.3 8.2 %shard_map.38 = f32[512,256]{1,0:T(8,128)S(1)} custom-call(s32[1]{0:T(128)} %bitcast.6.first_ref, s32[8,64]{1,0:T(8,128)S(1)} %select_reduce_fusion.slot_of_ref, bf16[64,1040,128]{2,1,0:T(8,128)(2,1)} %all-gather.2.cloned.1.call-done.vals_ref, bf16[8192,512]{1,0:T(8,128)(2,1)} %constant_dynamic-update-slice_fusion.panel_ref), custom_call_target="tpu_custom_call" | custom-call | flops 2147483648 | bytes 13107200 | tf_op jit(solution)/shard_map/pallas_call | solution.py:36
  173.5 1.3 collective-permute-start.1
  174.8 8.2 %shard_map.39 = f32[512,256]{1,0:T(8,128)S(1)} custom-call(s32[1]{0:T(128)} %bitcast.6.first_ref, s32[8,64]{1,0:T(8,128)S(1)} %select_reduce_fusion.slot_of_ref, bf16[64,1040,128]{2,1,0:T(8,128)(2,1)} %all-gather.2.cloned.1.call-done.vals_ref, bf16[8192,512]{1,0:T(8,128)(2,1)} %constant_dynamic-update-slice_fusion.panel_ref), custom_call_target="tpu_custom_call" | custom-call | flops 2147483648 | bytes 13107200 | tf_op jit(solution)/shard_map/pallas_call | solution.py:36
  183.0 0.4 collective-permute-start.2
  183.4 10.3 %shard_map.37 = f32[512,512]{1,0:T(8,128)S(1)} custom-call(s32[1]{0:T(128)} %bitcast.first_ref, s32[8,64]{1,0:T(8,128)S(1)} %select_reduce_fusion.slot_of_ref, bf16[64,1040,128]{2,1,0:T(8,128)(2,1)} %all-gather.2.cloned.1.call-done.vals_ref, bf16[8192,512]{1,0:T(8,128)(2,1)} %constant_dynamic-update-slice_fusion.panel_ref), custom_call_target="tpu_custom_call" | custom-call | flops 4294967296 | bytes 17825792 | tf_op jit(solution)/shard_map/pallas_call | solution.py:36
  193.6 0.0 collective-permute-done.1
  193.7 3.5 %collective-permute-done.2 = f32[512,256]{1,0:T(8,128)S(1)} collective-permute-done((f32[512,256]{1,0:T(8,128)S(1)}, f32[512,256]{1,0:T(8,128)S(1)}, u32[]{:S(2)}, u32[]{:S(2)}) %collective-permute-start.2) | collective-permute-done | bytes 524320 | tf_op jit(solution)/shard_map/ppermute | solution.py:105
  197.2 0.2 fusion.3
  197.4 9.3 %psum.7 = f32[512]{0:T(512)S(1)} all-reduce(f32[512]{0:T(512)S(1)} %fusion.3), channel_id=1, replica_groups=mesh['row'=2,'col_z'=8,'col_y'=4,'col_x'=2,'layer'=2] {'row','layer'}, use_global_device_ids=true, to_apply=%region_2.3 | all-reduce | flops 512 | bytes 4096 | tf_op jit(solution)/shard_map/psum | solution.py:109
  206.7 1.2 broadcast_divide_fusion
  (3 shorter events, 0.0 us)
Async XLA Ops:
  6.5 157.6 %all-gather.2.cloned.1.call-start = ((), (), s32[]{:S(2)}) async-start(), calls=%async_computation | async-start | bytes 17571840 | tf_op jit(solution)/shard_map/all_gather | solution.py:66
  17.5 9.8 %collective-permute-start = (bf16[4096,512]{1,0:T(8,128)(2,1)}, bf16[4096,512]{1,0:T(8,128)(2,1)}, u32[]{:S(2)}, u32[]{:S(2)}) collective-permute-start(bf16[4096,512]{1,0:T(8,128)(2,1)} %bitcast.10), channel_id=1, source_target_pairs={{0,128},{128,0},{1,129},{129,1},{2,130},{130,2},{3,131},{131,3},{4... | collective-permute-start | bytes 12582920 | tf_op jit(solution)/shard_map/ppermute | solution.py:76
  20.2 4.2 %copy-start = (bf16[1,4096,512]{2,1,0:T(8,128)(2,1)S(1)}, bf16[1,4096,512]{2,1,0:T(8,128)(2,1)}, u32[]{:S(2)}) copy-start(bf16[1,4096,512]{2,1,0:T(8,128)(2,1)} %param.7) | copy-start | bytes 12582916
  173.5 20.2 %collective-permute-start.1 = (f32[512,256]{1,0:T(8,128)S(1)}, f32[512,256]{1,0:T(8,128)S(1)}, u32[]{:S(2)}, u32[]{:S(2)}) collective-permute-start(f32[512,256]{1,0:T(8,128)S(1)} %shard_map.38), channel_id=1, source_target_pairs={{0,1},{1,0},{2,3},{3,2},{4,5},{5,4},{6,7},{7,6},{8,9},{9,8},{10,11... | collective-permute-start | bytes 1572872 | tf_op jit(solution)/shard_map/ppermute | solution.py:105
  183.0 14.2 %collective-permute-start.2 = (f32[512,256]{1,0:T(8,128)S(1)}, f32[512,256]{1,0:T(8,128)S(1)}, u32[]{:S(2)}, u32[]{:S(2)}) collective-permute-start(f32[512,256]{1,0:T(8,128)S(1)} %shard_map.39), channel_id=1, source_target_pairs={{0,1},{1,0},{2,3},{3,2},{4,5},{5,4},{6,7},{7,6},{8,9},{9,8},{10,11... | collective-permute-start | bytes 1572872 | tf_op jit(solution)/shard_map/ppermute | solution.py:105
Sparse Core Ops, SparseCore 0:
  17.6 146.4 all-gather.1

commit v11 on v10

--- a/solution.py
+++ b/solution.py
@@ -29,7 +29,7 @@
     out_ref[...] += jnp.dot(stage_ref[...], panel_ref[...], preferred_element_type=jnp.float32)
 
 
-def dense_rows(first, slot_of, gathered, panel, share, width=16, col_parts=1, col_part=0):
+def dense_rows(first, slot_of, gathered, panel, share, width=32, col_parts=1, col_part=0):
     slot_count = gathered.shape[0]
     block_size = gathered.shape[-1]
     out_cols = panel.shape[1] // col_parts

time: 215 us -> 214 us (level)
  transfers between devices with their start and end apart: 4 -> 4, of which waited for: 3 -> 3; matrix products, arithmetic and copies ran while one was open for 5% -> 5% of each run, Pallas kernels for 9% -> 8%
where the time goes in v11:
time: 214 us
  waiting for transfers between devices  137 us (64%)
  Pallas kernels  25.5 us (12%)
  blocking collectives  18.6 us (9%)
  between operations  13.4 us (6%)
  local copies, waits for them, and re-layouts  10.9 us (5%)
  starting transfers between devices  4.36 us (2%)
  other arithmetic  4.12 us (2%)
    all_gather x1, waiting for transfers between devices, gather_slots(): return lax.all_gather(packed, COL_PARTS[:2], axis=0, tiled=True)  132 us
    pallas_call x3, Pallas kernels, dense_rows(): pl.pallas_call(dense_rows_kernel, out_shape=jax.ShapeDtypeStruct((share *...  25.5 us
    all_gather x1, blocking collectives, gather_slots(): packed = lax.all_gather(packed, COL_PARTS[2], axis=0, tiled=True)  9.31 us
    psum x1, blocking collectives, body(): column_sums = lax.psum(jnp.sum(squares, axis=0), ('row', 'layer'))  9.26 us
    dynamic_update_slice x1, local copies, waits for them, and re-layouts, body(): lax.dynamic_update_slice_in_dim(panel, other_g, (1 - row) * half_rows, 0)  4.4 us
  transfers between devices with their start and end apart: 4, of which 3 were waited for; matrix products, arithmetic and copies ran while one was open for 5% of the time, Pallas kernels for 8%

profile of v11, /device:TPU:1, one launch (start us, length us, event | category | flops | bytes accessed | tf_op | source)
XLA Modules:
  0.0 214.1 jit_solution(16102203088707545717)
XLA Ops:
  6.5 0.0 all-gather.2.cloned.1.call-start
  6.5 0.7 convert_bitcast_fusion
  7.2 1.0 fusion.2
  8.2 9.3 %all_gather.6 = bf16[2,1040,128]{2,1,0:T(8,128)(2,1)} all-gather(bf16[1,1040,128]{2,1,0:T(8,128)(2,1)S(1)} %fusion.2), channel_id=1, replica_groups=mesh['row'=2,'col_z'=8,'col_y'=4,'col_x'=2,'layer'=2] {'col_x'}, dimensions={0}, use_global_device_ids=true | all-gather | bytes 798720 | tf_op jit(solution)/shard_map/all_gather | solution.py:65
  17.5 0.0 all-gather.2.cloned.1.call-update
  17.5 2.7 %collective-permute-start = (bf16[4096,512]{1,0:T(8,128)(2,1)}, bf16[4096,512]{1,0:T(8,128)(2,1)}, u32[]{:S(2)}, u32[]{:S(2)}) collective-permute-start(bf16[4096,512]{1,0:T(8,128)(2,1)} %bitcast.10), channel_id=1, source_target_pairs={{0,128},{128,0},{1,129},{129,1},{2,130},{130,2},{3,131},{131,3},{4... | collective-permute-start | bytes 12582920 | tf_op jit(solution)/shard_map/ppermute | solution.py:76
  20.2 4.2 %broadcast_in_dim.22 = bf16[8192,512]{1,0:T(8,128)(2,1)} broadcast(bf16[]{:T(256)} %constant.49.clone.1), dimensions={} | broadcast | bytes 8388610 | tf_op jit(solution)/shard_map/broadcast_in_dim | solution.py:77
  24.4 2.2 %constant_dynamic-update-slice_fusion.1 = bf16[8192,512]{1,0:T(8,128)(2,1)} fusion(bf16[8192,512]{1,0:T(8,128)(2,1)} %broadcast_in_dim.22, s32[]{:T(128)S(6)} %select_n.11, bf16[1,4096,512]{2,1,0:T(8,128)(2,1)S(1)} %copy-done), kind=kLoop, calls=%fused_computation.12 | loop fusion | bytes 8388612 | tf_op jit(solution)/shard_map/dynamic_update_slice | solution.py:78
  26.6 0.7 collective-permute-done
  27.4 4.4 %constant_dynamic-update-slice_fusion.panel_ref = bf16[8192,512]{1,0:T(8,128)(2,1)} fusion(bf16[8192,512]{1,0:T(8,128)(2,1)} %constant_dynamic-update-slice_fusion.1, bf16[4096,512]{1,0:T(8,128)(2,1)} %collective-permute-done, s32[]{:T(128)S(6)} %select_n.12), kind=kLoop, calls=%fused_computation.11 | loop fusion | bytes 8388612 | tf_op jit(solution)/shard_map/dynamic_update_slice | solution.py:79
  31.8 132.3 %all-gather.2.cloned.1.call-done.vals_ref = bf16[64,1040,128]{2,1,0:T(8,128)(2,1)} async-done(((bf16[2,1040,128]{2,1,0:T(8,128)(2,1)}), bf16[64,1040,128]{2,1,0:T(8,128)(2,1)}) %all-gather.2.cloned.1.call-update) | async-done | bytes 17039376 | tf_op jit(solution)/shard_map/all_gather | solution.py:66
  164.1 0.9 slice_convert_fusion
  165.0 0.1 copy.6
  165.1 0.2 select_reduce_fusion.slot_of_ref
  165.3 7.7 %shard_map.38 = f32[512,256]{1,0:T(8,128)S(1)} custom-call(s32[1]{0:T(128)} %bitcast.6.first_ref, s32[8,64]{1,0:T(8,128)S(1)} %select_reduce_fusion.slot_of_ref, bf16[64,1040,128]{2,1,0:T(8,128)(2,1)} %all-gather.2.cloned.1.call-done.vals_ref, bf16[8192,512]{1,0:T(8,128)(2,1)} %constant_dynamic-update-slice_fusion.panel_ref), custom_call_target="tpu_custom_call" | custom-call | flops 2147483648 | bytes 13107200 | tf_op jit(solution)/shard_map/pallas_call | solution.py:36
  172.9 1.2 collective-permute-start.1
  174.2 7.6 %shard_map.39 = f32[512,256]{1,0:T(8,128)S(1)} custom-call(s32[1]{0:T(128)} %bitcast.6.first_ref, s32[8,64]{1,0:T(8,128)S(1)} %select_reduce_fusion.slot_of_ref, bf16[64,1040,128]{2,1,0:T(8,128)(2,1)} %all-gather.2.cloned.1.call-done.vals_ref, bf16[8192,512]{1,0:T(8,128)(2,1)} %constant_dynamic-update-slice_fusion.panel_ref), custom_call_target="tpu_custom_call" | custom-call | flops 2147483648 | bytes 13107200 | tf_op jit(solution)/shard_map/pallas_call | solution.py:36
  181.8 0.4 collective-permute-start.2
  182.2 10.2 %shard_map.37 = f32[512,512]{1,0:T(8,128)S(1)} custom-call(s32[1]{0:T(128)} %bitcast.first_ref, s32[8,64]{1,0:T(8,128)S(1)} %select_reduce_fusion.slot_of_ref, bf16[64,1040,128]{2,1,0:T(8,128)(2,1)} %all-gather.2.cloned.1.call-done.vals_ref, bf16[8192,512]{1,0:T(8,128)(2,1)} %constant_dynamic-update-slice_fusion.panel_ref), custom_call_target="tpu_custom_call" | custom-call | flops 4294967296 | bytes 17825792 | tf_op jit(solution)/shard_map/pallas_call | solution.py:36
  192.4 0.0 collective-permute-done.1
  192.4 4.2 %collective-permute-done.2 = f32[512,256]{1,0:T(8,128)S(1)} collective-permute-done((f32[512,256]{1,0:T(8,128)S(1)}, f32[512,256]{1,0:T(8,128)S(1)}, u32[]{:S(2)}, u32[]{:S(2)}) %collective-permute-start.2) | collective-permute-done | bytes 524320 | tf_op jit(solution)/shard_map/ppermute | solution.py:105
  196.6 0.2 fusion.3
  196.9 9.3 %psum.7 = f32[512]{0:T(512)S(1)} all-reduce(f32[512]{0:T(512)S(1)} %fusion.3), channel_id=1, replica_groups=mesh['row'=2,'col_z'=8,'col_y'=4,'col_x'=2,'layer'=2] {'row','layer'}, use_global_device_ids=true, to_apply=%region_2.3 | all-reduce | flops 512 | bytes 4096 | tf_op jit(solution)/shard_map/psum | solution.py:109
  206.1 1.2 broadcast_divide_fusion
  (3 shorter events, 0.0 us)
Async XLA Ops:
  6.5 157.6 %all-gather.2.cloned.1.call-start = ((), (), s32[]{:S(2)}) async-start(), calls=%async_computation | async-start | bytes 17571840 | tf_op jit(solution)/shard_map/all_gather | solution.py:66
  17.5 9.8 %collective-permute-start = (bf16[4096,512]{1,0:T(8,128)(2,1)}, bf16[4096,512]{1,0:T(8,128)(2,1)}, u32[]{:S(2)}, u32[]{:S(2)}) collective-permute-start(bf16[4096,512]{1,0:T(8,128)(2,1)} %bitcast.10), channel_id=1, source_target_pairs={{0,128},{128,0},{1,129},{129,1},{2,130},{130,2},{3,131},{131,3},{4... | collective-permute-start | bytes 12582920 | tf_op jit(solution)/shard_map/ppermute | solution.py:76
  20.2 4.2 %copy-start = (bf16[1,4096,512]{2,1,0:T(8,128)(2,1)S(1)}, bf16[1,4096,512]{2,1,0:T(8,128)(2,1)}, u32[]{:S(2)}) copy-start(bf16[1,4096,512]{2,1,0:T(8,128)(2,1)} %param.7) | copy-start | bytes 12582916
  172.9 19.5 %collective-permute-start.1 = (f32[512,256]{1,0:T(8,128)S(1)}, f32[512,256]{1,0:T(8,128)S(1)}, u32[]{:S(2)}, u32[]{:S(2)}) collective-permute-start(f32[512,256]{1,0:T(8,128)S(1)} %shard_map.38), channel_id=1, source_target_pairs={{0,1},{1,0},{2,3},{3,2},{4,5},{5,4},{6,7},{7,6},{8,9},{9,8},{10,11... | collective-permute-start | bytes 1572872 | tf_op jit(solution)/shard_map/ppermute | solution.py:105
  181.8 14.8 %collective-permute-start.2 = (f32[512,256]{1,0:T(8,128)S(1)}, f32[512,256]{1,0:T(8,128)S(1)}, u32[]{:S(2)}, u32[]{:S(2)}) collective-permute-start(f32[512,256]{1,0:T(8,128)S(1)} %shard_map.39), channel_id=1, source_target_pairs={{0,1},{1,0},{2,3},{3,2},{4,5},{5,4},{6,7},{7,6},{8,9},{9,8},{10,11... | collective-permute-start | bytes 1572872 | tf_op jit(solution)/shard_map/ppermute | solution.py:105
Sparse Core Ops, SparseCore 0:
  17.6 146.4 all-gather.1

commit v12 on v11

--- a/solution.py
+++ b/solution.py
@@ -106,7 +106,7 @@
     summed = expand(keep_first) + jnp.concatenate(received, axis=1)
     squares = summed * summed
     total_rows = row_blocks * block_size * lax.axis_size("row")
-    column_sums = lax.psum(jnp.sum(squares, axis=0), ("row", "layer"))
+    column_sums = lax.psum(lax.psum(jnp.sum(squares, axis=0), "row"), "layer")
     return squares / (column_sums / total_rows + 1e-06)
 
 

time: 214 us -> 213 us (level)
    psum x1 -> x2, blocking collectives: 9.26 us -> 7.85 us  [body(): column_sums = lax.psum(lax.psum(jnp.sum(squares, axis=0), 'row'), 'layer')]
where the time goes in v12:
time: 213 us
  waiting for transfers between devices  137 us (64%)
  Pallas kernels  25.5 us (12%)
  blocking collectives  17.2 us (8%)
  between operations  13.4 us (6%)
  local copies, waits for them, and re-layouts  10.9 us (5%)
  starting transfers between devices  4.36 us (2%)
  other arithmetic  4.12 us (2%)
    all_gather x1, waiting for transfers between devices, gather_slots(): return lax.all_gather(packed, COL_PARTS[:2], axis=0, tiled=True)  132 us
    pallas_call x3, Pallas kernels, dense_rows(): pl.pallas_call(dense_rows_kernel, out_shape=jax.ShapeDtypeStruct((share *...  25.5 us
    all_gather x1, blocking collectives, gather_slots(): packed = lax.all_gather(packed, COL_PARTS[2], axis=0, tiled=True)  9.31 us
    psum x2, blocking collectives, body(): column_sums = lax.psum(lax.psum(jnp.sum(squares, axis=0), 'row'), 'layer')  7.85 us
    dynamic_update_slice x1, local copies, waits for them, and re-layouts, body(): lax.dynamic_update_slice_in_dim(panel, other_g, (1 - row) * half_rows, 0)  4.4 us
  transfers between devices with their start and end apart: 4, of which 3 were waited for; matrix products, arithmetic and copies ran while one was open for 5% of the time, Pallas kernels for 8%

profile of v12, /device:TPU:1, one launch (start us, length us, event | category | flops | bytes accessed | tf_op | source)
XLA Modules:
  0.0 212.7 jit_solution(16753943511158371581)
XLA Ops:
  6.5 0.7 convert_bitcast_fusion
  7.2 1.0 fusion.2
  8.2 9.3 %all_gather.6 = bf16[2,1040,128]{2,1,0:T(8,128)(2,1)} all-gather(bf16[1,1040,128]{2,1,0:T(8,128)(2,1)S(1)} %fusion.2), channel_id=1, replica_groups=mesh['row'=2,'col_z'=8,'col_y'=4,'col_x'=2,'layer'=2] {'col_x'}, dimensions={0}, use_global_device_ids=true | all-gather | bytes 798720 | tf_op jit(solution)/shard_map/all_gather | solution.py:65
  17.5 0.0 all-gather.2.cloned.1.call-update
  17.5 2.7 %collective-permute-start = (bf16[4096,512]{1,0:T(8,128)(2,1)}, bf16[4096,512]{1,0:T(8,128)(2,1)}, u32[]{:S(2)}, u32[]{:S(2)}) collective-permute-start(bf16[4096,512]{1,0:T(8,128)(2,1)} %bitcast.10), channel_id=1, source_target_pairs={{0,128},{128,0},{1,129},{129,1},{2,130},{130,2},{3,131},{131,3},{4... | collective-permute-start | bytes 12582920 | tf_op jit(solution)/shard_map/ppermute | solution.py:76
  20.2 4.2 %broadcast_in_dim.22 = bf16[8192,512]{1,0:T(8,128)(2,1)} broadcast(bf16[]{:T(256)} %constant.49.clone.1), dimensions={} | broadcast | bytes 8388610 | tf_op jit(solution)/shard_map/broadcast_in_dim | solution.py:77
  24.4 2.2 %constant_dynamic-update-slice_fusion.1 = bf16[8192,512]{1,0:T(8,128)(2,1)} fusion(bf16[8192,512]{1,0:T(8,128)(2,1)} %broadcast_in_dim.22, s32[]{:T(128)S(6)} %select_n.11, bf16[1,4096,512]{2,1,0:T(8,128)(2,1)S(1)} %copy-done), kind=kLoop, calls=%fused_computation.12 | loop fusion | bytes 8388612 | tf_op jit(solution)/shard_map/dynamic_update_slice | solution.py:78
  26.6 0.7 collective-permute-done
  27.4 4.4 %constant_dynamic-update-slice_fusion.panel_ref = bf16[8192,512]{1,0:T(8,128)(2,1)} fusion(bf16[8192,512]{1,0:T(8,128)(2,1)} %constant_dynamic-update-slice_fusion.1, bf16[4096,512]{1,0:T(8,128)(2,1)} %collective-permute-done, s32[]{:T(128)S(6)} %select_n.12), kind=kLoop, calls=%fused_computation.11 | loop fusion | bytes 8388612 | tf_op jit(solution)/shard_map/dynamic_update_slice | solution.py:79
  31.8 132.3 %all-gather.2.cloned.1.call-done.vals_ref = bf16[64,1040,128]{2,1,0:T(8,128)(2,1)} async-done(((bf16[2,1040,128]{2,1,0:T(8,128)(2,1)}), bf16[64,1040,128]{2,1,0:T(8,128)(2,1)}) %all-gather.2.cloned.1.call-update) | async-done | bytes 17039376 | tf_op jit(solution)/shard_map/all_gather | solution.py:66
  164.1 0.9 slice_convert_fusion
  165.0 0.1 copy.6
  165.1 0.2 select_reduce_fusion.slot_of_ref
  165.3 7.7 %shard_map.38 = f32[512,256]{1,0:T(8,128)S(1)} custom-call(s32[1]{0:T(128)} %bitcast.6.first_ref, s32[8,64]{1,0:T(8,128)S(1)} %select_reduce_fusion.slot_of_ref, bf16[64,1040,128]{2,1,0:T(8,128)(2,1)} %all-gather.2.cloned.1.call-done.vals_ref, bf16[8192,512]{1,0:T(8,128)(2,1)} %constant_dynamic-update-slice_fusion.panel_ref), custom_call_target="tpu_custom_call" | custom-call | flops 2147483648 | bytes 13107200 | tf_op jit(solution)/shard_map/pallas_call | solution.py:36
  172.9 1.2 collective-permute-start.1
  174.2 7.6 %shard_map.39 = f32[512,256]{1,0:T(8,128)S(1)} custom-call(s32[1]{0:T(128)} %bitcast.6.first_ref, s32[8,64]{1,0:T(8,128)S(1)} %select_reduce_fusion.slot_of_ref, bf16[64,1040,128]{2,1,0:T(8,128)(2,1)} %all-gather.2.cloned.1.call-done.vals_ref, bf16[8192,512]{1,0:T(8,128)(2,1)} %constant_dynamic-update-slice_fusion.panel_ref), custom_call_target="tpu_custom_call" | custom-call | flops 2147483648 | bytes 13107200 | tf_op jit(solution)/shard_map/pallas_call | solution.py:36
  181.8 0.4 collective-permute-start.2
  182.2 10.2 %shard_map.37 = f32[512,512]{1,0:T(8,128)S(1)} custom-call(s32[1]{0:T(128)} %bitcast.first_ref, s32[8,64]{1,0:T(8,128)S(1)} %select_reduce_fusion.slot_of_ref, bf16[64,1040,128]{2,1,0:T(8,128)(2,1)} %all-gather.2.cloned.1.call-done.vals_ref, bf16[8192,512]{1,0:T(8,128)(2,1)} %constant_dynamic-update-slice_fusion.panel_ref), custom_call_target="tpu_custom_call" | custom-call | flops 4294967296 | bytes 17825792 | tf_op jit(solution)/shard_map/pallas_call | solution.py:36
  192.4 0.0 collective-permute-done.1
  192.4 4.2 %collective-permute-done.2 = f32[512,256]{1,0:T(8,128)S(1)} collective-permute-done((f32[512,256]{1,0:T(8,128)S(1)}, f32[512,256]{1,0:T(8,128)S(1)}, u32[]{:S(2)}, u32[]{:S(2)}) %collective-permute-start.2) | collective-permute-done | bytes 524320 | tf_op jit(solution)/shard_map/ppermute | solution.py:105
  196.6 0.2 fusion.3
  196.9 4.1 %psum.14 = f32[512]{0:T(512)S(1)} all-reduce(f32[512]{0:T(512)S(1)} %fusion.3), channel_id=1, replica_groups=mesh['row'=2,'col_z'=8,'col_y'=4,'col_x'=2,'layer'=2] {'row'}, use_global_device_ids=true, to_apply=%region_2.3 | all-reduce | flops 512 | bytes 4096 | tf_op jit(solution)/shard_map/psum | solution.py:109
  201.0 3.8 %psum.15 = f32[512]{0:T(512)S(1)} all-reduce(f32[512]{0:T(512)S(1)} %psum.14), channel_id=1, replica_groups=mesh['row'=2,'col_z'=8,'col_y'=4,'col_x'=2,'layer'=2] {'layer'}, use_global_device_ids=true, to_apply=%region_3.4 | all-reduce | flops 512 | bytes 4096 | tf_op jit(solution)/shard_map/psum | solution.py:109
  204.7 1.2 broadcast_divide_fusion
  (4 shorter events, 0.0 us)
Async XLA Ops:
  6.5 157.6 %all-gather.2.cloned.1.call-start = ((), (), s32[]{:S(2)}) async-start(), calls=%async_computation | async-start | bytes 17571840 | tf_op jit(solution)/shard_map/all_gather | solution.py:66
  17.5 9.8 %collective-permute-start = (bf16[4096,512]{1,0:T(8,128)(2,1)}, bf16[4096,512]{1,0:T(8,128)(2,1)}, u32[]{:S(2)}, u32[]{:S(2)}) collective-permute-start(bf16[4096,512]{1,0:T(8,128)(2,1)} %bitcast.10), channel_id=1, source_target_pairs={{0,128},{128,0},{1,129},{129,1},{2,130},{130,2},{3,131},{131,3},{4... | collective-permute-start | bytes 12582920 | tf_op jit(solution)/shard_map/ppermute | solution.py:76
  20.2 4.2 %copy-start = (bf16[1,4096,512]{2,1,0:T(8,128)(2,1)S(1)}, bf16[1,4096,512]{2,1,0:T(8,128)(2,1)}, u32[]{:S(2)}) copy-start(bf16[1,4096,512]{2,1,0:T(8,128)(2,1)} %param.7) | copy-start | bytes 12582916
  172.9 19.5 %collective-permute-start.1 = (f32[512,256]{1,0:T(8,128)S(1)}, f32[512,256]{1,0:T(8,128)S(1)}, u32[]{:S(2)}, u32[]{:S(2)}) collective-permute-start(f32[512,256]{1,0:T(8,128)S(1)} %shard_map.38), channel_id=1, source_target_pairs={{0,1},{1,0},{2,3},{3,2},{4,5},{5,4},{6,7},{7,6},{8,9},{9,8},{10,11... | collective-permute-start | bytes 1572872 | tf_op jit(solution)/shard_map/ppermute | solution.py:105
  181.8 14.8 %collective-permute-start.2 = (f32[512,256]{1,0:T(8,128)S(1)}, f32[512,256]{1,0:T(8,128)S(1)}, u32[]{:S(2)}, u32[]{:S(2)}) collective-permute-start(f32[512,256]{1,0:T(8,128)S(1)} %shard_map.39), channel_id=1, source_target_pairs={{0,1},{1,0},{2,3},{3,2},{4,5},{5,4},{6,7},{7,6},{8,9},{9,8},{10,11... | collective-permute-start | bytes 1572872 | tf_op jit(solution)/shard_map/ppermute | solution.py:105
Sparse Core Ops, SparseCore 0:
  17.6 146.4 all-gather.1

commit v13 on v12

--- a/solution.py
+++ b/solution.py
@@ -100,8 +100,8 @@
         return dense_rows(first, slot_of, gathered, panel, share)
 
     received = []
-    for part in range(2):
-        sent = dense_rows(send_first, slot_of, gathered, panel, share, col_parts=2, col_part=part)
+    for parts, part in ((4, 0), (4, 1), (2, 1)):
+        sent = dense_rows(send_first, slot_of, gathered, panel, share, col_parts=parts, col_part=part)
         received.append(lax.ppermute(sent, "layer", perm=[(0, 1), (1, 0)]))
     summed = expand(keep_first) + jnp.concatenate(received, axis=1)
     squares = summed * summed

time: 213 us -> 217 us (1.019)
  Pallas kernels: 25.5 us -> 32.6 us
  waiting for transfers between devices: 137 us -> 133 us
    pallas_call x3 -> x4, Pallas kernels: 25.5 us -> 32.6 us  [dense_rows(): pl.pallas_call(dense_rows_kernel, out_shape=jax.ShapeDtypeStruct((share *...]
    ppermute x2 -> x3, waiting for transfers between devices: 4.24 us -> 0.01 us  [body(): received.append(lax.ppermute(sent, 'layer', perm=[(0, 1), (1, 0)]))]
  transfers between devices with their start and end apart: 4 -> 5, of which waited for: 3 -> 2; matrix products, arithmetic and copies ran while one was open for 5% -> 5% of each run, Pallas kernels for 8% -> 12%
where the time goes in v13:
time: 217 us
  waiting for transfers between devices  133 us (61%)
  Pallas kernels  32.6 us (15%)
  blocking collectives  17.1 us (8%)
  between operations  13.5 us (6%)
  local copies, waits for them, and re-layouts  10.9 us (5%)
  starting transfers between devices  5.63 us (3%)
  other arithmetic  4.1 us (2%)
    all_gather x1, waiting for transfers between devices, gather_slots(): return lax.all_gather(packed, COL_PARTS[:2], axis=0, tiled=True)  132 us
    pallas_call x4, Pallas kernels, dense_rows(): pl.pallas_call(dense_rows_kernel, out_shape=jax.ShapeDtypeStruct((share *...  32.6 us
    all_gather x1, blocking collectives, gather_slots(): packed = lax.all_gather(packed, COL_PARTS[2], axis=0, tiled=True)  9.31 us
    psum x2, blocking collectives, body(): column_sums = lax.psum(lax.psum(jnp.sum(squares, axis=0), 'row'), 'layer')  7.77 us
    dynamic_update_slice x1, local copies, waits for them, and re-layouts, body(): lax.dynamic_update_slice_in_dim(panel, other_g, (1 - row) * half_rows, 0)  4.4 us
  transfers between devices with their start and end apart: 5, of which 2 were waited for; matrix products, arithmetic and copies ran while one was open for 5% of the time, Pallas kernels for 12%

profile of v13, /device:TPU:1, one launch (start us, length us, event | category | flops | bytes accessed | tf_op | source)
XLA Modules:
  0.0 216.8 jit_solution(11328330446304754658)
XLA Ops:
  6.5 0.7 convert_bitcast_fusion
  7.2 1.0 fusion.2
  8.2 9.3 %all_gather.6 = bf16[2,1040,128]{2,1,0:T(8,128)(2,1)} all-gather(bf16[1,1040,128]{2,1,0:T(8,128)(2,1)S(1)} %fusion.2), channel_id=1, replica_groups=mesh['row'=2,'col_z'=8,'col_y'=4,'col_x'=2,'layer'=2] {'col_x'}, dimensions={0}, use_global_device_ids=true | all-gather | bytes 798720 | tf_op jit(solution)/shard_map/all_gather | solution.py:65
  17.5 0.0 all-gather.2.cloned.1.call-update
  17.5 2.7 %collective-permute-start = (bf16[4096,512]{1,0:T(8,128)(2,1)}, bf16[4096,512]{1,0:T(8,128)(2,1)}, u32[]{:S(2)}, u32[]{:S(2)}) collective-permute-start(bf16[4096,512]{1,0:T(8,128)(2,1)} %bitcast.10), channel_id=1, source_target_pairs={{0,128},{128,0},{1,129},{129,1},{2,130},{130,2},{3,131},{131,3},{4... | collective-permute-start | bytes 12582920 | tf_op jit(solution)/shard_map/ppermute | solution.py:76
  20.2 4.2 %broadcast_in_dim.22 = bf16[8192,512]{1,0:T(8,128)(2,1)} broadcast(bf16[]{:T(256)} %constant.49.clone.1), dimensions={} | broadcast | bytes 8388610 | tf_op jit(solution)/shard_map/broadcast_in_dim | solution.py:77
  24.4 2.2 %constant_dynamic-update-slice_fusion.1 = bf16[8192,512]{1,0:T(8,128)(2,1)} fusion(bf16[8192,512]{1,0:T(8,128)(2,1)} %broadcast_in_dim.22, s32[]{:T(128)S(6)} %select_n.11, bf16[1,4096,512]{2,1,0:T(8,128)(2,1)S(1)} %copy-done), kind=kLoop, calls=%fused_computation.12 | loop fusion | bytes 8388612 | tf_op jit(solution)/shard_map/dynamic_update_slice | solution.py:78
  26.6 0.7 collective-permute-done
  27.4 4.4 %constant_dynamic-update-slice_fusion.panel_ref = bf16[8192,512]{1,0:T(8,128)(2,1)} fusion(bf16[8192,512]{1,0:T(8,128)(2,1)} %constant_dynamic-update-slice_fusion.1, bf16[4096,512]{1,0:T(8,128)(2,1)} %collective-permute-done, s32[]{:T(128)S(6)} %select_n.12), kind=kLoop, calls=%fused_computation.11 | loop fusion | bytes 8388612 | tf_op jit(solution)/shard_map/dynamic_update_slice | solution.py:79
  31.8 132.3 %all-gather.2.cloned.1.call-done.vals_ref = bf16[64,1040,128]{2,1,0:T(8,128)(2,1)} async-done(((bf16[2,1040,128]{2,1,0:T(8,128)(2,1)}), bf16[64,1040,128]{2,1,0:T(8,128)(2,1)}) %all-gather.2.cloned.1.call-update) | async-done | bytes 17039376 | tf_op jit(solution)/shard_map/all_gather | solution.py:66
  164.1 0.9 slice_convert_fusion
  165.0 0.1 copy.6
  165.1 0.2 select_reduce_fusion.slot_of_ref
  165.3 7.6 %shard_map.40 = f32[512,256]{1,0:T(8,128)S(1)} custom-call(s32[1]{0:T(128)} %bitcast.6.first_ref, s32[8,64]{1,0:T(8,128)S(1)} %select_reduce_fusion.slot_of_ref, bf16[64,1040,128]{2,1,0:T(8,128)(2,1)} %all-gather.2.cloned.1.call-done.vals_ref, bf16[8192,512]{1,0:T(8,128)(2,1)} %constant_dynamic-update-slice_fusion.panel_ref), custom_call_target="tpu_custom_call" | custom-call | flops 2147483648 | bytes 13107200 | tf_op jit(solution)/shard_map/pallas_call | solution.py:36
  172.9 1.3 collective-permute-start.3
  174.2 7.4 %shard_map.38 = f32[512,128]{1,0:T(8,128)S(1)} custom-call(s32[1]{0:T(128)} %bitcast.6.first_ref, s32[8,64]{1,0:T(8,128)S(1)} %select_reduce_fusion.slot_of_ref, bf16[64,1040,128]{2,1,0:T(8,128)(2,1)} %all-gather.2.cloned.1.call-done.vals_ref, bf16[8192,512]{1,0:T(8,128)(2,1)} %constant_dynamic-update-slice_fusion.panel_ref), custom_call_target="tpu_custom_call" | custom-call | flops 1073741824 | bytes 10747904 | tf_op jit(solution)/shard_map/pallas_call | solution.py:36
  181.6 0.4 collective-permute-start.1
  181.9 7.4 %shard_map.39 = f32[512,128]{1,0:T(8,128)S(1)} custom-call(s32[1]{0:T(128)} %bitcast.6.first_ref, s32[8,64]{1,0:T(8,128)S(1)} %select_reduce_fusion.slot_of_ref, bf16[64,1040,128]{2,1,0:T(8,128)(2,1)} %all-gather.2.cloned.1.call-done.vals_ref, bf16[8192,512]{1,0:T(8,128)(2,1)} %constant_dynamic-update-slice_fusion.panel_ref), custom_call_target="tpu_custom_call" | custom-call | flops 1073741824 | bytes 10747904 | tf_op jit(solution)/shard_map/pallas_call | solution.py:36
  189.3 1.3 collective-permute-start.2
  190.6 10.2 %shard_map.37 = f32[512,512]{1,0:T(8,128)S(1)} custom-call(s32[1]{0:T(128)} %bitcast.first_ref, s32[8,64]{1,0:T(8,128)S(1)} %select_reduce_fusion.slot_of_ref, bf16[64,1040,128]{2,1,0:T(8,128)(2,1)} %all-gather.2.cloned.1.call-done.vals_ref, bf16[8192,512]{1,0:T(8,128)(2,1)} %constant_dynamic-update-slice_fusion.panel_ref), custom_call_target="tpu_custom_call" | custom-call | flops 4294967296 | bytes 17825792 | tf_op jit(solution)/shard_map/pallas_call | solution.py:36
  200.8 0.2 fusion.3
  201.0 4.0 %psum.14 = f32[512]{0:T(512)S(1)} all-reduce(f32[512]{0:T(512)S(1)} %fusion.3), channel_id=1, replica_groups=mesh['row'=2,'col_z'=8,'col_y'=4,'col_x'=2,'layer'=2] {'row'}, use_global_device_ids=true, to_apply=%region_2.3 | all-reduce | flops 512 | bytes 4096 | tf_op jit(solution)/shard_map/psum | solution.py:109
  205.0 3.8 %psum.15 = f32[512]{0:T(512)S(1)} all-reduce(f32[512]{0:T(512)S(1)} %psum.14), channel_id=1, replica_groups=mesh['row'=2,'col_z'=8,'col_y'=4,'col_x'=2,'layer'=2] {'layer'}, use_global_device_ids=true, to_apply=%region_3.4 | all-reduce | flops 512 | bytes 4096 | tf_op jit(solution)/shard_map/psum | solution.py:109
  208.8 1.2 broadcast_divide_fusion
  (7 shorter events, 0.0 us)
Async XLA Ops:
  6.5 157.6 %all-gather.2.cloned.1.call-start = ((), (), s32[]{:S(2)}) async-start(), calls=%async_computation | async-start | bytes 17571840 | tf_op jit(solution)/shard_map/all_gather | solution.py:66
  17.5 9.8 %collective-permute-start = (bf16[4096,512]{1,0:T(8,128)(2,1)}, bf16[4096,512]{1,0:T(8,128)(2,1)}, u32[]{:S(2)}, u32[]{:S(2)}) collective-permute-start(bf16[4096,512]{1,0:T(8,128)(2,1)} %bitcast.10), channel_id=1, source_target_pairs={{0,128},{128,0},{1,129},{129,1},{2,130},{130,2},{3,131},{131,3},{4... | collective-permute-start | bytes 12582920 | tf_op jit(solution)/shard_map/ppermute | solution.py:76
  20.2 4.2 %copy-start = (bf16[1,4096,512]{2,1,0:T(8,128)(2,1)S(1)}, bf16[1,4096,512]{2,1,0:T(8,128)(2,1)}, u32[]{:S(2)}) copy-start(bf16[1,4096,512]{2,1,0:T(8,128)(2,1)} %param.7) | copy-start | bytes 12582916
  172.9 27.9 %collective-permute-start.3 = (f32[512,256]{1,0:T(8,128)S(1)}, f32[512,256]{1,0:T(8,128)S(1)}, u32[]{:S(2)}, u32[]{:S(2)}) collective-permute-start(f32[512,256]{1,0:T(8,128)S(1)} %shard_map.40), channel_id=1, source_target_pairs={{0,1},{1,0},{2,3},{3,2},{4,5},{5,4},{6,7},{7,6},{8,9},{9,8},{10,11... | collective-permute-start | bytes 1572872 | tf_op jit(solution)/shard_map/ppermute | solution.py:105
  181.6 19.2 %collective-permute-start.1 = (f32[512,128]{1,0:T(8,128)S(1)}, f32[512,128]{1,0:T(8,128)S(1)}, u32[]{:S(2)}, u32[]{:S(2)}) collective-permute-start(f32[512,128]{1,0:T(8,128)S(1)} %shard_map.38), channel_id=1, source_target_pairs={{0,1},{1,0},{2,3},{3,2},{4,5},{5,4},{6,7},{7,6},{8,9},{9,8},{10,11... | collective-permute-start | bytes 786440 | tf_op jit(solution)/shard_map/ppermute | solution.py:105
  189.3 11.5 %collective-permute-start.2 = (f32[512,128]{1,0:T(8,128)S(1)}, f32[512,128]{1,0:T(8,128)S(1)}, u32[]{:S(2)}, u32[]{:S(2)}) collective-permute-start(f32[512,128]{1,0:T(8,128)S(1)} %shard_map.39), channel_id=1, source_target_pairs={{0,1},{1,0},{2,3},{3,2},{4,5},{5,4},{6,7},{7,6},{8,9},{9,8},{10,11... | collective-permute-start | bytes 786440 | tf_op jit(solution)/shard_map/ppermute | solution.py:105
Sparse Core Ops, SparseCore 0:
  17.6 146.4 all-gather.1

commit v14 on v12

--- a/solution.py
+++ b/solution.py
@@ -106,7 +106,9 @@
     summed = expand(keep_first) + jnp.concatenate(received, axis=1)
     squares = summed * summed
     total_rows = row_blocks * block_size * lax.axis_size("row")
-    column_sums = lax.psum(lax.psum(jnp.sum(squares, axis=0), "row"), "layer")
+    column_sums = jnp.sum(squares, axis=0)
+    for axis in ("row", "layer"):
+        column_sums = column_sums + lax.ppermute(column_sums, axis, perm=[(0, 1), (1, 0)])
     return squares / (column_sums / total_rows + 1e-06)
 
 

time: 213 us -> 210 us (0.986)
  blocking collectives: 17.2 us -> 9.31 us
  starting transfers between devices: 4.36 us -> 7.59 us
    psum x2 -> x0, blocking collectives: 7.85 us -> none  [body(): column_sums = lax.psum(lax.psum(jnp.sum(squares, axis=0), 'row'), 'layer')]
    ppermute x0 -> x2, starting transfers between devices: none -> 3.23 us  [body(): lax.ppermute(column_sums, axis, perm=[(0, 1), (1, 0)])]
  transfers between devices with their start and end apart: 4 -> 6, of which waited for: 3 -> 5; matrix products, arithmetic and copies ran while one was open for 5% -> 5% of each run, Pallas kernels for 8% -> 8%
where the time goes in v14:
time: 210 us
  waiting for transfers between devices  139 us (66%)
  Pallas kernels  25.4 us (12%)
  between operations  13.4 us (6%)
  local copies, waits for them, and re-layouts  10.9 us (5%)
  blocking collectives  9.31 us (4%)
  starting transfers between devices  7.59 us (4%)
  other arithmetic  4.16 us (2%)
    all_gather x1, waiting for transfers between devices, gather_slots(): return lax.all_gather(packed, COL_PARTS[:2], axis=0, tiled=True)  132 us
    pallas_call x3, Pallas kernels, dense_rows(): pl.pallas_call(dense_rows_kernel, out_shape=jax.ShapeDtypeStruct((share *...  25.4 us
    all_gather x1, blocking collectives, gather_slots(): packed = lax.all_gather(packed, COL_PARTS[2], axis=0, tiled=True)  9.31 us
    dynamic_update_slice x1, local copies, waits for them, and re-layouts, body(): lax.dynamic_update_slice_in_dim(panel, other_g, (1 - row) * half_rows, 0)  4.4 us
    ppermute x2, waiting for transfers between devices, body(): received.append(lax.ppermute(sent, 'layer', perm=[(0, 1), (1, 0)]))  4.24 us
  transfers between devices with their start and end apart: 6, of which 5 were waited for; matrix products, arithmetic and copies ran while one was open for 5% of the time, Pallas kernels for 8%

profile of v14, /device:TPU:1, one launch (start us, length us, event | category | flops | bytes accessed | tf_op | source)
XLA Modules:
  0.0 210.2 jit_solution(5867600172329426389)
XLA Ops:
  6.5 0.7 convert_bitcast_fusion
  7.2 1.0 fusion.2
  8.2 9.3 %all_gather.6 = bf16[2,1040,128]{2,1,0:T(8,128)(2,1)} all-gather(bf16[1,1040,128]{2,1,0:T(8,128)(2,1)S(1)} %fusion.2), channel_id=1, replica_groups=mesh['row'=2,'col_z'=8,'col_y'=4,'col_x'=2,'layer'=2] {'col_x'}, dimensions={0}, use_global_device_ids=true | all-gather | bytes 798720 | tf_op jit(solution)/shard_map/all_gather | solution.py:65
  17.5 2.7 %collective-permute-start = (bf16[4096,512]{1,0:T(8,128)(2,1)}, bf16[4096,512]{1,0:T(8,128)(2,1)}, u32[]{:S(2)}, u32[]{:S(2)}) collective-permute-start(bf16[4096,512]{1,0:T(8,128)(2,1)} %bitcast.10), channel_id=1, source_target_pairs={{0,128},{128,0},{1,129},{129,1},{2,130},{130,2},{3,131},{131,3},{4... | collective-permute-start | bytes 12582920 | tf_op jit(solution)/shard_map/ppermute | solution.py:76
  20.2 4.2 %broadcast_in_dim.22 = bf16[8192,512]{1,0:T(8,128)(2,1)} broadcast(bf16[]{:T(256)} %constant.49.clone.1), dimensions={} | broadcast | bytes 8388610 | tf_op jit(solution)/shard_map/broadcast_in_dim | solution.py:77
  24.4 2.3 %constant_dynamic-update-slice_fusion.1 = bf16[8192,512]{1,0:T(8,128)(2,1)} fusion(bf16[8192,512]{1,0:T(8,128)(2,1)} %broadcast_in_dim.22, s32[]{:T(128)S(6)} %select_n.11, bf16[1,4096,512]{2,1,0:T(8,128)(2,1)S(1)} %copy-done), kind=kLoop, calls=%fused_computation.12 | loop fusion | bytes 8388612 | tf_op jit(solution)/shard_map/dynamic_update_slice | solution.py:78
  26.7 0.7 collective-permute-done
  27.4 4.4 %constant_dynamic-update-slice_fusion.panel_ref = bf16[8192,512]{1,0:T(8,128)(2,1)} fusion(bf16[8192,512]{1,0:T(8,128)(2,1)} %constant_dynamic-update-slice_fusion.1, bf16[4096,512]{1,0:T(8,128)(2,1)} %collective-permute-done, s32[]{:T(128)S(6)} %select_n.12), kind=kLoop, calls=%fused_computation.11 | loop fusion | bytes 8388612 | tf_op jit(solution)/shard_map/dynamic_update_slice | solution.py:79
  31.8 132.3 %all-gather.2.cloned.1.call-done.vals_ref = bf16[64,1040,128]{2,1,0:T(8,128)(2,1)} async-done(((bf16[2,1040,128]{2,1,0:T(8,128)(2,1)}), bf16[64,1040,128]{2,1,0:T(8,128)(2,1)}) %all-gather.2.cloned.1.call-update) | async-done | bytes 17039376 | tf_op jit(solution)/shard_map/all_gather | solution.py:66
  164.1 0.9 slice_convert_fusion
  165.0 0.1 copy.6
  165.1 0.2 select_reduce_fusion.slot_of_ref
  165.3 7.6 %shard_map.38 = f32[512,256]{1,0:T(8,128)S(1)} custom-call(s32[1]{0:T(128)} %bitcast.6.first_ref, s32[8,64]{1,0:T(8,128)S(1)} %select_reduce_fusion.slot_of_ref, bf16[64,1040,128]{2,1,0:T(8,128)(2,1)} %all-gather.2.cloned.1.call-done.vals_ref, bf16[8192,512]{1,0:T(8,128)(2,1)} %constant_dynamic-update-slice_fusion.panel_ref), custom_call_target="tpu_custom_call" | custom-call | flops 2147483648 | bytes 13107200 | tf_op jit(solution)/shard_map/pallas_call | solution.py:36
  172.9 1.3 collective-permute-start.1
  174.2 7.6 %shard_map.39 = f32[512,256]{1,0:T(8,128)S(1)} custom-call(s32[1]{0:T(128)} %bitcast.6.first_ref, s32[8,64]{1,0:T(8,128)S(1)} %select_reduce_fusion.slot_of_ref, bf16[64,1040,128]{2,1,0:T(8,128)(2,1)} %all-gather.2.cloned.1.call-done.vals_ref, bf16[8192,512]{1,0:T(8,128)(2,1)} %constant_dynamic-update-slice_fusion.panel_ref), custom_call_target="tpu_custom_call" | custom-call | flops 2147483648 | bytes 13107200 | tf_op jit(solution)/shard_map/pallas_call | solution.py:36
  181.8 0.4 collective-permute-start.2
  182.2 10.2 %shard_map.37 = f32[512,512]{1,0:T(8,128)S(1)} custom-call(s32[1]{0:T(128)} %bitcast.first_ref, s32[8,64]{1,0:T(8,128)S(1)} %select_reduce_fusion.slot_of_ref, bf16[64,1040,128]{2,1,0:T(8,128)(2,1)} %all-gather.2.cloned.1.call-done.vals_ref, bf16[8192,512]{1,0:T(8,128)(2,1)} %constant_dynamic-update-slice_fusion.panel_ref), custom_call_target="tpu_custom_call" | custom-call | flops 4294967296 | bytes 17825792 | tf_op jit(solution)/shard_map/pallas_call | solution.py:36
  192.4 4.2 %collective-permute-done.2 = f32[512,256]{1,0:T(8,128)S(1)} collective-permute-done((f32[512,256]{1,0:T(8,128)S(1)}, f32[512,256]{1,0:T(8,128)S(1)}, u32[]{:S(2)}, u32[]{:S(2)}) %collective-permute-start.2) | collective-permute-done | bytes 524320 | tf_op jit(solution)/shard_map/ppermute | solution.py:105
  196.6 0.2 fusion.3
  196.8 2.0 collective-permute-start.3
  198.9 0.8 collective-permute-done.3
  199.7 1.2 collective-permute-start.4
  200.9 1.2 collective-permute-done.4
  202.2 1.2 broadcast_divide_fusion
  (7 shorter events, 0.0 us)
Async XLA Ops:
  6.5 157.6 %all-gather.2.cloned.1.call-start = ((), (), s32[]{:S(2)}) async-start(), calls=%async_computation | async-start | bytes 17571840 | tf_op jit(solution)/shard_map/all_gather | solution.py:66
  17.5 9.8 %collective-permute-start = (bf16[4096,512]{1,0:T(8,128)(2,1)}, bf16[4096,512]{1,0:T(8,128)(2,1)}, u32[]{:S(2)}, u32[]{:S(2)}) collective-permute-start(bf16[4096,512]{1,0:T(8,128)(2,1)} %bitcast.10), channel_id=1, source_target_pairs={{0,128},{128,0},{1,129},{129,1},{2,130},{130,2},{3,131},{131,3},{4... | collective-permute-start | bytes 12582920 | tf_op jit(solution)/shard_map/ppermute | solution.py:76
  20.2 4.2 %copy-start = (bf16[1,4096,512]{2,1,0:T(8,128)(2,1)S(1)}, bf16[1,4096,512]{2,1,0:T(8,128)(2,1)}, u32[]{:S(2)}) copy-start(bf16[1,4096,512]{2,1,0:T(8,128)(2,1)} %param.7) | copy-start | bytes 12582916
  172.9 19.5 %collective-permute-start.1 = (f32[512,256]{1,0:T(8,128)S(1)}, f32[512,256]{1,0:T(8,128)S(1)}, u32[]{:S(2)}, u32[]{:S(2)}) collective-permute-start(f32[512,256]{1,0:T(8,128)S(1)} %shard_map.38), channel_id=1, source_target_pairs={{0,1},{1,0},{2,3},{3,2},{4,5},{5,4},{6,7},{7,6},{8,9},{9,8},{10,11... | collective-permute-start | bytes 1572872 | tf_op jit(solution)/shard_map/ppermute | solution.py:105
  181.8 14.8 %collective-permute-start.2 = (f32[512,256]{1,0:T(8,128)S(1)}, f32[512,256]{1,0:T(8,128)S(1)}, u32[]{:S(2)}, u32[]{:S(2)}) collective-permute-start(f32[512,256]{1,0:T(8,128)S(1)} %shard_map.39), channel_id=1, source_target_pairs={{0,1},{1,0},{2,3},{3,2},{4,5},{5,4},{6,7},{7,6},{8,9},{9,8},{10,11... | collective-permute-start | bytes 1572872 | tf_op jit(solution)/shard_map/ppermute | solution.py:105
  196.8 2.9 %collective-permute-start.3 = (f32[512]{0:T(512)S(1)}, f32[512]{0:T(512)S(1)}, u32[]{:S(2)}, u32[]{:S(2)}) collective-permute-start(f32[512]{0:T(512)S(1)} %fusion.3), channel_id=1, source_target_pairs={{0,128},{128,0},{1,129},{129,1},{2,130},{130,2},{3,131},{131,3},{4... | collective-permute-start | bytes 6152 | tf_op jit(solution)/shard_map/ppermute | solution.py:111
  199.7 2.4 %collective-permute-start.4 = (f32[512]{0:T(512)S(1)}, f32[512]{0:T(512)S(1)}, u32[]{:S(2)}, u32[]{:S(2)}) collective-permute-start(f32[512]{0:T(512)S(1)} %add.28), channel_id=1, source_target_pairs={{0,1},{1,0},{2,3},{3,2},{4,5},{5,4},{6,7},{7,6},{8,9},{9,8},{10,11... | collective-permute-start | bytes 6152 | tf_op jit(solution)/shard_map/ppermute | solution.py:111
Sparse Core Ops, SparseCore 0:
  17.6 146.4 all-gather.1

commit v15 on v14

--- a/solution.py
+++ b/solution.py
@@ -8,16 +8,17 @@
 
 def dense_rows_kernel(first_ref, slot_of_ref, vals_ref, panel_ref, out_ref, stage_ref):
     block_size = vals_ref.shape[-1]
-    share = vals_ref.shape[1] // block_size
+    group = vals_ref.shape[1] // block_size
     width = stage_ref.shape[1] // block_size
-    j = pl.program_id(0)
-    first = first_ref[0]
+    p = pl.program_id(0)
+    j = pl.program_id(1)
+    first = first_ref[0] + p * group
 
     @pl.when(j == 0)
     def _():
         out_ref[...] = jnp.zeros_like(out_ref)
 
-    for i in range(share):
+    for i in range(group):
         for kk in range(width):
             slot = slot_of_ref[first + i, j * width + kk]
             rows = pl.ds(i * block_size, block_size)
@@ -29,29 +30,32 @@
     out_ref[...] += jnp.dot(stage_ref[...], panel_ref[...], preferred_element_type=jnp.float32)
 
 
-def dense_rows(first, slot_of, gathered, panel, share, width=32, col_parts=1, col_part=0):
+def dense_rows(first, slot_of, gathered, panel, share, width=32, col_parts=1, col_part=0, group=None):
+    group = share if group is None else group
     slot_count = gathered.shape[0]
     block_size = gathered.shape[-1]
     out_cols = panel.shape[1] // col_parts
+    vals_mode = {"pipeline_mode": pl.Buffered(1)} if group == share else {}
     return pl.pallas_call(
         dense_rows_kernel,
         out_shape=jax.ShapeDtypeStruct((share * block_size, out_cols), jnp.float32),
         grid_spec=pltpu.PrefetchScalarGridSpec(
             num_scalar_prefetch=2,
-            grid=(panel.shape[0] // (width * block_size),),
+            grid=(share // group, panel.shape[0] // (width * block_size)),
             in_specs=[
-                pl.BlockSpec((slot_count, share * block_size, block_size),
-                             lambda j, f, t: (0, f[0] // share, 0), pipeline_mode=pl.Buffered(1)),
-                pl.BlockSpec((width * block_size, out_cols), lambda j, f, t: (j, col_part)),
+                pl.BlockSpec((slot_count, group * block_size, block_size),
+                             lambda p, j, f, t: (0, f[0] // group + p, 0), **vals_mode),
+                pl.BlockSpec((width * block_size, out_cols), lambda p, j, f, t: (j, col_part)),
             ],
-            out_specs=pl.BlockSpec((share * block_size, out_cols), lambda j, f, t: (0, 0)),
-            scratch_shapes=[pltpu.VMEM((share * block_size, width * block_size), jnp.bfloat16)],
+            out_specs=pl.BlockSpec((group * block_size, out_cols), lambda p, j, f, t: (p, 0)),
+            scratch_shapes=[pltpu.VMEM((group * block_size, width * block_size), jnp.bfloat16)],
         ),
         compiler_params=pltpu.CompilerParams(vmem_limit_bytes=48 * 1024 * 1024),
         cost_estimate=pl.CostEstimate(
             flops=2 * share * block_size * panel.shape[0] * out_cols,
             transcendentals=0,
-            bytes_accessed=slot_count * share * block_size * block_size * 2 + panel.size * 2 // col_parts + share * block_size * out_cols * 4,
+            bytes_accessed=slot_count * share * block_size * block_size * 2
+            + panel.size * 2 // col_parts * (share // group) + share * block_size * out_cols * 4,
         ),
     )(first, slot_of, gathered, panel)
 
@@ -101,7 +105,7 @@
 
     received = []
     for part in range(2):
-        sent = dense_rows(send_first, slot_of, gathered, panel, share, col_parts=2, col_part=part)
+        sent = dense_rows(send_first, slot_of, gathered, panel, share, col_parts=2, col_part=part, group=share // 2)
         received.append(lax.ppermute(sent, "layer", perm=[(0, 1), (1, 0)]))
     summed = expand(keep_first) + jnp.concatenate(received, axis=1)
     squares = summed * summed

time: 210 us -> 212 us (level)
  Pallas kernels: 25.4 us -> 28.4 us
    pallas_call x3, Pallas kernels: 25.4 us -> 28.4 us  [dense_rows(): pl.pallas_call(dense_rows_kernel, out_shape=jax.ShapeDtypeStruct((share *...]
  transfers between devices with their start and end apart: 6 -> 6, of which waited for: 5 -> 5; matrix products, arithmetic and copies ran while one was open for 5% -> 5% of each run, Pallas kernels for 8% -> 9%
where the time goes in v15:
time: 212 us
  waiting for transfers between devices  138 us (65%)
  Pallas kernels  28.4 us (13%)
  between operations  13.4 us (6%)
  local copies, waits for them, and re-layouts  10.9 us (5%)
  blocking collectives  9.31 us (4%)
  starting transfers between devices  7.04 us (3%)
  other arithmetic  4.16 us (2%)
    all_gather x1, waiting for transfers between devices, gather_slots(): return lax.all_gather(packed, COL_PARTS[:2], axis=0, tiled=True)  132 us
    pallas_call x3, Pallas kernels, dense_rows(): pl.pallas_call(dense_rows_kernel, out_shape=jax.ShapeDtypeStruct((share *...  28.4 us
    all_gather x1, blocking collectives, gather_slots(): packed = lax.all_gather(packed, COL_PARTS[2], axis=0, tiled=True)  9.31 us
    dynamic_update_slice x1, local copies, waits for them, and re-layouts, body(): lax.dynamic_update_slice_in_dim(panel, other_g, (1 - row) * half_rows, 0)  4.4 us
  transfers between devices with their start and end apart: 6, of which 5 were waited for; matrix products, arithmetic and copies ran while one was open for 5% of the time, Pallas kernels for 9%

profile of v15, /device:TPU:1, one launch (start us, length us, event | category | flops | bytes accessed | tf_op | source)
XLA Modules:
  0.0 211.7 jit_solution(13186984179181273704)
XLA Ops:
  6.5 0.7 convert_bitcast_fusion
  7.2 1.0 fusion.2
  8.2 9.3 %all_gather.6 = bf16[2,1040,128]{2,1,0:T(8,128)(2,1)} all-gather(bf16[1,1040,128]{2,1,0:T(8,128)(2,1)S(1)} %fusion.2), channel_id=1, replica_groups=mesh['row'=2,'col_z'=8,'col_y'=4,'col_x'=2,'layer'=2] {'col_x'}, dimensions={0}, use_global_device_ids=true | all-gather | bytes 798720 | tf_op jit(solution)/shard_map/all_gather | solution.py:69
  17.5 2.7 %collective-permute-start = (bf16[4096,512]{1,0:T(8,128)(2,1)}, bf16[4096,512]{1,0:T(8,128)(2,1)}, u32[]{:S(2)}, u32[]{:S(2)}) collective-permute-start(bf16[4096,512]{1,0:T(8,128)(2,1)} %bitcast.10), channel_id=1, source_target_pairs={{0,128},{128,0},{1,129},{129,1},{2,130},{130,2},{3,131},{131,3},{4... | collective-permute-start | bytes 12582920 | tf_op jit(solution)/shard_map/ppermute | solution.py:80
  20.2 4.2 %broadcast_in_dim.22 = bf16[8192,512]{1,0:T(8,128)(2,1)} broadcast(bf16[]{:T(256)} %constant.49.clone.1), dimensions={} | broadcast | bytes 8388610 | tf_op jit(solution)/shard_map/broadcast_in_dim | solution.py:81
  24.4 2.3 %constant_dynamic-update-slice_fusion.1 = bf16[8192,512]{1,0:T(8,128)(2,1)} fusion(bf16[8192,512]{1,0:T(8,128)(2,1)} %broadcast_in_dim.22, s32[]{:T(128)S(6)} %select_n.11, bf16[1,4096,512]{2,1,0:T(8,128)(2,1)S(1)} %copy-done), kind=kLoop, calls=%fused_computation.12 | loop fusion | bytes 8388612 | tf_op jit(solution)/shard_map/dynamic_update_slice | solution.py:82
  26.7 0.7 collective-permute-done
  27.4 4.4 %constant_dynamic-update-slice_fusion.panel_ref = bf16[8192,512]{1,0:T(8,128)(2,1)} fusion(bf16[8192,512]{1,0:T(8,128)(2,1)} %constant_dynamic-update-slice_fusion.1, bf16[4096,512]{1,0:T(8,128)(2,1)} %collective-permute-done, s32[]{:T(128)S(6)} %select_n.12), kind=kLoop, calls=%fused_computation.11 | loop fusion | bytes 8388612 | tf_op jit(solution)/shard_map/dynamic_update_slice | solution.py:83
  31.8 132.3 %all-gather.2.cloned.1.call-done.vals_ref = bf16[64,1040,128]{2,1,0:T(8,128)(2,1)} async-done(((bf16[2,1040,128]{2,1,0:T(8,128)(2,1)}), bf16[64,1040,128]{2,1,0:T(8,128)(2,1)}) %all-gather.2.cloned.1.call-update) | async-done | bytes 17039376 | tf_op jit(solution)/shard_map/all_gather | solution.py:70
  164.1 0.9 slice_convert_fusion
  165.0 0.1 copy.6
  165.1 0.2 select_reduce_fusion.slot_of_ref
  165.3 9.1 %shard_map.38 = f32[512,256]{1,0:T(8,128)S(1)} custom-call(s32[1]{0:T(128)} %bitcast.6.first_ref, s32[8,64]{1,0:T(8,128)S(1)} %select_reduce_fusion.slot_of_ref, bf16[64,1040,128]{2,1,0:T(8,128)(2,1)} %all-gather.2.cloned.1.call-done.vals_ref, bf16[8192,512]{1,0:T(8,128)(2,1)} %constant_dynamic-update-slice_fusion.panel_ref), custom_call_target="tpu_custom_call" | custom-call | flops 2147483648 | bytes 17301504 | tf_op jit(solution)/shard_map/pallas_call | solution.py:39
  174.4 1.3 collective-permute-start.1
  175.7 9.1 %shard_map.39 = f32[512,256]{1,0:T(8,128)S(1)} custom-call(s32[1]{0:T(128)} %bitcast.6.first_ref, s32[8,64]{1,0:T(8,128)S(1)} %select_reduce_fusion.slot_of_ref, bf16[64,1040,128]{2,1,0:T(8,128)(2,1)} %all-gather.2.cloned.1.call-done.vals_ref, bf16[8192,512]{1,0:T(8,128)(2,1)} %constant_dynamic-update-slice_fusion.panel_ref), custom_call_target="tpu_custom_call" | custom-call | flops 2147483648 | bytes 17301504 | tf_op jit(solution)/shard_map/pallas_call | solution.py:39
  184.8 0.4 collective-permute-start.2
  185.1 10.2 %shard_map.37 = f32[512,512]{1,0:T(8,128)S(1)} custom-call(s32[1]{0:T(128)} %bitcast.first_ref, s32[8,64]{1,0:T(8,128)S(1)} %select_reduce_fusion.slot_of_ref, bf16[64,1040,128]{2,1,0:T(8,128)(2,1)} %all-gather.2.cloned.1.call-done.vals_ref, bf16[8192,512]{1,0:T(8,128)(2,1)} %constant_dynamic-update-slice_fusion.panel_ref), custom_call_target="tpu_custom_call" | custom-call | flops 4294967296 | bytes 17825792 | tf_op jit(solution)/shard_map/pallas_call | solution.py:39
  195.3 3.3 %collective-permute-done.2 = f32[512,256]{1,0:T(8,128)S(1)} collective-permute-done((f32[512,256]{1,0:T(8,128)S(1)}, f32[512,256]{1,0:T(8,128)S(1)}, u32[]{:S(2)}, u32[]{:S(2)}) %collective-permute-start.2) | collective-permute-done | bytes 524320 | tf_op jit(solution)/shard_map/ppermute | solution.py:109
  198.6 0.2 fusion.3
  198.9 1.5 collective-permute-start.3
  200.4 0.8 collective-permute-done.3
  201.2 1.2 collective-permute-start.4
  202.4 1.2 collective-permute-done.4
  203.6 1.2 broadcast_divide_fusion
  (7 shorter events, 0.0 us)
Async XLA Ops:
  6.5 157.6 %all-gather.2.cloned.1.call-start = ((), (), s32[]{:S(2)}) async-start(), calls=%async_computation | async-start | bytes 17571840 | tf_op jit(solution)/shard_map/all_gather | solution.py:70
  17.5 9.8 %collective-permute-start = (bf16[4096,512]{1,0:T(8,128)(2,1)}, bf16[4096,512]{1,0:T(8,128)(2,1)}, u32[]{:S(2)}, u32[]{:S(2)}) collective-permute-start(bf16[4096,512]{1,0:T(8,128)(2,1)} %bitcast.10), channel_id=1, source_target_pairs={{0,128},{128,0},{1,129},{129,1},{2,130},{130,2},{3,131},{131,3},{4... | collective-permute-start | bytes 12582920 | tf_op jit(solution)/shard_map/ppermute | solution.py:80
  20.2 4.2 %copy-start = (bf16[1,4096,512]{2,1,0:T(8,128)(2,1)S(1)}, bf16[1,4096,512]{2,1,0:T(8,128)(2,1)}, u32[]{:S(2)}) copy-start(bf16[1,4096,512]{2,1,0:T(8,128)(2,1)} %param.7) | copy-start | bytes 12582916
  174.4 20.9 %collective-permute-start.1 = (f32[512,256]{1,0:T(8,128)S(1)}, f32[512,256]{1,0:T(8,128)S(1)}, u32[]{:S(2)}, u32[]{:S(2)}) collective-permute-start(f32[512,256]{1,0:T(8,128)S(1)} %shard_map.38), channel_id=1, source_target_pairs={{0,1},{1,0},{2,3},{3,2},{4,5},{5,4},{6,7},{7,6},{8,9},{9,8},{10,11... | collective-permute-start | bytes 1572872 | tf_op jit(solution)/shard_map/ppermute | solution.py:109
  184.8 13.8 %collective-permute-start.2 = (f32[512,256]{1,0:T(8,128)S(1)}, f32[512,256]{1,0:T(8,128)S(1)}, u32[]{:S(2)}, u32[]{:S(2)}) collective-permute-start(f32[512,256]{1,0:T(8,128)S(1)} %shard_map.39), channel_id=1, source_target_pairs={{0,1},{1,0},{2,3},{3,2},{4,5},{5,4},{6,7},{7,6},{8,9},{9,8},{10,11... | collective-permute-start | bytes 1572872 | tf_op jit(solution)/shard_map/ppermute | solution.py:109
  198.9 2.3 %collective-permute-start.3 = (f32[512]{0:T(512)S(1)}, f32[512]{0:T(512)S(1)}, u32[]{:S(2)}, u32[]{:S(2)}) collective-permute-start(f32[512]{0:T(512)S(1)} %fusion.3), channel_id=1, source_target_pairs={{0,128},{128,0},{1,129},{129,1},{2,130},{130,2},{3,131},{131,3},{4... | collective-permute-start | bytes 6152 | tf_op jit(solution)/shard_map/ppermute | solution.py:115
  201.2 2.4 %collective-permute-start.4 = (f32[512]{0:T(512)S(1)}, f32[512]{0:T(512)S(1)}, u32[]{:S(2)}, u32[]{:S(2)}) collective-permute-start(f32[512]{0:T(512)S(1)} %add.28), channel_id=1, source_target_pairs={{0,1},{1,0},{2,3},{3,2},{4,5},{5,4},{6,7},{7,6},{8,9},{9,8},{10,11... | collective-permute-start | bytes 6152 | tf_op jit(solution)/shard_map/ppermute | solution.py:115
Sparse Core Ops, SparseCore 0:
  17.6 146.4 all-gather.1

commit v16 on v14

--- a/solution.py
+++ b/solution.py
@@ -100,10 +100,11 @@
         return dense_rows(first, slot_of, gathered, panel, share)
 
     received = []
+    half = share // 2
     for part in range(2):
-        sent = dense_rows(send_first, slot_of, gathered, panel, share, col_parts=2, col_part=part)
+        sent = dense_rows(send_first + part * half, slot_of, gathered, panel, half)
         received.append(lax.ppermute(sent, "layer", perm=[(0, 1), (1, 0)]))
-    summed = expand(keep_first) + jnp.concatenate(received, axis=1)
+    summed = expand(keep_first) + jnp.concatenate(received, axis=0)
     squares = summed * summed
     total_rows = row_blocks * block_size * lax.axis_size("row")
     column_sums = jnp.sum(squares, axis=0)

time: 210 us -> 210 us (level)
  no operation moved by 1% of the time
where the time goes in v16:
time: 210 us; the launch traced here: 209 us
  waiting for transfers between devices  140 us (67%)
  Pallas kernels  23.6 us (11%)
  between operations  13.4 us (6%)
  local copies, waits for them, and re-layouts  10.9 us (5%)
  blocking collectives  9.31 us (4%)
  starting transfers between devices  7.6 us (4%)
  other arithmetic  4.25 us (2%)
    all_gather x1, waiting for transfers between devices, gather_slots(): return lax.all_gather(packed, COL_PARTS[:2], axis=0, tiled=True)  132 us
    pallas_call x3, Pallas kernels, dense_rows(): pl.pallas_call(dense_rows_kernel, out_shape=jax.ShapeDtypeStruct((share *...  23.6 us
    all_gather x1, blocking collectives, gather_slots(): packed = lax.all_gather(packed, COL_PARTS[2], axis=0, tiled=True)  9.31 us
    ppermute x2, waiting for transfers between devices, body(): received.append(lax.ppermute(sent, 'layer', perm=[(0, 1), (1, 0)]))  5.15 us
    dynamic_update_slice x1, local copies, waits for them, and re-layouts, body(): lax.dynamic_update_slice_in_dim(panel, other_g, (1 - row) * half_rows, 0)  4.4 us
  transfers between devices with their start and end apart: 6, of which 5 were waited for; matrix products, arithmetic and copies ran while one was open for 5% of the time, Pallas kernels for 8%

profile of v16, /device:TPU:1, one launch (start us, length us, event | category | flops | bytes accessed | tf_op | source)
XLA Modules:
  0.0 209.4 jit_solution(12738153048668743539)
XLA Ops:
  6.5 0.7 convert_bitcast_fusion
  7.2 1.0 fusion.2
  8.2 9.3 %all_gather.6 = bf16[2,1040,128]{2,1,0:T(8,128)(2,1)} all-gather(bf16[1,1040,128]{2,1,0:T(8,128)(2,1)S(1)} %fusion.2), channel_id=1, replica_groups=mesh['row'=2,'col_z'=8,'col_y'=4,'col_x'=2,'layer'=2] {'col_x'}, dimensions={0}, use_global_device_ids=true | all-gather | bytes 798720 | tf_op jit(solution)/shard_map/all_gather | solution.py:65
  17.5 2.7 %collective-permute-start = (bf16[4096,512]{1,0:T(8,128)(2,1)}, bf16[4096,512]{1,0:T(8,128)(2,1)}, u32[]{:S(2)}, u32[]{:S(2)}) collective-permute-start(bf16[4096,512]{1,0:T(8,128)(2,1)} %bitcast.10), channel_id=1, source_target_pairs={{0,128},{128,0},{1,129},{129,1},{2,130},{130,2},{3,131},{131,3},{4... | collective-permute-start | bytes 12582920 | tf_op jit(solution)/shard_map/ppermute | solution.py:76
  20.2 4.2 %broadcast_in_dim.22 = bf16[8192,512]{1,0:T(8,128)(2,1)} broadcast(bf16[]{:T(256)} %constant.50.clone.1), dimensions={} | broadcast | bytes 8388610 | tf_op jit(solution)/shard_map/broadcast_in_dim | solution.py:77
  24.4 2.3 %constant_dynamic-update-slice_fusion.1 = bf16[8192,512]{1,0:T(8,128)(2,1)} fusion(bf16[8192,512]{1,0:T(8,128)(2,1)} %broadcast_in_dim.22, s32[]{:T(128)S(6)} %select_n.11, bf16[1,4096,512]{2,1,0:T(8,128)(2,1)S(1)} %copy-done), kind=kLoop, calls=%fused_computation.12 | loop fusion | bytes 8388612 | tf_op jit(solution)/shard_map/dynamic_update_slice | solution.py:78
  26.7 0.7 collective-permute-done
  27.4 4.4 %constant_dynamic-update-slice_fusion.panel_ref = bf16[8192,512]{1,0:T(8,128)(2,1)} fusion(bf16[8192,512]{1,0:T(8,128)(2,1)} %constant_dynamic-update-slice_fusion.1, bf16[4096,512]{1,0:T(8,128)(2,1)} %collective-permute-done, s32[]{:T(128)S(6)} %select_n.12), kind=kLoop, calls=%fused_computation.11 | loop fusion | bytes 8388612 | tf_op jit(solution)/shard_map/dynamic_update_slice | solution.py:79
  31.8 132.3 %all-gather.2.cloned.1.call-done.vals_ref = bf16[64,1040,128]{2,1,0:T(8,128)(2,1)} async-done(((bf16[2,1040,128]{2,1,0:T(8,128)(2,1)}), bf16[64,1040,128]{2,1,0:T(8,128)(2,1)}) %all-gather.2.cloned.1.call-update) | async-done | bytes 17039376 | tf_op jit(solution)/shard_map/all_gather | solution.py:66
  164.1 0.9 slice_convert_fusion
  165.0 0.1 copy.6
  165.1 0.2 select_reduce_fusion.slot_of_ref
  165.3 6.7 %shard_map.39 = f32[256,512]{1,0:T(8,128)S(1)} custom-call(s32[1]{0:T(128)S(6)} %add.30.first_ref, s32[8,64]{1,0:T(8,128)S(1)} %select_reduce_fusion.slot_of_ref, bf16[64,1040,128]{2,1,0:T(8,128)(2,1)} %all-gather.2.cloned.1.call-done.vals_ref, bf16[8192,512]{1,0:T(8,128)(2,1)} %constant_dynamic-update-slice_fusion.panel_ref), custom_call_target="tpu_custom_call" | custom-call | flops 2147483648 | bytes 13107200 | tf_op jit(solution)/shard_map/pallas_call | solution.py:36
  172.0 1.3 collective-permute-start.2
  173.3 6.7 %shard_map.38 = f32[256,512]{1,0:T(8,128)S(1)} custom-call(s32[1]{0:T(128)} %bitcast.6.first_ref, s32[8,64]{1,0:T(8,128)S(1)} %select_reduce_fusion.slot_of_ref, bf16[64,1040,128]{2,1,0:T(8,128)(2,1)} %all-gather.2.cloned.1.call-done.vals_ref, bf16[8192,512]{1,0:T(8,128)(2,1)} %constant_dynamic-update-slice_fusion.panel_ref), custom_call_target="tpu_custom_call" | custom-call | flops 2147483648 | bytes 13107200 | tf_op jit(solution)/shard_map/pallas_call | solution.py:36
  180.0 0.4 collective-permute-start.1
  180.3 10.2 %shard_map.37 = f32[512,512]{1,0:T(8,128)S(1)} custom-call(s32[1]{0:T(128)} %bitcast.first_ref, s32[8,64]{1,0:T(8,128)S(1)} %select_reduce_fusion.slot_of_ref, bf16[64,1040,128]{2,1,0:T(8,128)(2,1)} %all-gather.2.cloned.1.call-done.vals_ref, bf16[8192,512]{1,0:T(8,128)(2,1)} %constant_dynamic-update-slice_fusion.panel_ref), custom_call_target="tpu_custom_call" | custom-call | flops 4294967296 | bytes 17825792 | tf_op jit(solution)/shard_map/pallas_call | solution.py:36
  190.5 5.1 %collective-permute-done.1 = f32[256,512]{1,0:T(8,128)S(1)} collective-permute-done((f32[256,512]{1,0:T(8,128)S(1)}, f32[256,512]{1,0:T(8,128)S(1)}, u32[]{:S(2)}, u32[]{:S(2)}) %collective-permute-start.1) | collective-permute-done | bytes 524320 | tf_op jit(solution)/shard_map/ppermute | solution.py:106
  195.7 0.3 fusion.3
  196.0 2.0 collective-permute-start.3
  198.0 0.8 collective-permute-done.3
  198.9 1.2 collective-permute-start.4
  200.0 1.2 collective-permute-done.4
  201.3 1.2 broadcast_divide_fusion
  (7 shorter events, 0.0 us)
Async XLA Ops:
  6.5 157.6 %all-gather.2.cloned.1.call-start = ((), (), s32[]{:S(2)}) async-start(), calls=%async_computation | async-start | bytes 17571840 | tf_op jit(solution)/shard_map/all_gather | solution.py:66
  17.5 9.8 %collective-permute-start = (bf16[4096,512]{1,0:T(8,128)(2,1)}, bf16[4096,512]{1,0:T(8,128)(2,1)}, u32[]{:S(2)}, u32[]{:S(2)}) collective-permute-start(bf16[4096,512]{1,0:T(8,128)(2,1)} %bitcast.10), channel_id=1, source_target_pairs={{0,128},{128,0},{1,129},{129,1},{2,130},{130,2},{3,131},{131,3},{4... | collective-permute-start | bytes 12582920 | tf_op jit(solution)/shard_map/ppermute | solution.py:76
  20.2 4.2 %copy-start = (bf16[1,4096,512]{2,1,0:T(8,128)(2,1)S(1)}, bf16[1,4096,512]{2,1,0:T(8,128)(2,1)}, u32[]{:S(2)}) copy-start(bf16[1,4096,512]{2,1,0:T(8,128)(2,1)} %param.7) | copy-start | bytes 12582916
  172.0 18.5 %collective-permute-start.2 = (f32[256,512]{1,0:T(8,128)S(1)}, f32[256,512]{1,0:T(8,128)S(1)}, u32[]{:S(2)}, u32[]{:S(2)}) collective-permute-start(f32[256,512]{1,0:T(8,128)S(1)} %shard_map.39), channel_id=1, source_target_pairs={{0,1},{1,0},{2,3},{3,2},{4,5},{5,4},{6,7},{7,6},{8,9},{9,8},{10,11... | collective-permute-start | bytes 1572872 | tf_op jit(solution)/shard_map/ppermute | solution.py:106
  180.0 15.7 %collective-permute-start.1 = (f32[256,512]{1,0:T(8,128)S(1)}, f32[256,512]{1,0:T(8,128)S(1)}, u32[]{:S(2)}, u32[]{:S(2)}) collective-permute-start(f32[256,512]{1,0:T(8,128)S(1)} %shard_map.38), channel_id=1, source_target_pairs={{0,1},{1,0},{2,3},{3,2},{4,5},{5,4},{6,7},{7,6},{8,9},{9,8},{10,11... | collective-permute-start | bytes 1572872 | tf_op jit(solution)/shard_map/ppermute | solution.py:106
  196.0 2.9 %collective-permute-start.3 = (f32[512]{0:T(512)S(1)}, f32[512]{0:T(512)S(1)}, u32[]{:S(2)}, u32[]{:S(2)}) collective-permute-start(f32[512]{0:T(512)S(1)} %fusion.3), channel_id=1, source_target_pairs={{0,128},{128,0},{1,129},{129,1},{2,130},{130,2},{3,131},{131,3},{4... | collective-permute-start | bytes 6152 | tf_op jit(solution)/shard_map/ppermute | solution.py:112
  198.9 2.4 %collective-permute-start.4 = (f32[512]{0:T(512)S(1)}, f32[512]{0:T(512)S(1)}, u32[]{:S(2)}, u32[]{:S(2)}) collective-permute-start(f32[512]{0:T(512)S(1)} %add.32), channel_id=1, source_target_pairs={{0,1},{1,0},{2,3},{3,2},{4,5},{5,4},{6,7},{7,6},{8,9},{9,8},{10,11... | collective-permute-start | bytes 6152 | tf_op jit(solution)/shard_map/ppermute | solution.py:112
Sparse Core Ops, SparseCore 0:
  17.6 146.4 all-gather.1

commit v17 on v16

--- a/solution.py
+++ b/solution.py
@@ -102,7 +102,7 @@
     received = []
     half = share // 2
     for part in range(2):
-        sent = dense_rows(send_first + part * half, slot_of, gathered, panel, half)
+        sent = dense_rows(send_first + part * half, slot_of, gathered, panel, half, width=16)
         received.append(lax.ppermute(sent, "layer", perm=[(0, 1), (1, 0)]))
     summed = expand(keep_first) + jnp.concatenate(received, axis=0)
     squares = summed * summed

time: 210 us -> 210 us (level)
  no operation moved by 1% of the time
where the time goes in v17:
time: 210 us
  waiting for transfers between devices  140 us (67%)
  Pallas kernels  25.2 us (12%)
  between operations  13.4 us (6%)
  local copies, waits for them, and re-layouts  10.9 us (5%)
  blocking collectives  9.31 us (4%)
  starting transfers between devices  7.58 us (4%)
  other arithmetic  4.25 us (2%)
    all_gather x1, waiting for transfers between devices, gather_slots(): return lax.all_gather(packed, COL_PARTS[:2], axis=0, tiled=True)  132 us
    pallas_call x3, Pallas kernels, dense_rows(): pl.pallas_call(dense_rows_kernel, out_shape=jax.ShapeDtypeStruct((share *...  25.2 us
    all_gather x1, blocking collectives, gather_slots(): packed = lax.all_gather(packed, COL_PARTS[2], axis=0, tiled=True)  9.31 us
    dynamic_update_slice x1, local copies, waits for them, and re-layouts, body(): lax.dynamic_update_slice_in_dim(panel, other_g, (1 - row) * half_rows, 0)  4.4 us
    ppermute x2, waiting for transfers between devices, body(): received.append(lax.ppermute(sent, 'layer', perm=[(0, 1), (1, 0)]))  4.37 us
  transfers between devices with their start and end apart: 6, of which 5 were waited for; matrix products, arithmetic and copies ran while one was open for 5% of the time, Pallas kernels for 8%

profile of v17, /device:TPU:1, one launch (start us, length us, event | category | flops | bytes accessed | tf_op | source)
XLA Modules:
  0.0 210.1 jit_solution(11982959672594670282)
XLA Ops:
  6.5 0.7 convert_bitcast_fusion
  7.2 1.0 fusion.2
  8.2 9.3 %all_gather.6 = bf16[2,1040,128]{2,1,0:T(8,128)(2,1)} all-gather(bf16[1,1040,128]{2,1,0:T(8,128)(2,1)S(1)} %fusion.2), channel_id=1, replica_groups=mesh['row'=2,'col_z'=8,'col_y'=4,'col_x'=2,'layer'=2] {'col_x'}, dimensions={0}, use_global_device_ids=true | all-gather | bytes 798720 | tf_op jit(solution)/shard_map/all_gather | solution.py:65
  17.5 2.7 %collective-permute-start = (bf16[4096,512]{1,0:T(8,128)(2,1)}, bf16[4096,512]{1,0:T(8,128)(2,1)}, u32[]{:S(2)}, u32[]{:S(2)}) collective-permute-start(bf16[4096,512]{1,0:T(8,128)(2,1)} %bitcast.10), channel_id=1, source_target_pairs={{0,128},{128,0},{1,129},{129,1},{2,130},{130,2},{3,131},{131,3},{4... | collective-permute-start | bytes 12582920 | tf_op jit(solution)/shard_map/ppermute | solution.py:76
  20.2 4.2 %broadcast_in_dim.22 = bf16[8192,512]{1,0:T(8,128)(2,1)} broadcast(bf16[]{:T(256)} %constant.50.clone.1), dimensions={} | broadcast | bytes 8388610 | tf_op jit(solution)/shard_map/broadcast_in_dim | solution.py:77
  24.4 2.3 %constant_dynamic-update-slice_fusion.1 = bf16[8192,512]{1,0:T(8,128)(2,1)} fusion(bf16[8192,512]{1,0:T(8,128)(2,1)} %broadcast_in_dim.22, s32[]{:T(128)S(6)} %select_n.11, bf16[1,4096,512]{2,1,0:T(8,128)(2,1)S(1)} %copy-done), kind=kLoop, calls=%fused_computation.12 | loop fusion | bytes 8388612 | tf_op jit(solution)/shard_map/dynamic_update_slice | solution.py:78
  26.7 0.7 collective-permute-done
  27.4 4.4 %constant_dynamic-update-slice_fusion.panel_ref = bf16[8192,512]{1,0:T(8,128)(2,1)} fusion(bf16[8192,512]{1,0:T(8,128)(2,1)} %constant_dynamic-update-slice_fusion.1, bf16[4096,512]{1,0:T(8,128)(2,1)} %collective-permute-done, s32[]{:T(128)S(6)} %select_n.12), kind=kLoop, calls=%fused_computation.11 | loop fusion | bytes 8388612 | tf_op jit(solution)/shard_map/dynamic_update_slice | solution.py:79
  31.8 132.3 %all-gather.2.cloned.1.call-done.vals_ref = bf16[64,1040,128]{2,1,0:T(8,128)(2,1)} async-done(((bf16[2,1040,128]{2,1,0:T(8,128)(2,1)}), bf16[64,1040,128]{2,1,0:T(8,128)(2,1)}) %all-gather.2.cloned.1.call-update) | async-done | bytes 17039376 | tf_op jit(solution)/shard_map/all_gather | solution.py:66
  164.1 0.9 slice_convert_fusion
  165.0 0.1 copy.6
  165.1 0.2 select_reduce_fusion.slot_of_ref
  165.3 7.5 %shard_map.39 = f32[256,512]{1,0:T(8,128)S(1)} custom-call(s32[1]{0:T(128)S(6)} %add.30.first_ref, s32[8,64]{1,0:T(8,128)S(1)} %select_reduce_fusion.slot_of_ref, bf16[64,1040,128]{2,1,0:T(8,128)(2,1)} %all-gather.2.cloned.1.call-done.vals_ref, bf16[8192,512]{1,0:T(8,128)(2,1)} %constant_dynamic-update-slice_fusion.panel_ref), custom_call_target="tpu_custom_call" | custom-call | flops 2147483648 | bytes 13107200 | tf_op jit(solution)/shard_map/pallas_call | solution.py:36
  172.8 1.3 collective-permute-start.2
  174.0 7.5 %shard_map.38 = f32[256,512]{1,0:T(8,128)S(1)} custom-call(s32[1]{0:T(128)} %bitcast.6.first_ref, s32[8,64]{1,0:T(8,128)S(1)} %select_reduce_fusion.slot_of_ref, bf16[64,1040,128]{2,1,0:T(8,128)(2,1)} %all-gather.2.cloned.1.call-done.vals_ref, bf16[8192,512]{1,0:T(8,128)(2,1)} %constant_dynamic-update-slice_fusion.panel_ref), custom_call_target="tpu_custom_call" | custom-call | flops 2147483648 | bytes 13107200 | tf_op jit(solution)/shard_map/pallas_call | solution.py:36
  181.5 0.4 collective-permute-start.1
  181.9 10.2 %shard_map.37 = f32[512,512]{1,0:T(8,128)S(1)} custom-call(s32[1]{0:T(128)} %bitcast.first_ref, s32[8,64]{1,0:T(8,128)S(1)} %select_reduce_fusion.slot_of_ref, bf16[64,1040,128]{2,1,0:T(8,128)(2,1)} %all-gather.2.cloned.1.call-done.vals_ref, bf16[8192,512]{1,0:T(8,128)(2,1)} %constant_dynamic-update-slice_fusion.panel_ref), custom_call_target="tpu_custom_call" | custom-call | flops 4294967296 | bytes 17825792 | tf_op jit(solution)/shard_map/pallas_call | solution.py:36
  192.1 4.4 %collective-permute-done.1 = f32[256,512]{1,0:T(8,128)S(1)} collective-permute-done((f32[256,512]{1,0:T(8,128)S(1)}, f32[256,512]{1,0:T(8,128)S(1)}, u32[]{:S(2)}, u32[]{:S(2)}) %collective-permute-start.1) | collective-permute-done | bytes 524320 | tf_op jit(solution)/shard_map/ppermute | solution.py:106
  196.5 0.3 fusion.3
  196.8 2.0 collective-permute-start.3
  198.8 0.8 collective-permute-done.3
  199.6 1.2 collective-permute-start.4
  200.8 1.3 collective-permute-done.4
  202.1 1.2 broadcast_divide_fusion
  (7 shorter events, 0.0 us)
Async XLA Ops:
  6.5 157.6 %all-gather.2.cloned.1.call-start = ((), (), s32[]{:S(2)}) async-start(), calls=%async_computation | async-start | bytes 17571840 | tf_op jit(solution)/shard_map/all_gather | solution.py:66
  17.5 9.8 %collective-permute-start = (bf16[4096,512]{1,0:T(8,128)(2,1)}, bf16[4096,512]{1,0:T(8,128)(2,1)}, u32[]{:S(2)}, u32[]{:S(2)}) collective-permute-start(bf16[4096,512]{1,0:T(8,128)(2,1)} %bitcast.10), channel_id=1, source_target_pairs={{0,128},{128,0},{1,129},{129,1},{2,130},{130,2},{3,131},{131,3},{4... | collective-permute-start | bytes 12582920 | tf_op jit(solution)/shard_map/ppermute | solution.py:76
  20.2 4.2 %copy-start = (bf16[1,4096,512]{2,1,0:T(8,128)(2,1)S(1)}, bf16[1,4096,512]{2,1,0:T(8,128)(2,1)}, u32[]{:S(2)}) copy-start(bf16[1,4096,512]{2,1,0:T(8,128)(2,1)} %param.7) | copy-start | bytes 12582916
  172.8 19.3 %collective-permute-start.2 = (f32[256,512]{1,0:T(8,128)S(1)}, f32[256,512]{1,0:T(8,128)S(1)}, u32[]{:S(2)}, u32[]{:S(2)}) collective-permute-start(f32[256,512]{1,0:T(8,128)S(1)} %shard_map.39), channel_id=1, source_target_pairs={{0,1},{1,0},{2,3},{3,2},{4,5},{5,4},{6,7},{7,6},{8,9},{9,8},{10,11... | collective-permute-start | bytes 1572872 | tf_op jit(solution)/shard_map/ppermute | solution.py:106
  181.5 14.9 %collective-permute-start.1 = (f32[256,512]{1,0:T(8,128)S(1)}, f32[256,512]{1,0:T(8,128)S(1)}, u32[]{:S(2)}, u32[]{:S(2)}) collective-permute-start(f32[256,512]{1,0:T(8,128)S(1)} %shard_map.38), channel_id=1, source_target_pairs={{0,1},{1,0},{2,3},{3,2},{4,5},{5,4},{6,7},{7,6},{8,9},{9,8},{10,11... | collective-permute-start | bytes 1572872 | tf_op jit(solution)/shard_map/ppermute | solution.py:106
  196.8 2.9 %collective-permute-start.3 = (f32[512]{0:T(512)S(1)}, f32[512]{0:T(512)S(1)}, u32[]{:S(2)}, u32[]{:S(2)}) collective-permute-start(f32[512]{0:T(512)S(1)} %fusion.3), channel_id=1, source_target_pairs={{0,128},{128,0},{1,129},{129,1},{2,130},{130,2},{3,131},{131,3},{4... | collective-permute-start | bytes 6152 | tf_op jit(solution)/shard_map/ppermute | solution.py:112
  199.6 2.4 %collective-permute-start.4 = (f32[512]{0:T(512)S(1)}, f32[512]{0:T(512)S(1)}, u32[]{:S(2)}, u32[]{:S(2)}) collective-permute-start(f32[512]{0:T(512)S(1)} %add.32), channel_id=1, source_target_pairs={{0,1},{1,0},{2,3},{3,2},{4,5},{5,4},{6,7},{7,6},{8,9},{9,8},{10,11... | collective-permute-start | bytes 6152 | tf_op jit(solution)/shard_map/ppermute | solution.py:112
Sparse Core Ops, SparseCore 0:
  17.6 146.4 all-gather.1

commit v18 on v16

--- a/solution.py
+++ b/solution.py
@@ -60,9 +60,14 @@
 COL_PARTS = ("col_z", "col_y", "col_x")
 
 
-def gather_slots(packed, split):
+def gather_slots(stacked, col_tile, split):
+    packed = jnp.concatenate([stacked, col_tile], axis=1)
     if split:
-        packed = lax.all_gather(packed, COL_PARTS[2], axis=0, tiled=True)
+        swap = [(0, 1), (1, 0)]
+        partner = jnp.concatenate(
+            [lax.ppermute(stacked, COL_PARTS[2], swap), lax.ppermute(col_tile, COL_PARTS[2], swap)], axis=1
+        )
+        packed = jnp.concatenate([packed, partner], axis=0)
         return lax.all_gather(packed, COL_PARTS[:2], axis=0, tiled=True)
     return lax.all_gather(packed, "col", axis=0, tiled=True)
 
@@ -84,8 +89,7 @@
     stacked = flow_vals.reshape(1, row_blocks * block_size, block_size)
     col_tile = jnp.zeros((1, 16, block_size), jnp.bfloat16)
     col_tile = col_tile.at[0, 0, :row_blocks].set(flow_cols.reshape(row_blocks).astype(jnp.bfloat16))
-    packed = jnp.concatenate([stacked, col_tile], axis=1)
-    gathered = gather_slots(packed, split)
+    gathered = gather_slots(stacked, col_tile, split)
     slot_cols = gathered[:, row_blocks * block_size, :row_blocks].astype(jnp.int32).T
     slot_count = gathered.shape[0]
     hit = slot_cols[:, :, None] == jnp.arange(block_count, dtype=jnp.int32)[None, None, :]

time: 210 us -> 209 us (level)
  blocking collectives: 9.31 us -> 0 us
  waiting for transfers between devices: 140 us -> 145 us
  starting transfers between devices: 7.6 us -> 11.1 us
    all_gather x1 -> x0, blocking collectives: 9.31 us -> none  [gather_slots(): packed = lax.all_gather(packed, COL_PARTS[2], axis=0, tiled=True)]
    ppermute x0 -> x2, waiting for transfers between devices: none -> 4.62 us  [the longest x1 4.62 us: gather_slots(): lax.ppermute(col_tile, COL_PARTS[2], swap)]
    ppermute x0 -> x2, starting transfers between devices: none -> 3.58 us  [the longest x1 3.57 us: gather_slots(): lax.ppermute(stacked, COL_PARTS[2], swap)]
  transfers between devices with their start and end apart: 6 -> 8, of which waited for: 5 -> 6; matrix products, arithmetic and copies ran while one was open for 5% -> 6% of each run, Pallas kernels for 8% -> 8%
where the time goes in v18:
time: 209 us
  waiting for transfers between devices  145 us (69%)
  Pallas kernels  23.6 us (11%)
  between operations  13.4 us (6%)
  starting transfers between devices  11.1 us (5%)
  local copies, waits for them, and re-layouts  10.9 us (5%)
  other arithmetic  5.06 us (2%)
    all_gather x1, waiting for transfers between devices, gather_slots(): return lax.all_gather(packed, COL_PARTS[:2], axis=0, tiled=True)  132 us
    pallas_call x3, Pallas kernels, dense_rows(): pl.pallas_call(dense_rows_kernel, out_shape=jax.ShapeDtypeStruct((share *...  23.6 us
    ppermute x2, waiting for transfers between devices, body(): received.append(lax.ppermute(sent, 'layer', perm=[(0, 1), (1, 0)]))  5.16 us
    ppermute x1, waiting for transfers between devices, gather_slots(): lax.ppermute(col_tile, COL_PARTS[2], swap)  4.62 us
    dynamic_update_slice x1, local copies, waits for them, and re-layouts, body(): lax.dynamic_update_slice_in_dim(panel, other_g, (1 - row) * half_rows, 0)  4.39 us
  transfers between devices with their start and end apart: 8, of which 6 were waited for; matrix products, arithmetic and copies ran while one was open for 6% of the time, Pallas kernels for 8%

profile of v18, /device:TPU:1, one launch (start us, length us, event | category | flops | bytes accessed | tf_op | source)
XLA Modules:
  0.0 208.9 jit_solution(7042016404593733207)
XLA Ops:
  6.5 3.6 %collective-permute-start = (bf16[1,1024,128]{2,1,0:T(8,128)(2,1)}, bf16[1,1024,128]{2,1,0:T(8,128)(2,1)S(1)}, u32[]{:S(2)}, u32[]{:S(2)}) collective-permute-start(bf16[1,1024,128]{2,1,0:T(8,128)(2,1)} %bitcast.11), channel_id=1, source_target_pairs={{0,2},{2,0},{1,3},{3,1},{4,6},{6,4},{5,7},{7,5},{8,10},{10,8},{9,1... | collective-permute-start | bytes 786440 | tf_op jit(solution)/shard_map/ppermute | solution.py:68
  10.1 0.7 convert_bitcast_fusion
  10.8 4.6 %collective-permute-done.1 = bf16[1,16,128]{2,1,0:T(8,128)(2,1)S(1)} collective-permute-done((bf16[1,16,128]{2,1,0:T(8,128)(2,1)S(1)}, bf16[1,16,128]{2,1,0:T(8,128)(2,1)S(1)}, u32[]{:S(2)}, u32[]{:S(2)}) %collective-permute-start.1) | collective-permute-done | bytes 4128 | tf_op jit(solution)/shard_map/ppermute | solution.py:68
  15.4 1.8 maximum_maximum_fusion
  17.2 2.6 %collective-permute-start.2 = (bf16[4096,512]{1,0:T(8,128)(2,1)}, bf16[4096,512]{1,0:T(8,128)(2,1)}, u32[]{:S(2)}, u32[]{:S(2)}) collective-permute-start(bf16[4096,512]{1,0:T(8,128)(2,1)} %bitcast.10), channel_id=1, source_target_pairs={{0,128},{128,0},{1,129},{129,1},{2,130},{130,2},{3,131},{131,3},{4... | collective-permute-start | bytes 12582920 | tf_op jit(solution)/shard_map/ppermute | solution.py:81
  19.9 4.2 %broadcast_in_dim.22 = bf16[8192,512]{1,0:T(8,128)(2,1)} broadcast(bf16[]{:T(256)} %constant.50.clone.1), dimensions={} | broadcast | bytes 8388610 | tf_op jit(solution)/shard_map/broadcast_in_dim | solution.py:82
  24.0 2.3 %constant_dynamic-update-slice_fusion.1 = bf16[8192,512]{1,0:T(8,128)(2,1)} fusion(bf16[8192,512]{1,0:T(8,128)(2,1)} %broadcast_in_dim.22, s32[]{:T(128)S(6)} %select_n.11, bf16[1,4096,512]{2,1,0:T(8,128)(2,1)S(1)} %copy-done), kind=kLoop, calls=%fused_computation.10 | loop fusion | bytes 8388612 | tf_op jit(solution)/shard_map/dynamic_update_slice | solution.py:83
  26.3 0.7 collective-permute-done.2
  27.0 4.4 %constant_dynamic-update-slice_fusion.panel_ref = bf16[8192,512]{1,0:T(8,128)(2,1)} fusion(bf16[8192,512]{1,0:T(8,128)(2,1)} %constant_dynamic-update-slice_fusion.1, bf16[4096,512]{1,0:T(8,128)(2,1)} %collective-permute-done.2, s32[]{:T(128)S(6)} %select_n.12), kind=kLoop, calls=%fused_computation.9 | loop fusion | bytes 8388612 | tf_op jit(solution)/shard_map/dynamic_update_slice | solution.py:84
  31.4 132.3 %all-gather.2.cloned.1.call-done.vals_ref = bf16[64,1040,128]{2,1,0:T(8,128)(2,1)} async-done(((bf16[2,1040,128]{2,1,0:T(8,128)(2,1)}), bf16[64,1040,128]{2,1,0:T(8,128)(2,1)}) %all-gather.2.cloned.1.call-update) | async-done | bytes 17039376 | tf_op jit(solution)/shard_map/all_gather | solution.py:71
  163.7 0.9 slice_convert_fusion
  164.7 0.2 select_reduce_fusion.slot_of_ref
  164.8 6.7 %shard_map.39 = f32[256,512]{1,0:T(8,128)S(1)} custom-call(s32[1]{0:T(128)S(6)} %add.30.first_ref, s32[8,64]{1,0:T(8,128)S(1)} %select_reduce_fusion.slot_of_ref, bf16[64,1040,128]{2,1,0:T(8,128)(2,1)} %all-gather.2.cloned.1.call-done.vals_ref, bf16[8192,512]{1,0:T(8,128)(2,1)} %constant_dynamic-update-slice_fusion.panel_ref), custom_call_target="tpu_custom_call" | custom-call | flops 2147483648 | bytes 13107200 | tf_op jit(solution)/shard_map/pallas_call | solution.py:36
  171.6 1.3 collective-permute-start.4
  172.8 6.7 %shard_map.38 = f32[256,512]{1,0:T(8,128)S(1)} custom-call(s32[1]{0:T(128)} %bitcast.6.first_ref, s32[8,64]{1,0:T(8,128)S(1)} %select_reduce_fusion.slot_of_ref, bf16[64,1040,128]{2,1,0:T(8,128)(2,1)} %all-gather.2.cloned.1.call-done.vals_ref, bf16[8192,512]{1,0:T(8,128)(2,1)} %constant_dynamic-update-slice_fusion.panel_ref), custom_call_target="tpu_custom_call" | custom-call | flops 2147483648 | bytes 13107200 | tf_op jit(solution)/shard_map/pallas_call | solution.py:36
  179.6 0.4 collective-permute-start.3
  179.9 10.2 %shard_map.37 = f32[512,512]{1,0:T(8,128)S(1)} custom-call(s32[1]{0:T(128)} %bitcast.first_ref, s32[8,64]{1,0:T(8,128)S(1)} %select_reduce_fusion.slot_of_ref, bf16[64,1040,128]{2,1,0:T(8,128)(2,1)} %all-gather.2.cloned.1.call-done.vals_ref, bf16[8192,512]{1,0:T(8,128)(2,1)} %constant_dynamic-update-slice_fusion.panel_ref), custom_call_target="tpu_custom_call" | custom-call | flops 4294967296 | bytes 17825792 | tf_op jit(solution)/shard_map/pallas_call | solution.py:36
  190.1 5.2 %collective-permute-done.3 = f32[256,512]{1,0:T(8,128)S(1)} collective-permute-done((f32[256,512]{1,0:T(8,128)S(1)}, f32[256,512]{1,0:T(8,128)S(1)}, u32[]{:S(2)}, u32[]{:S(2)}) %collective-permute-start.3) | collective-permute-done | bytes 524320 | tf_op jit(solution)/shard_map/ppermute | solution.py:110
  195.3 0.3 fusion.1
  195.6 2.0 collective-permute-start.5
  197.6 0.8 collective-permute-done.5
  198.4 1.2 collective-permute-start.6
  199.6 1.2 collective-permute-done.6
  200.9 1.2 broadcast_divide_fusion
  (11 shorter events, 0.1 us)
Async XLA Ops:
  6.5 157.1 %all-gather.2.cloned.1.call-start = ((), (), s32[]{:S(2)}) async-start(), calls=%async_computation | async-start | bytes 17571840 | tf_op jit(solution)/shard_map/all_gather | solution.py:71
  6.5 8.9 %collective-permute-start = (bf16[1,1024,128]{2,1,0:T(8,128)(2,1)}, bf16[1,1024,128]{2,1,0:T(8,128)(2,1)S(1)}, u32[]{:S(2)}, u32[]{:S(2)}) collective-permute-start(bf16[1,1024,128]{2,1,0:T(8,128)(2,1)} %bitcast.11), channel_id=1, source_target_pairs={{0,2},{2,0},{1,3},{3,1},{4,6},{6,4},{5,7},{7,5},{8,10},{10,8},{9,1... | collective-permute-start | bytes 786440 | tf_op jit(solution)/shard_map/ppermute | solution.py:68
  10.8 4.6 %collective-permute-start.1 = (bf16[1,16,128]{2,1,0:T(8,128)(2,1)S(1)}, bf16[1,16,128]{2,1,0:T(8,128)(2,1)S(1)}, u32[]{:S(2)}, u32[]{:S(2)}) collective-permute-start(bf16[1,16,128]{2,1,0:T(8,128)(2,1)S(1)} %scatter.4), channel_id=1, source_target_pairs={{0,2},{2,0},{1,3},{3,1},{4,6},{6,4},{5,7},{7,5},{8,10},{10,8},{9,1... | collective-permute-start | bytes 12296 | tf_op jit(solution)/shard_map/ppermute | solution.py:68
  17.2 9.8 %collective-permute-start.2 = (bf16[4096,512]{1,0:T(8,128)(2,1)}, bf16[4096,512]{1,0:T(8,128)(2,1)}, u32[]{:S(2)}, u32[]{:S(2)}) collective-permute-start(bf16[4096,512]{1,0:T(8,128)(2,1)} %bitcast.10), channel_id=1, source_target_pairs={{0,128},{128,0},{1,129},{129,1},{2,130},{130,2},{3,131},{131,3},{4... | collective-permute-start | bytes 12582920 | tf_op jit(solution)/shard_map/ppermute | solution.py:81
  19.8 4.2 %copy-start = (bf16[1,4096,512]{2,1,0:T(8,128)(2,1)S(1)}, bf16[1,4096,512]{2,1,0:T(8,128)(2,1)}, u32[]{:S(2)}) copy-start(bf16[1,4096,512]{2,1,0:T(8,128)(2,1)} %param.7) | copy-start | bytes 12582916
  171.6 18.5 %collective-permute-start.4 = (f32[256,512]{1,0:T(8,128)S(1)}, f32[256,512]{1,0:T(8,128)S(1)}, u32[]{:S(2)}, u32[]{:S(2)}) collective-permute-start(f32[256,512]{1,0:T(8,128)S(1)} %shard_map.39), channel_id=1, source_target_pairs={{0,1},{1,0},{2,3},{3,2},{4,5},{5,4},{6,7},{7,6},{8,9},{9,8},{10,11... | collective-permute-start | bytes 1572872 | tf_op jit(solution)/shard_map/ppermute | solution.py:110
  179.6 15.7 %collective-permute-start.3 = (f32[256,512]{1,0:T(8,128)S(1)}, f32[256,512]{1,0:T(8,128)S(1)}, u32[]{:S(2)}, u32[]{:S(2)}) collective-permute-start(f32[256,512]{1,0:T(8,128)S(1)} %shard_map.38), channel_id=1, source_target_pairs={{0,1},{1,0},{2,3},{3,2},{4,5},{5,4},{6,7},{7,6},{8,9},{9,8},{10,11... | collective-permute-start | bytes 1572872 | tf_op jit(solution)/shard_map/ppermute | solution.py:110
  195.6 2.9 %collective-permute-start.5 = (f32[512]{0:T(512)S(1)}, f32[512]{0:T(512)S(1)}, u32[]{:S(2)}, u32[]{:S(2)}) collective-permute-start(f32[512]{0:T(512)S(1)} %fusion.1), channel_id=1, source_target_pairs={{0,128},{128,0},{1,129},{129,1},{2,130},{130,2},{3,131},{131,3},{4... | collective-permute-start | bytes 6152 | tf_op jit(solution)/shard_map/ppermute | solution.py:116
  198.4 2.4 %collective-permute-start.6 = (f32[512]{0:T(512)S(1)}, f32[512]{0:T(512)S(1)}, u32[]{:S(2)}, u32[]{:S(2)}) collective-permute-start(f32[512]{0:T(512)S(1)} %add.32), channel_id=1, source_target_pairs={{0,1},{1,0},{2,3},{3,2},{4,5},{5,4},{6,7},{7,6},{8,9},{9,8},{10,11... | collective-permute-start | bytes 6152 | tf_op jit(solution)/shard_map/ppermute | solution.py:116
Sparse Core Ops, SparseCore 0:
  17.3 146.3 all-gather.1
